TPU v7x, 256 devices: a whole 4x4x8 slice. The times are simulated.
256 devices in a mesh: rep: 4 (over y), exp: 64 (over z, x, core).
Axes of the slice: x: 4, y: 4, z: 8, core: 2. Of those that a mesh axis runs over, the one named last changes fastest.
Arguments:
- cache_keys: bfloat16 [256, 2048, 512], P(('rep', 'exp')), may hold values from -6.5 to 6.5
- cache_values: bfloat16 [256, 2048, 512], P(('rep', 'exp')), may hold values from -6 to 6
- lengths: int32 [256], P(('rep', 'exp')), may hold values from 512 to 2048, as said below
- drift_rows: int32 [2, 256, 8], P(None, ('rep', 'exp')), may hold values from 0 to 2047, as said below
- block_in: bfloat16 [256, 8, 4096], P(('rep', 'exp')), may hold values from -6 to 6
- drift_in: bfloat16 [2, 256, 8, 4096], P(None, ('rep', 'exp')), may hold values from -6 to 6
- queries: bfloat16 [2, 256, 16, 4096], P(None, ('rep', 'exp')), may hold values from -150 to 150
- new_keys: bfloat16 [2, 256, 16, 512], P(None, ('rep', 'exp')), may hold values from -6 to 6
- new_values: bfloat16 [2, 256, 16, 512], P(None, ('rep', 'exp')), may hold values from -6 to 6
- norm_gain: float32 [4096], replicated, may hold values from 0.25 to 1.75
- expert_ids: int32 [2, 256, 16, 8], P(None, ('rep', 'exp')), may hold values from 0 to 63, all different within a row; in each aligned block of 16 rows (0 to 15, 16 to 31, ..., all dimensions but the last counted through in order) at most 3 rows name the same one
- gate_weights: bfloat16 [2, 256, 16, 8], P(None, ('rep', 'exp')), may hold values from 0.049804688 to 0.3984375
- w_gate: bfloat16 [64, 4096, 1024], P('exp', None, 'rep'), may hold values from -0.09375 to 0.09375
- w_up: bfloat16 [64, 4096, 1024], P('exp', None, 'rep'), may hold values from -0.09375 to 0.09375
- w_down: bfloat16 [64, 1024, 4096], P('exp', 'rep'), may hold values from -0.1875 to 0.1875
Outputs:
- out: bfloat16 [2, 256, 16, 4096], P(None, ('rep', 'exp'))
Inputs may be any that keep to these rules, and one draw needn't show every extreme that they name: `lengths`: one request has exactly 2048. `drift_rows`: for each step and request, 8 different positions in increasing order, all below that request's length. `expert_ids`: each row names 8 different experts; within one step the rows of one request name any expert at most 3 times, a bound that some block reaches.
All inputs are finite; a program needn't handle non-finite values.
Results may differ from a plain program's by a relative error of at most 0.012.
Values may be sent and summed in bfloat16 or wider, within the bound.
No kernel may reach another device: no remote copies, remote signals or barrier semaphores. Data moves between devices by JAX's collectives and lax.ppermute only.
A program may use at most 128 MiB of HBM per device.

v0:
```python
import jax
import jax.numpy as jnp
from jax import lax
from jax.sharding import PartitionSpec as P

H = 32
KVH = 4
HD = 128
TOP = 8
BLOCK = 8


def attend(query_rows, key_rows, value_rows, block_keys, block_values, length):
    row_count = query_rows.shape[0]
    group_size = H // KVH
    query_head_rows = query_rows.reshape(row_count, KVH, group_size, HD)
    cache_k = key_rows.reshape(-1, KVH, HD)
    cached_value_rows = value_rows.reshape(-1, KVH, HD)
    prompt_key_rows = block_keys.reshape(-1, KVH, HD)
    prompt_value_rows = block_values.reshape(-1, KVH, HD)
    logit_scale_factor = HD ** (-0.5)
    cache_scores = (
        jnp.einsum("rkgd,ckd->kgrc", query_head_rows, cache_k, preferred_element_type=jnp.float32)
        * logit_scale_factor
    )
    prompt_score_rows = (
        jnp.einsum(
            "afhu,nfu->fhan", query_head_rows, prompt_key_rows, preferred_element_type=jnp.float32
        )
        * logit_scale_factor
    )
    cache_mask = jnp.arange(cache_k.shape[0]) < length
    own_mask = (jnp.arange(row_count) < BLOCK)[:, None]
    cache_scores = jnp.where(cache_mask, cache_scores, -1e30)
    prompt_score_rows = jnp.where(own_mask, prompt_score_rows, -1e30)
    peak = jnp.maximum(jnp.max(cache_scores, axis=-1), jnp.max(prompt_score_rows, axis=-1))
    cache_exp = jnp.exp(cache_scores - peak[..., None])
    own_exp = jnp.exp(prompt_score_rows - peak[..., None])
    denom = jnp.sum(cache_exp, axis=-1) + jnp.sum(own_exp, axis=-1)
    cached_weight_share = (cache_exp / denom[..., None]).astype(jnp.bfloat16)
    prompt_weight_share = (own_exp / denom[..., None]).astype(jnp.bfloat16)
    blended_output = jnp.einsum(
        "qimt,tqj->mqij", cached_weight_share, cached_value_rows, preferred_element_type=jnp.float32
    )
    blended_output = blended_output + jnp.einsum(
        "iywf,fie->wiye", prompt_weight_share, prompt_value_rows, preferred_element_type=jnp.float32
    )
    return blended_output.reshape(row_count, H * HD)


def route_table(routed, gate_share, experts, capacity):
    member = routed[:, :, None] == jnp.arange(experts)[None, None, :]
    weight = jnp.sum(jnp.where(member, gate_share[:, :, None].astype(jnp.float32), 0.0), axis=1)
    chosen = jnp.any(member, axis=1).astype(jnp.int32)
    slot_rank = jnp.cumsum(chosen, axis=0) - chosen
    taken = (slot_rank[:, :, None] == jnp.arange(capacity)[None, None, :]) & (
        chosen[:, :, None] == 1
    )
    return jnp.where(taken, weight[:, :, None], 0.0).astype(jnp.bfloat16)


def expert_terms(routed_rows, gate_part, up_part, down_part):
    flat_rows = routed_rows.reshape(-1, routed_rows.shape[-1])
    gate_act = jnp.dot(flat_rows, gate_part, preferred_element_type=jnp.float32)
    up_act = jnp.dot(flat_rows, up_part, preferred_element_type=jnp.float32)
    hidden = (jax.nn.silu(gate_act) * up_act).astype(jnp.bfloat16)
    produced = jnp.dot(hidden, down_part, preferred_element_type=jnp.float32).astype(jnp.bfloat16)
    return produced.reshape(routed_rows.shape)


def on_device(
    cache_keys,
    cache_values,
    lengths,
    drift_rows,
    block_in,
    drift_in,
    queries,
    new_keys,
    new_values,
    norm_gain,
    expert_ids,
    gate_weights,
    w_gate,
    w_up,
    w_down,
):
    rep_count = lax.axis_size("rep")
    experts = lax.axis_size("exp") * w_gate.shape[0]
    row_count = queries.shape[2]
    capacity = min(row_count, (3 * row_count * TOP + 2 * experts - 1) // (2 * experts))
    key_rows = cache_keys[0]
    value_rows = cache_values[0]
    carried = block_in[0]
    results = []
    for denoise in range(2):
        key_rows = key_rows.at[drift_rows[denoise, 0]].set(new_keys[denoise, 0, BLOCK:])
        value_rows = value_rows.at[drift_rows[denoise, 0]].set(new_values[denoise, 0, BLOCK:])
        attended = attend(
            queries[denoise, 0],
            key_rows,
            value_rows,
            new_keys[denoise, 0, :BLOCK],
            new_values[denoise, 0, :BLOCK],
            lengths[0],
        )
        inputs = jnp.concatenate([carried, drift_in[denoise, 0]], axis=0).astype(jnp.float32)
        residual = inputs + attended
        inverse = lax.rsqrt(jnp.mean(residual * residual, axis=-1, keepdims=True) + 1e-06)
        normed = (residual * inverse * norm_gain).astype(jnp.bfloat16)
        slot_table = route_table(
            expert_ids[denoise, 0], gate_weights[denoise, 0], experts, capacity
        )
        flat_table = slot_table.reshape(row_count, experts * capacity)
        all_rows, all_tables = (
            lax.all_gather(normed, "rep", axis=0, tiled=True),
            lax.all_gather(flat_table, "rep", axis=0, tiled=True),
        )
        all_rows = all_rows.reshape(rep_count, row_count, -1)
        all_tables = all_tables.reshape(rep_count, row_count, experts, capacity)
        chosen_slots = (all_tables != 0).astype(jnp.bfloat16)
        dispatched = jnp.einsum(
            "orec,ord->eocd", chosen_slots, all_rows, preferred_element_type=jnp.float32
        ).astype(jnp.bfloat16)
        produced = expert_terms(
            lax.all_to_all(dispatched, "exp", split_axis=0, concat_axis=0, tiled=True),
            w_gate[0],
            w_up[0],
            w_down[0],
        )
        expert_out = lax.all_to_all(produced, "exp", split_axis=0, concat_axis=0, tiled=True)
        combined = jnp.einsum(
            "orec,eocd->ord", all_tables, expert_out, preferred_element_type=jnp.float32
        )
        moe = lax.psum_scatter(
            combined.reshape(rep_count * row_count, -1).astype(jnp.bfloat16),
            "rep",
            scatter_dimension=0,
            tiled=True,
        ).astype(jnp.float32)
        result = (residual + moe).astype(jnp.bfloat16)
        results.append(result)
        carried = result[:BLOCK]
    return jnp.stack(results)[:, None]


def solution(mesh):
    placed = (
        P(("rep", "exp"), None, None),
        P(("rep", "exp"), None, None),
        P(("rep", "exp")),
        P(None, ("rep", "exp"), None),
        P(("rep", "exp"), None, None),
        P(None, ("rep", "exp"), None, None),
        P(None, ("rep", "exp"), None, None),
        P(None, ("rep", "exp"), None, None),
        P(None, ("rep", "exp"), None, None),
        P(),
        P(None, ("rep", "exp"), None, None),
        P(None, ("rep", "exp"), None, None),
        P("exp", None, "rep"),
        P("exp", None, "rep"),
        P("exp", "rep", None),
    )
    return jax.shard_map(
        on_device,
        mesh=mesh,
        in_specs=placed,
        out_specs=P(None, ("rep", "exp"), None, None),
        check_vma=False,
    )
```

profile of v0, /device:TPU:24, one launch (start us, length us, event | category | flops | bytes accessed | tf_op | source)
XLA Modules:
  0.0 954.5 jit_solution(4832013460404431543)
XLA Ops:
  45.9 13.5 %all_gather.13 = bf16[64,4096]{1,0:T(8,128)(2,1)S(1)} all-gather(bf16[16,4096]{1,0:T(8,128)(2,1)S(1)} %multiply_convert_fusion.1), channel_id=1, replica_groups=mesh['rep'=4,'exp'=64] {'rep'}, dimensions={0}, use_global_device_ids=true | all-gather | bytes 655360 | tf_op jit(solution)/shard_map/all_gather | solution.py:116
  62.0 12.1 %all_gather.12 = bf16[64,192]{1,0:T(8,128)(2,1)S(1)} all-gather(bf16[16,192]{1,0:T(8,128)(2,1)S(1)} %get-tuple-element.21), channel_id=1, replica_groups=mesh['rep'=4,'exp'=64] {'rep'}, dimensions={0}, use_global_device_ids=true | all-gather | bytes 30720 | tf_op jit(solution)/shard_map/all_gather | solution.py:117
  79.0 10.3 %copy.171 = bf16[64,4,3,4096]{3,1,2,0:T(4,128)(2,1)} copy(bf16[64,4,3,4096]{3,0,2,1:T(8,128)(2,1)} %fusion.4) | data formatting | bytes 12582912 | tf_op jit(solution)/shard_map/convert_element_type | solution.py:124
  89.3 153.5 %all_to_all.20 = bf16[64,4,3,4096]{3,1,2,0:T(4,128)(2,1)} all-to-all(bf16[64,4,3,4096]{3,1,2,0:T(4,128)(2,1)} %copy.171), channel_id=1, replica_groups=mesh['rep'=4,'exp'=64] {'exp'}, dimensions={0} | all-to-all | bytes 12582912 | tf_op jit(solution)/shard_map/all_to_all | solution.py:126
  242.8 16.1 %copy.172 = bf16[64,4,3,4096]{3,2,1,0:T(4,128)(2,1)} copy(bf16[64,4,3,4096]{3,1,2,0:T(4,128)(2,1)} %all_to_all.20) | data formatting | bytes 12582912 | tf_op jit(solution)/shard_map/all_to_all | solution.py:126
  258.9 14.2 %reshape.215 = bf16[768,4096]{1,0:T(8,128)(2,1)} reshape(bf16[64,4,3,4096]{3,2,1,0:T(4,128)(2,1)} %copy.172) | data formatting | bytes 12582912 | tf_op jit(solution)/shard_map/reshape | solution.py:63
  273.1 6.1 fusion.34
  279.2 12.7 %convolution_convert_fusion.1 = bf16[768,4096]{1,0:T(8,128)(2,1)} fusion(bf16[1,256,4096]{2,1,0:T(8,128)(2,1)S(1)} %copy-done, bf16[768,4096]{1,0:T(8,128)(2,1)} %reshape.215, bf16[1,4096,256]{2,1,0:T(8,128)(2,1)} %param.28, f32[768,256]{1,0:T(8,128)} %fusion.34), kind=kOutput, calls=%fused_computation.5 | convolution fusion | flops 3225550848 | bytes 17563648 | tf_op jit(solution)/shard_map/dot_general | solution.py:67
  291.9 13.0 %reshape.216 = bf16[64,4,3,4096]{3,2,1,0:T(4,128)(2,1)} reshape(bf16[768,4096]{1,0:T(8,128)(2,1)} %convolution_convert_fusion.1) | data formatting | bytes 12582912 | tf_op jit(solution)/shard_map/reshape | solution.py:68
  305.0 21.5 %copy.173 = bf16[64,4,3,4096]{3,1,2,0:T(4,128)(2,1)} copy(bf16[64,4,3,4096]{3,2,1,0:T(4,128)(2,1)} %reshape.216) | data formatting | bytes 12582912 | tf_op jit(solution)/shard_map/reshape | solution.py:68
  333.5 139.9 %all-to-all-done.1 = bf16[64,4,3,4096]{3,1,2,0:T(4,128)(2,1)} async-done(((bf16[64,4,3,4096]{3,1,2,0:T(4,128)(2,1)}), bf16[64,4,3,4096]{3,1,2,0:T(4,128)(2,1)}, u32[]{:S(2)}, u32[]{:S(2)}) %all-to-all-start.1) | async-done | bytes 6291488 | tf_op jit(solution)/shard_map/all_to_all | solution.py:131
  473.5 10.2 %fusion.15 = bf16[4,16,4096]{2,1,0:T(8,128)(2,1)} fusion(bf16[4,16,64,3]{2,1,3,0:T(8,128)(2,1)S(1)} %copy.174, bf16[64,4,3,4096]{3,1,2,0:T(4,128)(2,1)} %all-to-all-done.1), kind=kOutput, calls=%fused_computation.17 | convolution fusion | flops 100925440 | bytes 6840320 | tf_op jit(solution)/shard_map/orec,eocd->ord/dot_general | solution.py:132
  495.0 12.3 %all_gather.14 = bf16[64,192]{1,0:T(8,128)(2,1)S(1)} all-gather(bf16[16,192]{1,0:T(8,128)(2,1)S(1)} %get-tuple-element.22), channel_id=1, replica_groups=mesh['rep'=4,'exp'=64] {'rep'}, dimensions={0}, use_global_device_ids=true | all-gather | bytes 30720 | tf_op jit(solution)/shard_map/all_gather | solution.py:117
  515.4 12.8 %all_gather.15 = bf16[64,4096]{1,0:T(8,128)(2,1)S(1)} all-gather(bf16[16,4096]{1,0:T(8,128)(2,1)S(1)} %multiply_convert_fusion), channel_id=1, replica_groups=mesh['rep'=4,'exp'=64] {'rep'}, dimensions={0}, use_global_device_ids=true | all-gather | bytes 655360 | tf_op jit(solution)/shard_map/all_gather | solution.py:116
  532.7 10.3 %copy.191 = bf16[64,4,3,4096]{3,1,2,0:T(4,128)(2,1)} copy(bf16[64,4,3,4096]{3,0,2,1:T(8,128)(2,1)} %fusion.5) | data formatting | bytes 12582912 | tf_op jit(solution)/shard_map/convert_element_type | solution.py:124
  543.0 147.1 %all_to_all.21 = bf16[64,4,3,4096]{3,1,2,0:T(4,128)(2,1)} all-to-all(bf16[64,4,3,4096]{3,1,2,0:T(4,128)(2,1)} %copy.191), channel_id=1, replica_groups=mesh['rep'=4,'exp'=64] {'exp'}, dimensions={0} | all-to-all | bytes 12582912 | tf_op jit(solution)/shard_map/all_to_all | solution.py:126
  690.1 16.1 %copy.192 = bf16[64,4,3,4096]{3,2,1,0:T(4,128)(2,1)} copy(bf16[64,4,3,4096]{3,1,2,0:T(4,128)(2,1)} %all_to_all.21) | data formatting | bytes 12582912 | tf_op jit(solution)/shard_map/all_to_all | solution.py:126
  706.2 13.7 %reshape.222 = bf16[768,4096]{1,0:T(8,128)(2,1)} reshape(bf16[64,4,3,4096]{3,2,1,0:T(4,128)(2,1)} %copy.192) | data formatting | bytes 12582912 | tf_op jit(solution)/shard_map/reshape | solution.py:63
  726.0 12.7 %convolution_convert_fusion = bf16[768,4096]{1,0:T(8,128)(2,1)} fusion(bf16[1,256,4096]{2,1,0:T(8,128)(2,1)S(1)} %copy-done, bf16[768,4096]{1,0:T(8,128)(2,1)} %reshape.222, bf16[1,4096,256]{2,1,0:T(8,128)(2,1)} %param.28, f32[768,256]{1,0:T(8,128)} %fusion.32), kind=kOutput, calls=%fused_computation.4 | convolution fusion | flops 3225550848 | bytes 17563648 | tf_op jit(solution)/shard_map/dot_general | solution.py:67
  738.7 13.1 %reshape.223 = bf16[64,4,3,4096]{3,2,1,0:T(4,128)(2,1)} reshape(bf16[768,4096]{1,0:T(8,128)(2,1)} %convolution_convert_fusion) | data formatting | bytes 12582912 | tf_op jit(solution)/shard_map/reshape | solution.py:68
  751.8 21.6 %copy.193 = bf16[64,4,3,4096]{3,1,2,0:T(4,128)(2,1)} copy(bf16[64,4,3,4096]{3,2,1,0:T(4,128)(2,1)} %reshape.223) | data formatting | bytes 12582912 | tf_op jit(solution)/shard_map/reshape | solution.py:68
  773.4 146.6 %all_to_all.22 = bf16[64,4,3,4096]{3,1,2,0:T(4,128)(2,1)S(1)} all-to-all(bf16[64,4,3,4096]{3,1,2,0:T(4,128)(2,1)} %copy.193), channel_id=1, replica_groups=mesh['rep'=4,'exp'=64] {'exp'}, dimensions={0} | all-to-all | bytes 12582912 | tf_op jit(solution)/shard_map/all_to_all | solution.py:131
  920.0 7.4 fusion.12
  927.4 18.0 %reduce-scatter.5.cloned.1.call-done = bf16[16,4096]{1,0:T(8,128)(2,1)} async-done(((bf16[64,4096]{1,0:T(8,128)(2,1)}), bf16[16,4096]{1,0:T(8,128)(2,1)}) %reduce-scatter.5.cloned.1.call-update) | async-done | bytes 131088 | tf_op jit(solution)/shard_map/reduce_scatter | solution.py:135
  (138 shorter events, 84.5 us)
Async XLA Ops:
  6.5 272.7 %copy-start = (bf16[1,256,4096]{2,1,0:T(8,128)(2,1)S(1)}, bf16[1,256,4096]{2,1,0:T(8,128)(2,1)}, u32[]{:S(2)}) copy-start(bf16[1,256,4096]{2,1,0:T(8,128)(2,1)} %param.29) | copy-start | bytes 6291460
  6.5 3.2 copy-start.1
  6.5 5.3 copy-start.17
  6.5 5.4 copy-start.9
  11.1 8.7 copy-start.5
  11.2 25.4 %copy-start.15 = (pred[16]{0:T(512)(128)(4,1)}, pred[16]{0:T(512)(128)(4,1)S(1)}, u32[]{:S(2)}) copy-start(pred[16]{0:T(512)(128)(4,1)S(1)} %iota_compare_fusion.3) | copy-start | bytes 52
  11.9 12.0 %copy-start.18 = (s32[8]{0:T(128)}, s32[8]{0:T(128)S(1)}, u32[]{:S(2)}) copy-start(s32[8]{0:T(128)S(1)} %get-tuple-element.23) | copy-start | bytes 100
  19.9 8.0 copy-start.11
  27.9 8.1 copy-start.6
  37.0 2.8 copy-start.2
  39.9 4.0 copy-start.3
  43.9 1.4 copy-start.4
  43.9 1.8 copy-start.7
  43.9 15.5 %copy-start.13 = (s32[2,1,16,8]{2,3,1,0:T(8,128)S(1)}, s32[2,1,16,8]{2,3,1,0:T(8,128)}, u32[]{:S(2)}) copy-start(s32[2,1,16,8]{2,3,1,0:T(8,128)} %param.25) | copy-start | bytes 3076
  45.2 15.6 %copy-start.14 = (bf16[2,1,16,8]{2,3,1,0:T(8,128)(2,1)S(1)}, bf16[2,1,16,8]{2,3,1,0:T(8,128)(2,1)}, u32[]{:S(2)}) copy-start(bf16[2,1,16,8]{2,3,1,0:T(8,128)(2,1)} %param.26) | copy-start | bytes 1540
  326.5 5.9 copy-start.16
  326.5 7.0 copy-start.10
  326.5 147.0 %all-to-all-start.1 = ((bf16[64,4,3,4096]{3,1,2,0:T(4,128)(2,1)}), bf16[64,4,3,4096]{3,1,2,0:T(4,128)(2,1)}, u32[]{:S(2)}, u32[]{:S(2)}) async-start(bf16[64,4,3,4096]{3,1,2,0:T(4,128)(2,1)} %copy.173), calls=%async_computation.1 | async-start | bytes 12582912 | tf_op jit(solution)/shard_map/all_to_all | solution.py:131
  332.3 180.4 %reduce-scatter.3.cloned.1.call-start = ((), (), s32[]{:S(2)}) async-start(), calls=%async_computation.6 | async-start | bytes 655360 | tf_op jit(solution)/shard_map/reduce_scatter | solution.py:135
  333.5 153.4 %copy-start.12 = (bf16[2,1,16,512]{3,2,1,0:T(8,128)(2,1)S(1)}, bf16[2,1,16,512]{3,2,1,0:T(8,128)(2,1)}, u32[]{:S(2)}) copy-start(bf16[2,1,16,512]{3,2,1,0:T(8,128)(2,1)} %param.23) | copy-start | bytes 98308
  483.7 461.7 %reduce-scatter.5.cloned.1.call-start = ((), (), s32[]{:S(2)}) async-start(), calls=%async_computation.7 | async-start | bytes 655360 | tf_op jit(solution)/shard_map/reduce_scatter | solution.py:135
  507.8 6.0 copy-start.8
Sparse Core Ops, SparseCore 0:
  483.8 18.0 reduce-scatter.2
  927.6 17.8 reduce-scatter.4
where the time goes:
time: 966 us; the launch traced here: 954 us
  blocking collectives  498 us (52%)
  local copies, waits for them, and re-layouts  190 us (20%)
  waiting for transfers between devices  158 us (16%)
  matrix products  80.4 us (8%)
  between operations  15 us (2%)
    all_to_all x2, blocking collectives, on_device(): lax.all_to_all(dispatched, 'exp', split_axis=0, concat_axis=0, tiled=True)  301 us
    all_to_all x1, blocking collectives, on_device(): lax.all_to_all(produced, 'exp', split_axis=0, concat_axis=0, tiled=True)  147 us
    all_to_all x1, waiting for transfers between devices, on_device(): lax.all_to_all(produced, 'exp', split_axis=0, concat_axis=0, tiled=True)  140 us
    reshape x4, local copies, waits for them, and re-layouts, expert_terms(): return produced.reshape(routed_rows.shape)  69.2 us
    all_to_all x2, local copies, waits for them, and re-layouts, on_device(): lax.all_to_all(dispatched, 'exp', split_axis=0, concat_axis=0, tiled=True)  32.2 us
    reshape x2, local copies, waits for them, and re-layouts, expert_terms(): flat_rows = routed_rows.reshape(-1, routed_rows.shape[-1])  27.9 us
    all_gather x2, blocking collectives, on_device(): lax.all_gather(normed, 'rep', axis=0, tiled=True)  26.2 us
    dot_general x2, matrix products, expert_terms(): jnp.dot(hidden, down_part, preferred_element_type=jnp.float32)  25.4 us
  transfers between devices with their start and end apart: 3, of which 2 were waited for; matrix products, arithmetic and copies ran while one was open for 2% of the time, Pallas kernels for 0%

commit v1 on v0

v1 whole, which is shorter than its diff:
```python
import jax
import jax.numpy as jnp
from jax import lax
from jax.experimental import pallas as pl
from jax.experimental.pallas import tpu as pltpu
from jax.sharding import PartitionSpec as P

H = 32
KVH = 4
GROUP = H // KVH
HD = 128
D = H * HD
TOP = 8
BLOCK = 8
ROWS = 16
CAP = 3
EXPERTS = 64
SLOTS = EXPERTS * CAP
CACHE = 2048
QUARTER = 256
NEG = -1e30
VMEM_LIMIT = 56 * 1024 * 1024


def smem_spec():
    return pl.BlockSpec(memory_space=pltpu.SMEM)


def each_slot(ids_ref, denoise, counts, visit):
    for e in range(EXPERTS):
        counts[e] = 0

    @pl.loop(0, ROWS)
    def _(t):
        picked = []
        for j in range(TOP):
            e = ids_ref[denoise, 0, t, j]
            c = counts[e]
            counts[e] = c + 1
            picked.append(e * CAP + jnp.minimum(c, CAP - 1))
        visit(t, picked)


def normalize(residual, gain):
    inverse = lax.rsqrt(jnp.mean(residual * residual, axis=-1, keepdims=True) + 1e-06)
    return residual * inverse * gain


def dispatch(normed, ids_ref, denoise, counts, spread, packed, send_ref):
    for k in range(H):
        spread[pl.ds(k, ROWS, stride=H), :] = normed[:, k * HD : (k + 1) * HD]
    packed[...] = spread[...].reshape(ROWS, H, HD).astype(jnp.bfloat16)
    send_ref[...] = jnp.zeros_like(send_ref)

    def visit(t, picked):
        row = packed[t]
        for slot in picked:
            send_ref[slot] = row

    each_slot(ids_ref, denoise, counts, visit)


def combine(terms_ref, ids_ref, gates_ref, denoise, counts, spread):
    def visit(t, picked):
        total = jnp.zeros((H, HD), jnp.float32)
        for j, slot in enumerate(picked):
            total = total + gates_ref[denoise, 0, t, j] * terms_ref[slot].astype(jnp.float32)
        spread[pl.ds(pl.multiple_of(t * H, H), H), :] = total

    each_slot(ids_ref, denoise, counts, visit)
    return jnp.concatenate([spread[pl.ds(k, ROWS, stride=H), :] for k in range(H)], axis=1)


def attend_head(denoise, lengths_ref, drift_ref, q_ref, k_ref, v_ref, nk_ref, nv_ref, bias, attended):
    head = pl.program_id(0)
    extra = ROWS * (denoise + 1)

    @pl.when(head == 0)
    def _():
        place = lax.broadcasted_iota(jnp.int32, (1, CACHE), 1)
        admitted = place < lengths_ref[0]
        for step in range(denoise + 1):
            for b in range(BLOCK):
                admitted = admitted & (place != drift_ref[step, 0, b])
        bias[...] = jnp.where(admitted, 0.0, NEG)

    queries = jnp.concatenate([q_ref[:, g * HD : (g + 1) * HD] for g in range(GROUP)], axis=0)
    contract_last = (((1,), (1,)), ((), ()))
    scale = HD ** (-0.5)
    scores = lax.dot_general(queries, k_ref[...], contract_last, preferred_element_type=jnp.float32)
    scores = scores * scale + bias[...]
    fresh_k = nk_ref[0 : denoise + 1].reshape(extra, HD)
    fresh_v = nv_ref[0 : denoise + 1].reshape(extra, HD)
    fresh = lax.dot_general(queries, fresh_k, contract_last, preferred_element_type=jnp.float32)
    row = lax.broadcasted_iota(jnp.int32, (GROUP * ROWS, extra), 0)
    col = lax.broadcasted_iota(jnp.int32, (GROUP * ROWS, extra), 1)
    place = col % ROWS
    allowed = (col >= denoise * ROWS) & ((place >= BLOCK) | (row % ROWS < BLOCK))
    if denoise == 1:
        for b in range(BLOCK):
            kept = drift_ref[1, 0, 0] != drift_ref[0, 0, b]
            for other in range(1, BLOCK):
                kept = kept & (drift_ref[1, 0, other] != drift_ref[0, 0, b])
            allowed = allowed | ((col == BLOCK + b) & kept)
    fresh = jnp.where(allowed, fresh * scale, NEG)
    peak = jnp.maximum(
        jnp.max(scores, axis=-1, keepdims=True), jnp.max(fresh, axis=-1, keepdims=True)
    )
    scores = jnp.exp(scores - peak)
    fresh = jnp.exp(fresh - peak)
    denom = jnp.sum(scores, axis=-1, keepdims=True) + jnp.sum(fresh, axis=-1, keepdims=True)
    mixed = jnp.dot(scores.astype(jnp.bfloat16), v_ref[...], preferred_element_type=jnp.float32)
    mixed = mixed + jnp.dot(fresh.astype(jnp.bfloat16), fresh_v, preferred_element_type=jnp.float32)
    mixed = mixed / denom
    wide = jnp.concatenate([mixed[g * ROWS : (g + 1) * ROWS] for g in range(GROUP)], axis=1)
    attended[:, pl.ds(pl.multiple_of(head * GROUP * HD, GROUP * HD), GROUP * HD)] = wide


def attention_specs(denoise):
    return [
        smem_spec(),
        smem_spec(),
        pl.BlockSpec((None, None, ROWS, GROUP * HD), lambda h: (denoise, 0, 0, h)),
        pl.BlockSpec((None, CACHE, HD), lambda h: (0, 0, h)),
        pl.BlockSpec((None, CACHE, HD), lambda h: (0, 0, h)),
        pl.BlockSpec((2, None, ROWS, HD), lambda h: (0, 0, 0, h)),
        pl.BlockSpec((2, None, ROWS, HD), lambda h: (0, 0, 0, h)),
    ]


def first_attention(lengths, drift_rows, queries, keys, values, new_keys, new_values, block_in, drift_in, gain, ids):
    def body(lengths_ref, drift_ref, q_ref, k_ref, v_ref, nk_ref, nv_ref, block_ref, drift_in_ref, gain_ref, ids_ref,
             residual_ref, send_ref, bias, attended, spread, packed, counts):
        attend_head(0, lengths_ref, drift_ref, q_ref, k_ref, v_ref, nk_ref, nv_ref, bias, attended)

        @pl.when(pl.program_id(0) == KVH - 1)
        def _():
            inputs = jnp.concatenate(
                [block_ref[...].astype(jnp.float32), drift_in_ref[...].astype(jnp.float32)], axis=0
            )
            residual = inputs + attended[...]
            residual_ref[...] = residual
            dispatch(normalize(residual, gain_ref[...]), ids_ref, 0, counts, spread, packed, send_ref)

    return pl.pallas_call(
        body,
        grid=(KVH,),
        in_specs=attention_specs(0)
        + [
            pl.BlockSpec((None, BLOCK, D), lambda h: (0, 0, 0)),
            pl.BlockSpec((None, None, BLOCK, D), lambda h: (0, 0, 0, 0)),
            pl.BlockSpec((1, D), lambda h: (0, 0)),
            smem_spec(),
        ],
        out_specs=[
            pl.BlockSpec((ROWS, D), lambda h: (0, 0)),
            pl.BlockSpec((SLOTS, H, HD), lambda h: (0, 0, 0)),
        ],
        out_shape=[
            jax.ShapeDtypeStruct((ROWS, D), jnp.float32),
            jax.ShapeDtypeStruct((SLOTS, H, HD), jnp.bfloat16),
        ],
        scratch_shapes=[
            pltpu.VMEM((1, CACHE), jnp.float32),
            pltpu.VMEM((ROWS, D), jnp.float32),
            pltpu.VMEM((ROWS * H, HD), jnp.float32),
            pltpu.VMEM((ROWS, H, HD), jnp.bfloat16),
            pltpu.SMEM((EXPERTS,), jnp.int32),
        ],
        compiler_params=pltpu.CompilerParams(vmem_limit_bytes=VMEM_LIMIT),
        name="first_attention",
    )(lengths, drift_rows, queries, keys, values, new_keys, new_values, block_in, drift_in, gain, ids)


def second_attention(lengths, drift_rows, queries, keys, values, new_keys, new_values):
    def body(lengths_ref, drift_ref, q_ref, k_ref, v_ref, nk_ref, nv_ref, attended, bias):
        attend_head(1, lengths_ref, drift_ref, q_ref, k_ref, v_ref, nk_ref, nv_ref, bias, attended)

    return pl.pallas_call(
        body,
        grid=(KVH,),
        in_specs=attention_specs(1),
        out_specs=pl.BlockSpec((ROWS, D), lambda h: (0, 0)),
        out_shape=jax.ShapeDtypeStruct((ROWS, D), jnp.float32),
        scratch_shapes=[pltpu.VMEM((1, CACHE), jnp.float32)],
        compiler_params=pltpu.CompilerParams(vmem_limit_bytes=VMEM_LIMIT),
        name="second_attention",
    )(lengths, drift_rows, queries, keys, values, new_keys, new_values)


def expert_half(rows, weights):
    pieces = len(weights) // 3

    def body(*refs):
        rows_ref = refs[0]
        weight_refs = refs[1 : 1 + 3 * pieces]
        out_ref = refs[1 + 3 * pieces]
        gate, up, down, spread, flat, hidden, sems = refs[2 + 3 * pieces :]
        copies = []
        for p in range(pieces):
            for kind, target in enumerate((gate, up, down)):
                copies.append(
                    pltpu.make_async_copy(
                        weight_refs[3 * p + kind], target.at[p], sems.at[3 * p + kind]
                    )
                )
        for copy in copies:
            copy.start()
        spread[...] = rows_ref[...].reshape(SLOTS * H, HD).astype(jnp.float32)
        for k in range(H):
            flat[:, k * HD : (k + 1) * HD] = spread[pl.ds(k, SLOTS, stride=H), :].astype(jnp.bfloat16)
        for p in range(pieces):
            copies[3 * p].wait()
            gated = jnp.dot(flat[...], gate[p], preferred_element_type=jnp.float32)
            copies[3 * p + 1].wait()
            raised = jnp.dot(flat[...], up[p], preferred_element_type=jnp.float32)
            hidden[p] = (jax.nn.silu(gated) * raised).astype(jnp.bfloat16)
        for p in range(pieces):
            copies[3 * p + 2].wait()
        width = 512
        for n in range(D // width):
            part = jnp.zeros((SLOTS, width), jnp.float32)
            for p in range(pieces):
                part = part + jnp.dot(
                    hidden[p], down[p, :, n * width : (n + 1) * width], preferred_element_type=jnp.float32
                )
            for k in range(width // HD):
                spread[pl.ds(n * (width // HD) + k, SLOTS, stride=H), :] = part[:, k * HD : (k + 1) * HD]
        out_ref[...] = spread[...].reshape(SLOTS, H, HD).astype(jnp.bfloat16)

    return pl.pallas_call(
        body,
        in_specs=[pl.BlockSpec(memory_space=pltpu.VMEM)] + [pl.BlockSpec(memory_space=pl.ANY)] * (3 * pieces),
        out_specs=pl.BlockSpec(memory_space=pltpu.VMEM),
        out_shape=jax.ShapeDtypeStruct((SLOTS, H, HD), jnp.bfloat16),
        scratch_shapes=[
            pltpu.VMEM((pieces, D, QUARTER), jnp.bfloat16),
            pltpu.VMEM((pieces, D, QUARTER), jnp.bfloat16),
            pltpu.VMEM((pieces, QUARTER, D), jnp.bfloat16),
            pltpu.VMEM((SLOTS * H, HD), jnp.float32),
            pltpu.VMEM((SLOTS, D), jnp.bfloat16),
            pltpu.VMEM((pieces, SLOTS, QUARTER), jnp.bfloat16),
            pltpu.SemaphoreType.DMA((3 * pieces,)),
        ],
        compiler_params=pltpu.CompilerParams(vmem_limit_bytes=VMEM_LIMIT),
        name="expert_half",
    )(rows, *weights)


def combine_and_dispatch(terms, residual, attended, drift_in, gain, ids, gates):
    def body(terms_ref, residual_ref, attended_ref, drift_in_ref, gain_ref, ids_ref, gates_ref,
             result_ref, next_ref, send_ref, spread, packed, counts):
        moe = combine(terms_ref, ids_ref, gates_ref, 0, counts, spread)
        result = (residual_ref[...] + moe).astype(jnp.bfloat16)
        result_ref[...] = result
        inputs = jnp.concatenate(
            [result.astype(jnp.float32)[:BLOCK], drift_in_ref[1, 0].astype(jnp.float32)], axis=0
        )
        following = inputs + attended_ref[...]
        next_ref[...] = following
        dispatch(normalize(following, gain_ref[...]), ids_ref, 1, counts, spread, packed, send_ref)

    vmem = pl.BlockSpec(memory_space=pltpu.VMEM)
    return pl.pallas_call(
        body,
        in_specs=[vmem] * 5 + [smem_spec()] * 2,
        out_specs=[vmem] * 3,
        out_shape=[
            jax.ShapeDtypeStruct((ROWS, D), jnp.bfloat16),
            jax.ShapeDtypeStruct((ROWS, D), jnp.float32),
            jax.ShapeDtypeStruct((SLOTS, H, HD), jnp.bfloat16),
        ],
        scratch_shapes=[
            pltpu.VMEM((ROWS * H, HD), jnp.float32),
            pltpu.VMEM((ROWS, H, HD), jnp.bfloat16),
            pltpu.SMEM((EXPERTS,), jnp.int32),
        ],
        compiler_params=pltpu.CompilerParams(vmem_limit_bytes=VMEM_LIMIT),
        name="combine_and_dispatch",
    )(terms, residual, attended, drift_in, gain, ids, gates)


def combine_last(terms, residual, first_result, ids, gates):
    def body(terms_ref, residual_ref, first_ref, ids_ref, gates_ref, out_ref, spread, counts):
        moe = combine(terms_ref, ids_ref, gates_ref, 1, counts, spread)
        out_ref[0, 0] = first_ref[...]
        out_ref[1, 0] = (residual_ref[...] + moe).astype(jnp.bfloat16)

    vmem = pl.BlockSpec(memory_space=pltpu.VMEM)
    return pl.pallas_call(
        body,
        in_specs=[vmem] * 3 + [smem_spec()] * 2,
        out_specs=vmem,
        out_shape=jax.ShapeDtypeStruct((2, 1, ROWS, D), jnp.bfloat16),
        scratch_shapes=[
            pltpu.VMEM((ROWS * H, HD), jnp.float32),
            pltpu.SMEM((EXPERTS,), jnp.int32),
        ],
        compiler_params=pltpu.CompilerParams(vmem_limit_bytes=VMEM_LIMIT),
        name="combine_last",
    )(terms, residual, first_result, ids, gates)


def pairings(reps, exps):
    across, beside = [], []
    for r in range(reps):
        for e in range(exps):
            near, far = r ^ 1, reps - 1 - r
            if e % 2:
                near, far = far, near
            beside.append((r * exps + e, near * exps + e))
            across.append((r * exps + e, far * exps + e))
    return beside, across


def on_device(
    cache_keys,
    cache_values,
    lengths,
    drift_rows,
    block_in,
    drift_in,
    queries,
    new_keys,
    new_values,
    norm_gain,
    expert_ids,
    gate_weights,
    w_gate,
    w_up,
    w_down,
):
    axes = ("rep", "exp")
    beside, across = pairings(lax.axis_size("rep"), lax.axis_size("exp"))
    own = (w_gate[0], w_up[0], w_down[0])
    paired = tuple(lax.ppermute(part, axes, beside) for part in own)
    weights = own + paired
    gain = norm_gain.reshape(1, D)
    gates = gate_weights.astype(jnp.float32)

    residual, send = first_attention(
        lengths, drift_rows, queries, cache_keys, cache_values, new_keys, new_values,
        block_in, drift_in, gain, expert_ids,
    )
    attended = second_attention(
        lengths, drift_rows, queries, cache_keys, cache_values, new_keys, new_values
    )

    def experts(send):
        rows = lax.all_to_all(send, "exp", split_axis=0, concat_axis=0, tiled=True)
        visiting = lax.ppermute(rows, axes, across)
        home_terms = expert_half(rows, weights)
        away_terms = lax.ppermute(expert_half(visiting, weights), axes, across)
        terms = (home_terms.astype(jnp.float32) + away_terms.astype(jnp.float32)).astype(jnp.bfloat16)
        return lax.all_to_all(terms, "exp", split_axis=0, concat_axis=0, tiled=True)

    terms = experts(send)
    result, residual, send = combine_and_dispatch(
        terms, residual, attended, drift_in, gain, expert_ids, gates
    )
    terms = experts(send)
    return combine_last(terms, residual, result, expert_ids, gates)


def solution(mesh):
    placed = (
        P(("rep", "exp"), None, None),
        P(("rep", "exp"), None, None),
        P(("rep", "exp")),
        P(None, ("rep", "exp"), None),
        P(("rep", "exp"), None, None),
        P(None, ("rep", "exp"), None, None),
        P(None, ("rep", "exp"), None, None),
        P(None, ("rep", "exp"), None, None),
        P(None, ("rep", "exp"), None, None),
        P(),
        P(None, ("rep", "exp"), None, None),
        P(None, ("rep", "exp"), None, None),
        P("exp", None, "rep"),
        P("exp", None, "rep"),
        P("exp", "rep", None),
    )
    return jax.shard_map(
        on_device,
        mesh=mesh,
        in_specs=placed,
        out_specs=P(None, ("rep", "exp"), None, None),
        check_vma=False,
    )
```

time: 966 us -> 363 us (0.38)
  blocking collectives: 498 us -> 90.8 us
  local copies, waits for them, and re-layouts: 190 us -> 5.11 us
  matrix products: 80.4 us -> 0 us
  Pallas kernels: 0 us -> 70.5 us
  starting transfers between devices: 5.9 us -> 27.5 us
  between operations: 15 us -> 1.01 us
    all_to_all x3 -> x2, blocking collectives: 447 us -> 90.8 us  [the longest x1 45.5 us: experts(): rows = lax.all_to_all(send, 'exp', split_axis=0, concat_axis=0, tiled=True)]
    reshape x14 -> x0, local copies, waits for them, and re-layouts: 114 us -> none  [the longest x4 69.2 us: expert_terms(): return produced.reshape(routed_rows.shape)]
    ppermute x0 -> x7, waiting for transfers between devices: none -> 87.6 us  [the longest x3 47.3 us: on_device(): paired = tuple((lax.ppermute(part, axes, beside) for part in own))]
    dot_general x16 -> x0, matrix products: 80.4 us -> none  [the longest x2 25.4 us: expert_terms(): jnp.dot(hidden, down_part, preferred_element_type=jnp.float32)]
    pallas_call x0 -> x8, Pallas kernels: none -> 70.5 us  [the longest x4 48.7 us: expert_half(): pl.pallas_call(body, in_specs=[pl.BlockSpec(memory_space=pltpu.VMEM)] + [...]
    all_to_all x1 -> x2, waiting for transfers between devices: 140 us -> 70.6 us  [the longest x1 37.1 us: experts(): rows = lax.all_to_all(send, 'exp', split_axis=0, concat_axis=0, tiled=True)]
    all_gather x4 -> x0, blocking collectives: 50.7 us -> none  [the longest x2 26.2 us: on_device(): lax.all_gather(normed, 'rep', axis=0, tiled=True)]
    all_to_all x2 -> x0, local copies, waits for them, and re-layouts: 32.2 us -> none  [on_device(): lax.all_to_all(dispatched, 'exp', split_axis=0, concat_axis=0, tiled=True)]
  transfers between devices with their start and end apart: 3 -> 9, of which waited for: 2 -> 7; matrix products, arithmetic and copies ran while one was open for 2% -> 0% of each run, Pallas kernels for 0% -> 8%
where the time goes in v1:
time: 363 us; the launch traced here: 359 us
  waiting for transfers between devices  158 us (44%)
  blocking collectives  90.8 us (25%)
  Pallas kernels  70.5 us (19%)
  starting transfers between devices  27.5 us (8%)
  other arithmetic  5.48 us (2%)
  local copies, waits for them, and re-layouts  5.11 us (1%)
    pallas_call x4, Pallas kernels, expert_half(): pl.pallas_call(body, in_specs=[pl.BlockSpec(memory_space=pltpu.VMEM)] + [...  48.7 us
    ppermute x3, waiting for transfers between devices, on_device(): paired = tuple((lax.ppermute(part, axes, beside) for part in own))  47.3 us
    all_to_all x1, blocking collectives, experts(): rows = lax.all_to_all(send, 'exp', split_axis=0, concat_axis=0, tiled=True)  45.5 us
    all_to_all x1, blocking collectives, experts(): return lax.all_to_all(terms, 'exp', split_axis=0, concat_axis=0, tiled=True)  45.4 us
    all_to_all x1, waiting for transfers between devices, experts(): rows = lax.all_to_all(send, 'exp', split_axis=0, concat_axis=0, tiled=True)  37.1 us
    all_to_all x1, waiting for transfers between devices, experts(): return lax.all_to_all(terms, 'exp', split_axis=0, concat_axis=0, tiled=True)  33.5 us
    ppermute x2, waiting for transfers between devices, experts(): visiting = lax.ppermute(rows, axes, across)  21.4 us
    ppermute x2, waiting for transfers between devices, experts(): away_terms = lax.ppermute(expert_half(visiting, weights), axes, across)  18.8 us
  transfers between devices with their start and end apart: 9, of which 7 were waited for; matrix products, arithmetic and copies ran while one was open for 0% of the time, Pallas kernels for 8%

profile of v1, /device:TPU:24, one launch (start us, length us, event | category | flops | bytes accessed | tf_op | source)
XLA Modules:
  0.0 358.6 jit_solution(17839868899426255769)
XLA Ops:
  0.0 1.4 copy.16.ids_ref
  2.0 7.8 %first_attention.1 = (f32[16,4096]{1,0:T(8,128)}, bf16[192,32,128]{2,1,0:T(8,128)(2,1)}) custom-call(s32[1]{0:T(128)S(6)} %copy.20.lengths_ref, s32[2,1,8]{2,1,0:T(1,128)} %drift_ref.3, bf16[2,1,16,4096]{3,2,1,0:T(8,128)(2,1)} %q_ref.3, bf16[1,2048,512]{2,1,0:T(8,128)(2,1)} %k_ref.3, bf16[1,2048,512]{2,1,0:T(8,128)(2,1)} %v_ref.3, ...), custom_call_target="tpu_custom_call" | custom-call | tf_op jit(solution)/shard_map/first_attention/pallas_call | solution.py:145
  9.8 12.3 %all-to-all-start = ((bf16[192,32,128]{2,1,0:T(8,128)(2,1)}), bf16[192,32,128]{2,1,0:T(8,128)(2,1)}, u32[]{:S(2)}, u32[]{:S(2)}) async-start(bf16[192,32,128]{2,1,0:T(8,128)(2,1)} %get-tuple-element.10), calls=%async_computation | async-start | bytes 3145728 | tf_op jit(solution)/shard_map/all_to_all | solution.py:350
  23.0 1.3 collective-permute-start.1
  25.0 37.1 %all-to-all-done.refs_0_ = bf16[192,32,128]{2,1,0:T(8,128)(2,1)} async-done(((bf16[192,32,128]{2,1,0:T(8,128)(2,1)}), bf16[192,32,128]{2,1,0:T(8,128)(2,1)}, u32[]{:S(2)}, u32[]{:S(2)}) %all-to-all-start) | async-done | bytes 1572896 | tf_op jit(solution)/shard_map/all_to_all | solution.py:350
  62.9 14.3 %collective-permute-done.1.refs_5_ = bf16[4096,256]{1,0:T(8,128)(2,1)} collective-permute-done((bf16[4096,256]{1,0:T(8,128)(2,1)}, bf16[4096,256]{1,0:T(8,128)(2,1)}, u32[]{:S(2)}, u32[]{:S(2)}) %collective-permute-start.1) | collective-permute-done | bytes 2097184 | tf_op jit(solution)/shard_map/ppermute | solution.py:336
  77.1 33.0 %collective-permute-done.2.refs_6_ = bf16[256,4096]{1,0:T(8,128)(2,1)} collective-permute-done((bf16[256,4096]{1,0:T(8,128)(2,1)}, bf16[256,4096]{1,0:T(8,128)(2,1)}, u32[]{:S(2)}, u32[]{:S(2)}) %collective-permute-start.2) | collective-permute-done | bytes 2097184 | tf_op jit(solution)/shard_map/ppermute | solution.py:336
  111.4 12.1 %expert_half.5 = bf16[192,32,128]{2,1,0:T(8,128)(2,1)} custom-call(bf16[192,32,128]{2,1,0:T(8,128)(2,1)} %copy-done.3, bf16[4096,256]{1,0:T(8,128)(2,1)} %bitcast.4, bf16[4096,256]{1,0:T(8,128)(2,1)} %bitcast.10, bf16[256,4096]{1,0:T(8,128)(2,1)} %bitcast.15, bf16[4096,256]{1,0:T(8,128)(2,1)} %collective-permute-done.refs_4_, ...), custom_call_target="tpu_custom_call" | custom-call | tf_op jit(solution)/shard_map/expert_half/pallas_call | solution.py:231
  124.0 12.2 %expert_half.4 = bf16[192,32,128]{2,1,0:T(8,128)(2,1)} custom-call(bf16[192,32,128]{2,1,0:T(8,128)(2,1)} %all-to-all-done.refs_0_, bf16[4096,256]{1,0:T(8,128)(2,1)} %bitcast.5, bf16[4096,256]{1,0:T(8,128)(2,1)} %bitcast.11, bf16[256,4096]{1,0:T(8,128)(2,1)} %bitcast.16, bf16[4096,256]{1,0:T(8,128)(2,1)} %collective-permute-done.refs_4_, ...), custom_call_target="tpu_custom_call" | custom-call | tf_op jit(solution)/shard_map/expert_half/pallas_call | solution.py:231
  136.3 9.4 %collective-permute-done.4 = bf16[192,32,128]{2,1,0:T(8,128)(2,1)S(1)} collective-permute-done((bf16[192,32,128]{2,1,0:T(8,128)(2,1)}, bf16[192,32,128]{2,1,0:T(8,128)(2,1)S(1)}, u32[]{:S(2)}, u32[]{:S(2)}) %collective-permute-start.4) | collective-permute-done | bytes 1572896 | tf_op jit(solution)/shard_map/ppermute | solution.py:353
  145.7 3.1 add_convert_fusion.1
  148.7 10.2 %all-to-all-start.1 = ((bf16[192,32,128]{2,1,0:T(8,128)(2,1)}), bf16[192,32,128]{2,1,0:T(8,128)(2,1)S(1)}, u32[]{:S(2)}, u32[]{:S(2)}) async-start(bf16[192,32,128]{2,1,0:T(8,128)(2,1)} %add_convert_fusion.1), calls=%async_computation.1 | async-start | bytes 3145728 | tf_op jit(solution)/shard_map/all_to_all | solution.py:355
  159.0 6.0 %second_attention.1.attended_ref = f32[16,4096]{1,0:T(8,128)} custom-call(s32[1]{0:T(128)S(6)} %copy.20.lengths_ref, s32[2,1,8]{2,1,0:T(1,128)} %drift_ref.3, bf16[2,1,16,4096]{3,2,1,0:T(8,128)(2,1)} %q_ref.3, bf16[1,2048,512]{2,1,0:T(8,128)(2,1)} %k_ref.3, bf16[1,2048,512]{2,1,0:T(8,128)(2,1)} %v_ref.3, bf16[2,1,16,512]{3,2,1,0:T(8,128)(2,1)} %nk_ref.3, ...), custom_call_target="tpu_custom_call" | custom-call | tf_op jit(solution)/shard_map/second_attention/pallas_call | solution.py:179
  165.6 33.5 %all-to-all-done.1.terms_ref = bf16[192,32,128]{2,1,0:T(8,128)(2,1)S(1)} async-done(((bf16[192,32,128]{2,1,0:T(8,128)(2,1)}), bf16[192,32,128]{2,1,0:T(8,128)(2,1)S(1)}, u32[]{:S(2)}, u32[]{:S(2)}) %all-to-all-start.1) | async-done | bytes 1572896 | tf_op jit(solution)/shard_map/all_to_all | solution.py:355
  199.1 1.2 copy-done.1
  200.3 4.9 %combine_and_dispatch.1 = (bf16[16,4096]{1,0:T(8,128)(2,1)}, f32[16,4096]{1,0:T(8,128)}, bf16[192,32,128]{2,1,0:T(8,128)(2,1)}) custom-call(bf16[192,32,128]{2,1,0:T(8,128)(2,1)} %copy-done.1, f32[16,4096]{1,0:T(8,128)} %get-tuple-element.11.residual_ref, f32[16,4096]{1,0:T(8,128)} %second_attention.1.attended_ref, bf16[2,1,8,4096]{3,2,1,0:T(8,128)(2,1)} %drift_in_ref.3, ...), custom_call_target="tpu_custom_call" | custom-call | tf_op jit(solution)/shard_map/combine_and_dispatch/pallas_call | solution.py:264
  205.3 45.5 %all_to_all.20.refs_0_ = bf16[192,32,128]{2,1,0:T(8,128)(2,1)S(1)} all-to-all(bf16[192,32,128]{2,1,0:T(8,128)(2,1)} %get-tuple-element.12), channel_id=1, replica_groups=mesh['rep'=4,'exp'=64] {'exp'}, dimensions={0} | all-to-all | bytes 3145728 | tf_op jit(solution)/shard_map/all_to_all | solution.py:350
  251.1 21.4 %collective-permute-done.5.refs_0_ = bf16[192,32,128]{2,1,0:T(8,128)(2,1)S(1)} collective-permute-done((bf16[192,32,128]{2,1,0:T(8,128)(2,1)S(1)}, bf16[192,32,128]{2,1,0:T(8,128)(2,1)S(1)}, u32[]{:S(2)}, u32[]{:S(2)}) %collective-permute-start.5) | collective-permute-done | bytes 1572896 | tf_op jit(solution)/shard_map/ppermute | solution.py:351
  273.7 12.2 %expert_half.7 = bf16[192,32,128]{2,1,0:T(8,128)(2,1)} custom-call(bf16[192,32,128]{2,1,0:T(8,128)(2,1)} %copy-done.4, bf16[4096,256]{1,0:T(8,128)(2,1)} %bitcast.6, bf16[4096,256]{1,0:T(8,128)(2,1)} %bitcast.12, bf16[256,4096]{1,0:T(8,128)(2,1)} %bitcast.17, bf16[4096,256]{1,0:T(8,128)(2,1)} %collective-permute-done.refs_4_, ...), custom_call_target="tpu_custom_call" | custom-call | tf_op jit(solution)/shard_map/expert_half/pallas_call | solution.py:231
  286.4 12.2 %expert_half.6 = bf16[192,32,128]{2,1,0:T(8,128)(2,1)} custom-call(bf16[192,32,128]{2,1,0:T(8,128)(2,1)} %copy-done.2, bf16[4096,256]{1,0:T(8,128)(2,1)} %bitcast.7, bf16[4096,256]{1,0:T(8,128)(2,1)} %bitcast.13, bf16[256,4096]{1,0:T(8,128)(2,1)} %bitcast.18, bf16[4096,256]{1,0:T(8,128)(2,1)} %collective-permute-done.refs_4_, ...), custom_call_target="tpu_custom_call" | custom-call | tf_op jit(solution)/shard_map/expert_half/pallas_call | solution.py:231
  298.6 9.5 %collective-permute-done.6 = bf16[192,32,128]{2,1,0:T(8,128)(2,1)S(1)} collective-permute-done((bf16[192,32,128]{2,1,0:T(8,128)(2,1)}, bf16[192,32,128]{2,1,0:T(8,128)(2,1)S(1)}, u32[]{:S(2)}, u32[]{:S(2)}) %collective-permute-start.6) | collective-permute-done | bytes 1572896 | tf_op jit(solution)/shard_map/ppermute | solution.py:353
  308.1 1.8 add_convert_fusion
  309.9 45.4 %all_to_all.21.terms_ref = bf16[192,32,128]{2,1,0:T(8,128)(2,1)} all-to-all(bf16[192,32,128]{2,1,0:T(8,128)(2,1)S(1)} %add_convert_fusion), channel_id=1, replica_groups=mesh['rep'=4,'exp'=64] {'exp'}, dimensions={0} | all-to-all | bytes 3145728 | tf_op jit(solution)/shard_map/all_to_all | solution.py:355
  355.3 3.1 combine_last.1
  (21 shorter events, 6.8 us)
Async XLA Ops:
  9.8 12.3 %copy-start = (bf16[1,4096,256]{2,1,0:T(8,128)(2,1)S(1)}, bf16[1,4096,256]{2,1,0:T(8,128)(2,1)}, u32[]{:S(2)}) copy-start(bf16[1,4096,256]{2,1,0:T(8,128)(2,1)} %param.27) | copy-start | bytes 6291460
  9.8 52.3 %all-to-all-start = ((bf16[192,32,128]{2,1,0:T(8,128)(2,1)}), bf16[192,32,128]{2,1,0:T(8,128)(2,1)}, u32[]{:S(2)}, u32[]{:S(2)}) async-start(bf16[192,32,128]{2,1,0:T(8,128)(2,1)} %get-tuple-element.10), calls=%async_computation | async-start | bytes 3145728 | tf_op jit(solution)/shard_map/all_to_all | solution.py:350
  22.1 40.7 %collective-permute-start = (bf16[4096,256]{1,0:T(8,128)(2,1)S(1)}, bf16[4096,256]{1,0:T(8,128)(2,1)}, u32[]{:S(2)}, u32[]{:S(2)}) collective-permute-start(bf16[4096,256]{1,0:T(8,128)(2,1)S(1)} %bitcast.8), channel_id=1, source_target_pairs={{0,64},{1,193},{2,66},{3,195},{4,68},{5,197},{6,70},{7,199},{8,72}... | collective-permute-start | bytes 6291464 | tf_op jit(solution)/shard_map/ppermute | solution.py:336
  23.0 54.2 %collective-permute-start.1 = (bf16[4096,256]{1,0:T(8,128)(2,1)}, bf16[4096,256]{1,0:T(8,128)(2,1)}, u32[]{:S(2)}, u32[]{:S(2)}) collective-permute-start(bf16[4096,256]{1,0:T(8,128)(2,1)} %bitcast.9), channel_id=1, source_target_pairs={{0,64},{1,193},{2,66},{3,195},{4,68},{5,197},{6,70},{7,199},{8,72}... | collective-permute-start | bytes 6291464 | tf_op jit(solution)/shard_map/ppermute | solution.py:336
  24.3 85.9 %collective-permute-start.2 = (bf16[256,4096]{1,0:T(8,128)(2,1)}, bf16[256,4096]{1,0:T(8,128)(2,1)}, u32[]{:S(2)}, u32[]{:S(2)}) collective-permute-start(bf16[256,4096]{1,0:T(8,128)(2,1)} %bitcast.14), channel_id=1, source_target_pairs={{0,64},{1,193},{2,66},{3,195},{4,68},{5,197},{6,70},{7,199},{8,72}... | collective-permute-start | bytes 6291464 | tf_op jit(solution)/shard_map/ppermute | solution.py:336
  62.1 48.0 %collective-permute-start.3 = (bf16[192,32,128]{2,1,0:T(8,128)(2,1)}, bf16[192,32,128]{2,1,0:T(8,128)(2,1)S(1)}, u32[]{:S(2)}, u32[]{:S(2)}) collective-permute-start(bf16[192,32,128]{2,1,0:T(8,128)(2,1)} %all-to-all-done.refs_0_), channel_id=1, source_target_pairs={{0,192},{1,65},{2,194},{3,67},{4,196},{5,69},{6,198},{7,71},{8,200... | collective-permute-start | bytes 4718600 | tf_op jit(solution)/shard_map/ppermute | solution.py:351
  110.2 1.2 copy-start.3
  123.6 22.1 %collective-permute-start.4 = (bf16[192,32,128]{2,1,0:T(8,128)(2,1)}, bf16[192,32,128]{2,1,0:T(8,128)(2,1)S(1)}, u32[]{:S(2)}, u32[]{:S(2)}) collective-permute-start(bf16[192,32,128]{2,1,0:T(8,128)(2,1)} %expert_half.5), channel_id=1, source_target_pairs={{0,192},{1,65},{2,194},{3,67},{4,196},{5,69},{6,198},{7,71},{8,200... | collective-permute-start | bytes 4718600 | tf_op jit(solution)/shard_map/ppermute | solution.py:353
  148.7 50.4 %all-to-all-start.1 = ((bf16[192,32,128]{2,1,0:T(8,128)(2,1)}), bf16[192,32,128]{2,1,0:T(8,128)(2,1)S(1)}, u32[]{:S(2)}, u32[]{:S(2)}) async-start(bf16[192,32,128]{2,1,0:T(8,128)(2,1)} %add_convert_fusion.1), calls=%async_computation.1 | async-start | bytes 3145728 | tf_op jit(solution)/shard_map/all_to_all | solution.py:355
  159.0 6.0 %copy-start.5 = (bf16[2,1,16,8]{2,3,1,0:T(8,128)(2,1)S(1)}, bf16[2,1,16,8]{2,3,1,0:T(8,128)(2,1)}, u32[]{:S(2)}) copy-start(bf16[2,1,16,8]{2,3,1,0:T(8,128)(2,1)} %param.26) | copy-start | bytes 1540
  199.1 1.2 copy-start.1
  250.7 35.2 %copy-start.2 = (bf16[192,32,128]{2,1,0:T(8,128)(2,1)}, bf16[192,32,128]{2,1,0:T(8,128)(2,1)S(1)}, u32[]{:S(2)}) copy-start(bf16[192,32,128]{2,1,0:T(8,128)(2,1)S(1)} %all_to_all.20.refs_0_) | copy-start | bytes 4718596
  250.7 21.8 %collective-permute-start.5 = (bf16[192,32,128]{2,1,0:T(8,128)(2,1)S(1)}, bf16[192,32,128]{2,1,0:T(8,128)(2,1)S(1)}, u32[]{:S(2)}, u32[]{:S(2)}) collective-permute-start(bf16[192,32,128]{2,1,0:T(8,128)(2,1)S(1)} %all_to_all.20.refs_0_), channel_id=1, source_target_pairs={{0,192},{1,65},{2,194},{3,67},{4,196},{5,69},{6,198},{7,71},{8,200... | collective-permute-start | bytes 4718600 | tf_op jit(solution)/shard_map/ppermute | solution.py:351
  272.5 1.2 copy-start.4
  285.9 22.2 %collective-permute-start.6 = (bf16[192,32,128]{2,1,0:T(8,128)(2,1)}, bf16[192,32,128]{2,1,0:T(8,128)(2,1)S(1)}, u32[]{:S(2)}, u32[]{:S(2)}) collective-permute-start(bf16[192,32,128]{2,1,0:T(8,128)(2,1)} %expert_half.7), channel_id=1, source_target_pairs={{0,192},{1,65},{2,194},{3,67},{4,196},{5,69},{6,198},{7,71},{8,200... | collective-permute-start | bytes 4718600 | tf_op jit(solution)/shard_map/ppermute | solution.py:353

commit v2 on v1

--- a/solution.py
+++ b/solution.py
@@ -195,7 +195,7 @@
         rows_ref = refs[0]
         weight_refs = refs[1 : 1 + 3 * pieces]
         out_ref = refs[1 + 3 * pieces]
-        gate, up, down, spread, flat, hidden, sems = refs[2 + 3 * pieces :]
+        gate, up, down, flat, hidden, sems = refs[2 + 3 * pieces :]
         copies = []
         for p in range(pieces):
             for kind, target in enumerate((gate, up, down)):
@@ -206,9 +206,9 @@
                 )
         for copy in copies:
             copy.start()
-        spread[...] = rows_ref[...].reshape(SLOTS * H, HD).astype(jnp.float32)
-        for k in range(H):
-            flat[:, k * HD : (k + 1) * HD] = spread[pl.ds(k, SLOTS, stride=H), :].astype(jnp.bfloat16)
+        for r in range(0, SLOTS, 16):
+            wide = rows_ref[r : r + 16].astype(jnp.float32).reshape(16, D)
+            flat[r : r + 16, :] = wide.astype(jnp.bfloat16)
         for p in range(pieces):
             copies[3 * p].wait()
             gated = jnp.dot(flat[...], gate[p], preferred_element_type=jnp.float32)
@@ -224,9 +224,8 @@
                 part = part + jnp.dot(
                     hidden[p], down[p, :, n * width : (n + 1) * width], preferred_element_type=jnp.float32
                 )
-            for k in range(width // HD):
-                spread[pl.ds(n * (width // HD) + k, SLOTS, stride=H), :] = part[:, k * HD : (k + 1) * HD]
-        out_ref[...] = spread[...].reshape(SLOTS, H, HD).astype(jnp.bfloat16)
+            heads = width // HD
+            out_ref[:, n * heads : (n + 1) * heads, :] = part.reshape(SLOTS, heads, HD).astype(jnp.bfloat16)
 
     return pl.pallas_call(
         body,
@@ -237,7 +236,6 @@
             pltpu.VMEM((pieces, D, QUARTER), jnp.bfloat16),
             pltpu.VMEM((pieces, D, QUARTER), jnp.bfloat16),
             pltpu.VMEM((pieces, QUARTER, D), jnp.bfloat16),
-            pltpu.VMEM((SLOTS * H, HD), jnp.float32),
             pltpu.VMEM((SLOTS, D), jnp.bfloat16),
             pltpu.VMEM((pieces, SLOTS, QUARTER), jnp.bfloat16),
             pltpu.SemaphoreType.DMA((3 * pieces,)),
@@ -333,8 +331,9 @@
     axes = ("rep", "exp")
     beside, across = pairings(lax.axis_size("rep"), lax.axis_size("exp"))
     own = (w_gate[0], w_up[0], w_down[0])
-    paired = tuple(lax.ppermute(part, axes, beside) for part in own)
-    weights = own + paired
+    paired_gate = lax.ppermute(own[0], axes, beside)
+    paired_gate, later = lax.optimization_barrier((paired_gate, own[1:]))
+    paired = (paired_gate,) + tuple(lax.ppermute(part, axes, beside) for part in later)
     gain = norm_gain.reshape(1, D)
     gates = gate_weights.astype(jnp.float32)
 
@@ -348,6 +347,7 @@
 
     def experts(send):
         rows = lax.all_to_all(send, "exp", split_axis=0, concat_axis=0, tiled=True)
+        rows, weights = lax.optimization_barrier((rows, own + paired))
         visiting = lax.ppermute(rows, axes, across)
         home_terms = expert_half(rows, weights)
         away_terms = lax.ppermute(expert_half(visiting, weights), axes, across)

time: 363 us -> 342 us (0.942)
  waiting for transfers between devices: 158 us -> 147 us
  Pallas kernels: 70.5 us -> 60 us
  starting transfers between devices: 27.5 us -> 31.7 us
    ppermute x3, waiting for transfers between devices: 47.3 us -> 15.6 us  [the longest x2 12.1 us: on_device(): lax.ppermute(part, axes, beside)]
    ppermute x2, waiting for transfers between devices: 21.4 us -> 41.3 us  [experts(): visiting = lax.ppermute(rows, axes, across)]
    pallas_call x4, Pallas kernels: 48.7 us -> 38.2 us  [expert_half(): pl.pallas_call(body, in_specs=[pl.BlockSpec(memory_space=pltpu.VMEM)] + [...]
  transfers between devices with their start and end apart: 9 -> 9, of which waited for: 7 -> 8; matrix products, arithmetic and copies ran while one was open for 0% -> 1% of each run, Pallas kernels for 8% -> 10%
where the time goes in v2:
time: 342 us; the launch traced here: 341 us
  waiting for transfers between devices  147 us (43%)
  blocking collectives  90.8 us (27%)
  Pallas kernels  60 us (18%)
  starting transfers between devices  31.7 us (9%)
  other arithmetic  5.48 us (2%)
  local copies, waits for them, and re-layouts  5.11 us (1%)
    all_to_all x1, blocking collectives, experts(): rows = lax.all_to_all(send, 'exp', split_axis=0, concat_axis=0, tiled=True)  45.5 us
    all_to_all x1, blocking collectives, experts(): return lax.all_to_all(terms, 'exp', split_axis=0, concat_axis=0, tiled=True)  45.4 us
    ppermute x2, waiting for transfers between devices, experts(): visiting = lax.ppermute(rows, axes, across)  41.3 us
    pallas_call x4, Pallas kernels, expert_half(): pl.pallas_call(body, in_specs=[pl.BlockSpec(memory_space=pltpu.VMEM)] + [...  38.2 us
    all_to_all x1, waiting for transfers between devices, experts(): rows = lax.all_to_all(send, 'exp', split_axis=0, concat_axis=0, tiled=True)  34.5 us
    all_to_all x1, waiting for transfers between devices, experts(): return lax.all_to_all(terms, 'exp', split_axis=0, concat_axis=0, tiled=True)  33.5 us
    ppermute x2, waiting for transfers between devices, experts(): away_terms = lax.ppermute(expert_half(visiting, weights), axes, across)  22.4 us
    all_to_all x1, starting transfers between devices, experts(): rows = lax.all_to_all(send, 'exp', split_axis=0, concat_axis=0, tiled=True)  12.3 us
  transfers between devices with their start and end apart: 9, of which 8 were waited for; matrix products, arithmetic and copies ran while one was open for 1% of the time, Pallas kernels for 10%

profile of v2, /device:TPU:24, one launch (start us, length us, event | category | flops | bytes accessed | tf_op | source)
XLA Modules:
  0.0 341.0 jit_solution(17880377091349899234)
XLA Ops:
  2.8 7.8 %first_attention.1 = (f32[16,4096]{1,0:T(8,128)}, bf16[192,32,128]{2,1,0:T(8,128)(2,1)}) custom-call(s32[1]{0:T(128)S(6)} %copy.20.lengths_ref, s32[2,1,8]{2,1,0:T(1,128)} %drift_ref.3, bf16[2,1,16,4096]{3,2,1,0:T(8,128)(2,1)} %q_ref.3, bf16[1,2048,512]{2,1,0:T(8,128)(2,1)} %k_ref.3, bf16[1,2048,512]{2,1,0:T(8,128)(2,1)} %v_ref.3, ...), custom_call_target="tpu_custom_call" | custom-call | tf_op jit(solution)/shard_map/first_attention/pallas_call | solution.py:145
  10.6 12.3 %all-to-all-start = ((bf16[192,32,128]{2,1,0:T(8,128)(2,1)}), bf16[192,32,128]{2,1,0:T(8,128)(2,1)}, u32[]{:S(2)}, u32[]{:S(2)}) async-start(bf16[192,32,128]{2,1,0:T(8,128)(2,1)} %get-tuple-element.27), calls=%async_computation | async-start | bytes 3145728 | tf_op jit(solution)/shard_map/all_to_all | solution.py:349
  22.9 3.5 %collective-permute-done.refs_4_ = bf16[4096,256]{1,0:T(8,128)(2,1)} collective-permute-done((bf16[4096,256]{1,0:T(8,128)(2,1)}, bf16[4096,256]{1,0:T(8,128)(2,1)}, u32[]{:S(2)}, u32[]{:S(2)}) %collective-permute-start) | collective-permute-done | bytes 2097184 | tf_op jit(solution)/shard_map/ppermute | solution.py:334
  28.4 34.5 %all-to-all-done.refs_0_ = bf16[192,32,128]{2,1,0:T(8,128)(2,1)} async-done(((bf16[192,32,128]{2,1,0:T(8,128)(2,1)}), bf16[192,32,128]{2,1,0:T(8,128)(2,1)}, u32[]{:S(2)}, u32[]{:S(2)}) %all-to-all-start) | async-done | bytes 1572896 | tf_op jit(solution)/shard_map/all_to_all | solution.py:349
  62.9 12.1 %collective-permute-done.2.refs_6_ = bf16[256,4096]{1,0:T(8,128)(2,1)} collective-permute-done((bf16[256,4096]{1,0:T(8,128)(2,1)}, bf16[256,4096]{1,0:T(8,128)(2,1)}, u32[]{:S(2)}, u32[]{:S(2)}) %collective-permute-start.2) | collective-permute-done | bytes 2097184 | tf_op jit(solution)/shard_map/ppermute | solution.py:336
  75.0 2.0 collective-permute-start.3
  76.9 19.9 %collective-permute-done.3.refs_0_ = bf16[192,32,128]{2,1,0:T(8,128)(2,1)S(1)} collective-permute-done((bf16[192,32,128]{2,1,0:T(8,128)(2,1)}, bf16[192,32,128]{2,1,0:T(8,128)(2,1)S(1)}, u32[]{:S(2)}, u32[]{:S(2)}) %collective-permute-start.3) | collective-permute-done | bytes 1572896 | tf_op jit(solution)/shard_map/ppermute | solution.py:351
  98.0 9.5 %expert_half.5 = bf16[192,32,128]{2,1,0:T(8,128)(2,1)} custom-call(bf16[192,32,128]{2,1,0:T(8,128)(2,1)} %copy-done.3, bf16[4096,256]{1,0:T(8,128)(2,1)} %bitcast.5, bf16[4096,256]{1,0:T(8,128)(2,1)} %bitcast.9, bf16[256,4096]{1,0:T(8,128)(2,1)} %bitcast.15, bf16[4096,256]{1,0:T(8,128)(2,1)} %collective-permute-done.refs_4_, ...), custom_call_target="tpu_custom_call" | custom-call | tf_op jit(solution)/shard_map/expert_half/pallas_call | solution.py:230
  107.6 2.2 collective-permute-start.4
  109.8 9.6 %expert_half.4 = bf16[192,32,128]{2,1,0:T(8,128)(2,1)} custom-call(bf16[192,32,128]{2,1,0:T(8,128)(2,1)} %all-to-all-done.refs_0_, bf16[4096,256]{1,0:T(8,128)(2,1)} %bitcast.6, bf16[4096,256]{1,0:T(8,128)(2,1)} %bitcast.10, bf16[256,4096]{1,0:T(8,128)(2,1)} %bitcast.16, bf16[4096,256]{1,0:T(8,128)(2,1)} %collective-permute-done.refs_4_, ...), custom_call_target="tpu_custom_call" | custom-call | tf_op jit(solution)/shard_map/expert_half/pallas_call | solution.py:230
  119.4 10.3 %collective-permute-done.4 = bf16[192,32,128]{2,1,0:T(8,128)(2,1)S(1)} collective-permute-done((bf16[192,32,128]{2,1,0:T(8,128)(2,1)}, bf16[192,32,128]{2,1,0:T(8,128)(2,1)S(1)}, u32[]{:S(2)}, u32[]{:S(2)}) %collective-permute-start.4) | collective-permute-done | bytes 1572896 | tf_op jit(solution)/shard_map/ppermute | solution.py:353
  129.7 3.1 add_convert_fusion.1
  132.7 11.9 %all-to-all-start.1 = ((bf16[192,32,128]{2,1,0:T(8,128)(2,1)}), bf16[192,32,128]{2,1,0:T(8,128)(2,1)S(1)}, u32[]{:S(2)}, u32[]{:S(2)}) async-start(bf16[192,32,128]{2,1,0:T(8,128)(2,1)} %add_convert_fusion.1), calls=%async_computation.1 | async-start | bytes 3145728 | tf_op jit(solution)/shard_map/all_to_all | solution.py:355
  144.7 6.0 %second_attention.1.attended_ref = f32[16,4096]{1,0:T(8,128)} custom-call(s32[1]{0:T(128)S(6)} %copy.20.lengths_ref, s32[2,1,8]{2,1,0:T(1,128)} %drift_ref.3, bf16[2,1,16,4096]{3,2,1,0:T(8,128)(2,1)} %q_ref.3, bf16[1,2048,512]{2,1,0:T(8,128)(2,1)} %k_ref.3, bf16[1,2048,512]{2,1,0:T(8,128)(2,1)} %v_ref.3, bf16[2,1,16,512]{3,2,1,0:T(8,128)(2,1)} %nk_ref.3, ...), custom_call_target="tpu_custom_call" | custom-call | tf_op jit(solution)/shard_map/second_attention/pallas_call | solution.py:179
  151.3 33.5 %all-to-all-done.1.terms_ref = bf16[192,32,128]{2,1,0:T(8,128)(2,1)S(1)} async-done(((bf16[192,32,128]{2,1,0:T(8,128)(2,1)}), bf16[192,32,128]{2,1,0:T(8,128)(2,1)S(1)}, u32[]{:S(2)}, u32[]{:S(2)}) %all-to-all-start.1) | async-done | bytes 1572896 | tf_op jit(solution)/shard_map/all_to_all | solution.py:355
  186.0 4.9 %combine_and_dispatch.1 = (bf16[16,4096]{1,0:T(8,128)(2,1)}, f32[16,4096]{1,0:T(8,128)}, bf16[192,32,128]{2,1,0:T(8,128)(2,1)}) custom-call(bf16[192,32,128]{2,1,0:T(8,128)(2,1)} %copy-done.1, f32[16,4096]{1,0:T(8,128)} %get-tuple-element.38.residual_ref, f32[16,4096]{1,0:T(8,128)} %second_attention.1.attended_ref, bf16[2,1,8,4096]{3,2,1,0:T(8,128)(2,1)} %drift_in_ref.3, ...), custom_call_target="tpu_custom_call" | custom-call | tf_op jit(solution)/shard_map/combine_and_dispatch/pallas_call | solution.py:262
  191.0 45.5 %all_to_all.20.refs_0_ = bf16[192,32,128]{2,1,0:T(8,128)(2,1)S(1)} all-to-all(bf16[192,32,128]{2,1,0:T(8,128)(2,1)} %get-tuple-element.39), channel_id=1, replica_groups=mesh['rep'=4,'exp'=64] {'exp'}, dimensions={0} | all-to-all | bytes 3145728 | tf_op jit(solution)/shard_map/all_to_all | solution.py:349
  236.7 21.4 %collective-permute-done.5.refs_0_ = bf16[192,32,128]{2,1,0:T(8,128)(2,1)S(1)} collective-permute-done((bf16[192,32,128]{2,1,0:T(8,128)(2,1)S(1)}, bf16[192,32,128]{2,1,0:T(8,128)(2,1)S(1)}, u32[]{:S(2)}, u32[]{:S(2)}) %collective-permute-start.5) | collective-permute-done | bytes 1572896 | tf_op jit(solution)/shard_map/ppermute | solution.py:351
  259.2 9.6 %expert_half.7 = bf16[192,32,128]{2,1,0:T(8,128)(2,1)} custom-call(bf16[192,32,128]{2,1,0:T(8,128)(2,1)} %copy-done.4, bf16[4096,256]{1,0:T(8,128)(2,1)} %bitcast.7, bf16[4096,256]{1,0:T(8,128)(2,1)} %bitcast.11, bf16[256,4096]{1,0:T(8,128)(2,1)} %bitcast.17, bf16[4096,256]{1,0:T(8,128)(2,1)} %collective-permute-done.refs_4_, ...), custom_call_target="tpu_custom_call" | custom-call | tf_op jit(solution)/shard_map/expert_half/pallas_call | solution.py:230
  269.1 9.5 %expert_half.6 = bf16[192,32,128]{2,1,0:T(8,128)(2,1)} custom-call(bf16[192,32,128]{2,1,0:T(8,128)(2,1)} %copy-done.2, bf16[4096,256]{1,0:T(8,128)(2,1)} %bitcast.8, bf16[4096,256]{1,0:T(8,128)(2,1)} %bitcast.12, bf16[256,4096]{1,0:T(8,128)(2,1)} %bitcast.18, bf16[4096,256]{1,0:T(8,128)(2,1)} %collective-permute-done.refs_4_, ...), custom_call_target="tpu_custom_call" | custom-call | tf_op jit(solution)/shard_map/expert_half/pallas_call | solution.py:230
  278.6 12.1 %collective-permute-done.6 = bf16[192,32,128]{2,1,0:T(8,128)(2,1)S(1)} collective-permute-done((bf16[192,32,128]{2,1,0:T(8,128)(2,1)}, bf16[192,32,128]{2,1,0:T(8,128)(2,1)S(1)}, u32[]{:S(2)}, u32[]{:S(2)}) %collective-permute-start.6) | collective-permute-done | bytes 1572896 | tf_op jit(solution)/shard_map/ppermute | solution.py:353
  290.7 1.8 add_convert_fusion
  292.5 45.4 %all_to_all.21.terms_ref = bf16[192,32,128]{2,1,0:T(8,128)(2,1)} all-to-all(bf16[192,32,128]{2,1,0:T(8,128)(2,1)S(1)} %add_convert_fusion), channel_id=1, replica_groups=mesh['rep'=4,'exp'=64] {'exp'}, dimensions={0} | all-to-all | bytes 3145728 | tf_op jit(solution)/shard_map/all_to_all | solution.py:355
  337.9 3.1 combine_last.1
  (21 shorter events, 9.0 us)
Async XLA Ops:
  0.0 26.4 %collective-permute-start = (bf16[4096,256]{1,0:T(8,128)(2,1)}, bf16[4096,256]{1,0:T(8,128)(2,1)}, u32[]{:S(2)}, u32[]{:S(2)}) collective-permute-start(bf16[4096,256]{1,0:T(8,128)(2,1)} %bitcast.4), channel_id=1, source_target_pairs={{0,64},{1,193},{2,66},{3,195},{4,68},{5,197},{6,70},{7,199},{8,72}... | collective-permute-start | bytes 6291464 | tf_op jit(solution)/shard_map/ppermute | solution.py:334
  10.6 15.8 %copy-start = (bf16[1,4096,256]{2,1,0:T(8,128)(2,1)S(1)}, bf16[1,4096,256]{2,1,0:T(8,128)(2,1)}, u32[]{:S(2)}) copy-start(bf16[1,4096,256]{2,1,0:T(8,128)(2,1)} %param.28) | copy-start | bytes 6291460
  10.6 52.3 %all-to-all-start = ((bf16[192,32,128]{2,1,0:T(8,128)(2,1)}), bf16[192,32,128]{2,1,0:T(8,128)(2,1)}, u32[]{:S(2)}, u32[]{:S(2)}) async-start(bf16[192,32,128]{2,1,0:T(8,128)(2,1)} %get-tuple-element.27), calls=%async_computation | async-start | bytes 3145728 | tf_op jit(solution)/shard_map/all_to_all | solution.py:349
  26.4 36.5 %collective-permute-start.1 = (bf16[4096,256]{1,0:T(8,128)(2,1)S(1)}, bf16[4096,256]{1,0:T(8,128)(2,1)}, u32[]{:S(2)}, u32[]{:S(2)}) collective-permute-start(bf16[4096,256]{1,0:T(8,128)(2,1)S(1)} %bitcast.13), channel_id=1, source_target_pairs={{0,64},{1,193},{2,66},{3,195},{4,68},{5,197},{6,70},{7,199},{8,72}... | collective-permute-start | bytes 6291464 | tf_op jit(solution)/shard_map/ppermute | solution.py:336
  27.1 47.9 %collective-permute-start.2 = (bf16[256,4096]{1,0:T(8,128)(2,1)}, bf16[256,4096]{1,0:T(8,128)(2,1)}, u32[]{:S(2)}, u32[]{:S(2)}) collective-permute-start(bf16[256,4096]{1,0:T(8,128)(2,1)} %bitcast.14), channel_id=1, source_target_pairs={{0,64},{1,193},{2,66},{3,195},{4,68},{5,197},{6,70},{7,199},{8,72}... | collective-permute-start | bytes 6291464 | tf_op jit(solution)/shard_map/ppermute | solution.py:336
  75.0 21.8 %collective-permute-start.3 = (bf16[192,32,128]{2,1,0:T(8,128)(2,1)}, bf16[192,32,128]{2,1,0:T(8,128)(2,1)S(1)}, u32[]{:S(2)}, u32[]{:S(2)}) collective-permute-start(bf16[192,32,128]{2,1,0:T(8,128)(2,1)} %all-to-all-done.refs_0_), channel_id=1, source_target_pairs={{0,192},{1,65},{2,194},{3,67},{4,196},{5,69},{6,198},{7,71},{8,200... | collective-permute-start | bytes 4718600 | tf_op jit(solution)/shard_map/ppermute | solution.py:351
  96.8 1.2 copy-start.3
  107.6 22.1 %collective-permute-start.4 = (bf16[192,32,128]{2,1,0:T(8,128)(2,1)}, bf16[192,32,128]{2,1,0:T(8,128)(2,1)S(1)}, u32[]{:S(2)}, u32[]{:S(2)}) collective-permute-start(bf16[192,32,128]{2,1,0:T(8,128)(2,1)} %expert_half.5), channel_id=1, source_target_pairs={{0,192},{1,65},{2,194},{3,67},{4,196},{5,69},{6,198},{7,71},{8,200... | collective-permute-start | bytes 4718600 | tf_op jit(solution)/shard_map/ppermute | solution.py:353
  132.7 52.1 %all-to-all-start.1 = ((bf16[192,32,128]{2,1,0:T(8,128)(2,1)}), bf16[192,32,128]{2,1,0:T(8,128)(2,1)S(1)}, u32[]{:S(2)}, u32[]{:S(2)}) async-start(bf16[192,32,128]{2,1,0:T(8,128)(2,1)} %add_convert_fusion.1), calls=%async_computation.1 | async-start | bytes 3145728 | tf_op jit(solution)/shard_map/all_to_all | solution.py:355
  144.7 6.0 %copy-start.5 = (bf16[2,1,16,8]{2,3,1,0:T(8,128)(2,1)S(1)}, bf16[2,1,16,8]{2,3,1,0:T(8,128)(2,1)}, u32[]{:S(2)}) copy-start(bf16[2,1,16,8]{2,3,1,0:T(8,128)(2,1)} %param.26) | copy-start | bytes 1540
  184.8 1.2 copy-start.1
  236.4 32.3 %copy-start.2 = (bf16[192,32,128]{2,1,0:T(8,128)(2,1)}, bf16[192,32,128]{2,1,0:T(8,128)(2,1)S(1)}, u32[]{:S(2)}) copy-start(bf16[192,32,128]{2,1,0:T(8,128)(2,1)S(1)} %all_to_all.20.refs_0_) | copy-start | bytes 4718596
  236.4 21.6 %collective-permute-start.5 = (bf16[192,32,128]{2,1,0:T(8,128)(2,1)S(1)}, bf16[192,32,128]{2,1,0:T(8,128)(2,1)S(1)}, u32[]{:S(2)}, u32[]{:S(2)}) collective-permute-start(bf16[192,32,128]{2,1,0:T(8,128)(2,1)S(1)} %all_to_all.20.refs_0_), channel_id=1, source_target_pairs={{0,192},{1,65},{2,194},{3,67},{4,196},{5,69},{6,198},{7,71},{8,200... | collective-permute-start | bytes 4718600 | tf_op jit(solution)/shard_map/ppermute | solution.py:351
  258.1 1.2 copy-start.4
  268.8 21.9 %collective-permute-start.6 = (bf16[192,32,128]{2,1,0:T(8,128)(2,1)}, bf16[192,32,128]{2,1,0:T(8,128)(2,1)S(1)}, u32[]{:S(2)}, u32[]{:S(2)}) collective-permute-start(bf16[192,32,128]{2,1,0:T(8,128)(2,1)} %expert_half.7), channel_id=1, source_target_pairs={{0,192},{1,65},{2,194},{3,67},{4,196},{5,69},{6,198},{7,71},{8,200... | collective-permute-start | bytes 4718600 | tf_op jit(solution)/shard_map/ppermute | solution.py:353

commit v3 on v2

--- a/solution.py
+++ b/solution.py
@@ -189,7 +189,7 @@
 
 
 def expert_half(rows, weights):
-    pieces = len(weights) // 3
+    pieces, count = len(weights) // 3, rows.shape[0]
 
     def body(*refs):
         rows_ref = refs[0]
@@ -206,7 +206,7 @@
                 )
         for copy in copies:
             copy.start()
-        for r in range(0, SLOTS, 16):
+        for r in range(0, count, 16):
             wide = rows_ref[r : r + 16].astype(jnp.float32).reshape(16, D)
             flat[r : r + 16, :] = wide.astype(jnp.bfloat16)
         for p in range(pieces):
@@ -219,30 +219,57 @@
             copies[3 * p + 2].wait()
         width = 512
         for n in range(D // width):
-            part = jnp.zeros((SLOTS, width), jnp.float32)
+            part = jnp.zeros((count, width), jnp.float32)
             for p in range(pieces):
                 part = part + jnp.dot(
                     hidden[p], down[p, :, n * width : (n + 1) * width], preferred_element_type=jnp.float32
                 )
             heads = width // HD
-            out_ref[:, n * heads : (n + 1) * heads, :] = part.reshape(SLOTS, heads, HD).astype(jnp.bfloat16)
+            out_ref[:, n * heads : (n + 1) * heads, :] = part.reshape(count, heads, HD).astype(jnp.bfloat16)
 
     return pl.pallas_call(
         body,
         in_specs=[pl.BlockSpec(memory_space=pltpu.VMEM)] + [pl.BlockSpec(memory_space=pl.ANY)] * (3 * pieces),
         out_specs=pl.BlockSpec(memory_space=pltpu.VMEM),
-        out_shape=jax.ShapeDtypeStruct((SLOTS, H, HD), jnp.bfloat16),
+        out_shape=jax.ShapeDtypeStruct((count, H, HD), jnp.bfloat16),
         scratch_shapes=[
             pltpu.VMEM((pieces, D, QUARTER), jnp.bfloat16),
             pltpu.VMEM((pieces, D, QUARTER), jnp.bfloat16),
             pltpu.VMEM((pieces, QUARTER, D), jnp.bfloat16),
-            pltpu.VMEM((SLOTS, D), jnp.bfloat16),
-            pltpu.VMEM((pieces, SLOTS, QUARTER), jnp.bfloat16),
+            pltpu.VMEM((count, D), jnp.bfloat16),
+            pltpu.VMEM((pieces, count, QUARTER), jnp.bfloat16),
             pltpu.SemaphoreType.DMA((3 * pieces,)),
         ],
         compiler_params=pltpu.CompilerParams(vmem_limit_bytes=VMEM_LIMIT),
         name="expert_half",
     )(rows, *weights)
+
+
+def add_halves(home, first, second):
+    steps = 2
+    size = SLOTS // (2 * steps)
+
+    def body(home_ref, first_ref, second_ref, out_ref):
+        def add(away_ref):
+            total = home_ref[...].astype(jnp.float32) + away_ref[...].astype(jnp.float32)
+            out_ref[...] = total.astype(jnp.bfloat16)
+
+        pl.when(pl.program_id(0) < steps)(lambda: add(first_ref))
+        pl.when(pl.program_id(0) >= steps)(lambda: add(second_ref))
+
+    block = (size, H, HD)
+    return pl.pallas_call(
+        body,
+        grid=(2 * steps,),
+        in_specs=[
+            pl.BlockSpec(block, lambda i: (i, 0, 0)),
+            pl.BlockSpec(block, lambda i: (jnp.minimum(i, steps - 1), 0, 0)),
+            pl.BlockSpec(block, lambda i: (jnp.maximum(i - steps, 0), 0, 0)),
+        ],
+        out_specs=pl.BlockSpec(block, lambda i: (i, 0, 0)),
+        out_shape=jax.ShapeDtypeStruct((SLOTS, H, HD), jnp.bfloat16),
+        name="add_halves",
+    )(home, first, second)
 
 
 def combine_and_dispatch(terms, residual, attended, drift_in, gain, ids, gates):
@@ -348,10 +375,11 @@
     def experts(send):
         rows = lax.all_to_all(send, "exp", split_axis=0, concat_axis=0, tiled=True)
         rows, weights = lax.optimization_barrier((rows, own + paired))
-        visiting = lax.ppermute(rows, axes, across)
+        halves = [slice(0, SLOTS // 2), slice(SLOTS // 2, SLOTS)]
+        visiting = [lax.ppermute(rows[half], axes, across) for half in halves]
+        away_terms = [lax.ppermute(expert_half(part, weights), axes, across) for part in visiting]
         home_terms = expert_half(rows, weights)
-        away_terms = lax.ppermute(expert_half(visiting, weights), axes, across)
-        terms = (home_terms.astype(jnp.float32) + away_terms.astype(jnp.float32)).astype(jnp.bfloat16)
+        terms = add_halves(home_terms, *away_terms)
         return lax.all_to_all(terms, "exp", split_axis=0, concat_axis=0, tiled=True)
 
     terms = experts(send)

time: 342 us -> 333 us (0.974)
  waiting for transfers between devices: 147 us -> 109 us
  Pallas kernels: 60 us -> 80.5 us
  starting transfers between devices: 31.7 us -> 38.9 us
  local copies, waits for them, and re-layouts: 5.11 us -> 10.9 us
  other arithmetic: 5.48 us -> 0.61 us
    ppermute x4 -> x8, waiting for transfers between devices: 63.6 us -> 25.9 us  [the longest x4 19.9 us: experts(): visiting = [lax.ppermute(rows[half], axes, across) for half in halves]]
    pallas_call x4 -> x6, Pallas kernels: 38.2 us -> 50.6 us  [expert_half(): pl.pallas_call(body, in_specs=[pl.BlockSpec(memory_space=pltpu.VMEM)] + [...]
    ppermute x4 -> x8, starting transfers between devices: 4.71 us -> 13.6 us  [the longest x4 7 us: experts(): lax.ppermute(expert_half(part, weights), axes, across)]
    pallas_call x0 -> x2, Pallas kernels: none -> 8.15 us  [add_halves(): pl.pallas_call(body, grid=(2 * steps,), in_specs=[pl.BlockSpec(block, lam...]
    convert_element_type x2 -> x0, other arithmetic: 4.87 us -> none  [experts(): (home_terms.astype(jnp.float32) + away_terms.astype(jnp.float32)).astype(...]
    unnamed x14 -> x26, local copies, waits for them, and re-layouts: 5.11 us -> 9.01 us
  transfers between devices with their start and end apart: 9 -> 13, of which waited for: 8 -> 8; matrix products, arithmetic and copies ran while one was open for 1% -> 1% of each run, Pallas kernels for 10% -> 19%
where the time goes in v3:
time: 333 us; the launch traced here: 332 us
  waiting for transfers between devices  109 us (33%)
  blocking collectives  91 us (27%)
  Pallas kernels  80.5 us (24%)
  starting transfers between devices  38.9 us (12%)
  local copies, waits for them, and re-layouts  10.9 us (3%)
    pallas_call x6, Pallas kernels, expert_half(): pl.pallas_call(body, in_specs=[pl.BlockSpec(memory_space=pltpu.VMEM)] + [...  50.6 us
    all_to_all x1, blocking collectives, experts(): return lax.all_to_all(terms, 'exp', split_axis=0, concat_axis=0, tiled=True)  45.6 us
    all_to_all x1, blocking collectives, experts(): rows = lax.all_to_all(send, 'exp', split_axis=0, concat_axis=0, tiled=True)  45.5 us
    all_to_all x1, waiting for transfers between devices, experts(): rows = lax.all_to_all(send, 'exp', split_axis=0, concat_axis=0, tiled=True)  34.5 us
    all_to_all x1, waiting for transfers between devices, experts(): return lax.all_to_all(terms, 'exp', split_axis=0, concat_axis=0, tiled=True)  33.5 us
    ppermute x4, waiting for transfers between devices, experts(): visiting = [lax.ppermute(rows[half], axes, across) for half in halves]  19.9 us
    all_to_all x1, starting transfers between devices, experts(): rows = lax.all_to_all(send, 'exp', split_axis=0, concat_axis=0, tiled=True)  12.3 us
    ppermute x2, waiting for transfers between devices, on_device(): lax.ppermute(part, axes, beside)  12.1 us
  transfers between devices with their start and end apart: 13, of which 8 were waited for; matrix products, arithmetic and copies ran while one was open for 1% of the time, Pallas kernels for 19%

profile of v3, /device:TPU:24, one launch (start us, length us, event | category | flops | bytes accessed | tf_op | source)
XLA Modules:
  0.0 332.2 jit_solution(10805763119629892112)
XLA Ops:
  2.8 7.8 %first_attention.1 = (f32[16,4096]{1,0:T(8,128)}, bf16[192,32,128]{2,1,0:T(8,128)(2,1)}) custom-call(s32[1]{0:T(128)S(6)} %copy.20.lengths_ref, s32[2,1,8]{2,1,0:T(1,128)} %drift_ref.3, bf16[2,1,16,4096]{3,2,1,0:T(8,128)(2,1)} %q_ref.3, bf16[1,2048,512]{2,1,0:T(8,128)(2,1)} %k_ref.3, bf16[1,2048,512]{2,1,0:T(8,128)(2,1)} %v_ref.3, ...), custom_call_target="tpu_custom_call" | custom-call | tf_op jit(solution)/shard_map/first_attention/pallas_call | solution.py:145
  10.5 12.3 %all-to-all-start = ((bf16[192,32,128]{2,1,0:T(8,128)(2,1)}), bf16[192,32,128]{2,1,0:T(8,128)(2,1)}, u32[]{:S(2)}, u32[]{:S(2)}) async-start(bf16[192,32,128]{2,1,0:T(8,128)(2,1)} %get-tuple-element.27), calls=%async_computation | async-start | bytes 3145728 | tf_op jit(solution)/shard_map/all_to_all | solution.py:376
  22.9 3.5 %collective-permute-done.refs_4_ = bf16[4096,256]{1,0:T(8,128)(2,1)} collective-permute-done((bf16[4096,256]{1,0:T(8,128)(2,1)}, bf16[4096,256]{1,0:T(8,128)(2,1)}, u32[]{:S(2)}, u32[]{:S(2)}) %collective-permute-start) | collective-permute-done | bytes 2097184 | tf_op jit(solution)/shard_map/ppermute | solution.py:361
  28.4 34.5 %all-to-all-done.refs_0_ = bf16[192,32,128]{2,1,0:T(8,128)(2,1)} async-done(((bf16[192,32,128]{2,1,0:T(8,128)(2,1)}), bf16[192,32,128]{2,1,0:T(8,128)(2,1)}, u32[]{:S(2)}, u32[]{:S(2)}) %all-to-all-start) | async-done | bytes 1572896 | tf_op jit(solution)/shard_map/all_to_all | solution.py:376
  62.9 12.1 %collective-permute-done.2.refs_6_ = bf16[256,4096]{1,0:T(8,128)(2,1)} collective-permute-done((bf16[256,4096]{1,0:T(8,128)(2,1)}, bf16[256,4096]{1,0:T(8,128)(2,1)}, u32[]{:S(2)}, u32[]{:S(2)}) %collective-permute-start.2) | collective-permute-done | bytes 2097184 | tf_op jit(solution)/shard_map/ppermute | solution.py:363
  79.9 10.0 %collective-permute-done.5.refs_0_ = bf16[96,32,128]{2,1,0:T(8,128)(2,1)S(1)} collective-permute-done((bf16[96,32,128]{2,1,0:T(8,128)(2,1)S(1)}, bf16[96,32,128]{2,1,0:T(8,128)(2,1)S(1)}, u32[]{:S(2)}, u32[]{:S(2)}) %collective-permute-start.5) | collective-permute-done | bytes 786464 | tf_op jit(solution)/shard_map/ppermute | solution.py:379
  90.8 7.8 %expert_half.8 = bf16[96,32,128]{2,1,0:T(8,128)(2,1)} custom-call(bf16[96,32,128]{2,1,0:T(8,128)(2,1)} %copy-done.9, bf16[4096,256]{1,0:T(8,128)(2,1)} %bitcast.5, bf16[4096,256]{1,0:T(8,128)(2,1)} %bitcast.11, bf16[256,4096]{1,0:T(8,128)(2,1)} %bitcast.19, bf16[4096,256]{1,0:T(8,128)(2,1)} %collective-permute-done.refs_4_, ...), custom_call_target="tpu_custom_call" | custom-call | tf_op jit(solution)/shard_map/expert_half/pallas_call | solution.py:230
  101.6 7.8 %expert_half.7 = bf16[96,32,128]{2,1,0:T(8,128)(2,1)} custom-call(bf16[96,32,128]{2,1,0:T(8,128)(2,1)} %copy-done.5, bf16[4096,256]{1,0:T(8,128)(2,1)} %bitcast.6, bf16[4096,256]{1,0:T(8,128)(2,1)} %bitcast.12, bf16[256,4096]{1,0:T(8,128)(2,1)} %bitcast.20, bf16[4096,256]{1,0:T(8,128)(2,1)} %collective-permute-done.refs_4_, ...), custom_call_target="tpu_custom_call" | custom-call | tf_op jit(solution)/shard_map/expert_half/pallas_call | solution.py:230
  111.0 9.6 %expert_half.6.home_ref = bf16[192,32,128]{2,1,0:T(8,128)(2,1)} custom-call(bf16[192,32,128]{2,1,0:T(8,128)(2,1)} %all-to-all-done.refs_0_, bf16[4096,256]{1,0:T(8,128)(2,1)} %bitcast.7, bf16[4096,256]{1,0:T(8,128)(2,1)} %bitcast.13, bf16[256,4096]{1,0:T(8,128)(2,1)} %bitcast.21, bf16[4096,256]{1,0:T(8,128)(2,1)} %collective-permute-done.refs_4_, ...), custom_call_target="tpu_custom_call" | custom-call | tf_op jit(solution)/shard_map/expert_half/pallas_call | solution.py:230
  124.1 4.1 %add_halves.2 = bf16[192,32,128]{2,1,0:T(8,128)(2,1)} custom-call(bf16[192,32,128]{2,1,0:T(8,128)(2,1)} %expert_half.6.home_ref, bf16[96,32,128]{2,1,0:T(8,128)(2,1)} %copy-done.8, bf16[96,32,128]{2,1,0:T(8,128)(2,1)} %copy-done.4), custom_call_target="tpu_custom_call" | custom-call | tf_op jit(solution)/shard_map/add_halves/pallas_call | solution.py:261
  128.1 10.3 %all-to-all-start.1 = ((bf16[192,32,128]{2,1,0:T(8,128)(2,1)}), bf16[192,32,128]{2,1,0:T(8,128)(2,1)S(1)}, u32[]{:S(2)}, u32[]{:S(2)}) async-start(bf16[192,32,128]{2,1,0:T(8,128)(2,1)} %add_halves.2), calls=%async_computation.1 | async-start | bytes 3145728 | tf_op jit(solution)/shard_map/all_to_all | solution.py:383
  138.5 6.0 %second_attention.1.attended_ref = f32[16,4096]{1,0:T(8,128)} custom-call(s32[1]{0:T(128)S(6)} %copy.20.lengths_ref, s32[2,1,8]{2,1,0:T(1,128)} %drift_ref.3, bf16[2,1,16,4096]{3,2,1,0:T(8,128)(2,1)} %q_ref.3, bf16[1,2048,512]{2,1,0:T(8,128)(2,1)} %k_ref.3, bf16[1,2048,512]{2,1,0:T(8,128)(2,1)} %v_ref.3, bf16[2,1,16,512]{3,2,1,0:T(8,128)(2,1)} %nk_ref.3, ...), custom_call_target="tpu_custom_call" | custom-call | tf_op jit(solution)/shard_map/second_attention/pallas_call | solution.py:179
  145.1 33.5 %all-to-all-done.1.terms_ref = bf16[192,32,128]{2,1,0:T(8,128)(2,1)S(1)} async-done(((bf16[192,32,128]{2,1,0:T(8,128)(2,1)}), bf16[192,32,128]{2,1,0:T(8,128)(2,1)S(1)}, u32[]{:S(2)}, u32[]{:S(2)}) %all-to-all-start.1) | async-done | bytes 1572896 | tf_op jit(solution)/shard_map/all_to_all | solution.py:383
  179.7 4.9 %combine_and_dispatch.1 = (bf16[16,4096]{1,0:T(8,128)(2,1)}, f32[16,4096]{1,0:T(8,128)}, bf16[192,32,128]{2,1,0:T(8,128)(2,1)}) custom-call(bf16[192,32,128]{2,1,0:T(8,128)(2,1)} %copy-done.2, f32[16,4096]{1,0:T(8,128)} %get-tuple-element.38.residual_ref, f32[16,4096]{1,0:T(8,128)} %second_attention.1.attended_ref, bf16[2,1,8,4096]{3,2,1,0:T(8,128)(2,1)} %drift_in_ref.3, ...), custom_call_target="tpu_custom_call" | custom-call | tf_op jit(solution)/shard_map/combine_and_dispatch/pallas_call | solution.py:289
  184.7 45.5 %all_to_all.20.refs_0_ = bf16[192,32,128]{2,1,0:T(8,128)(2,1)S(1)} all-to-all(bf16[192,32,128]{2,1,0:T(8,128)(2,1)} %get-tuple-element.39), channel_id=1, replica_groups=mesh['rep'=4,'exp'=64] {'exp'}, dimensions={0} | all-to-all | bytes 3145728 | tf_op jit(solution)/shard_map/all_to_all | solution.py:376
  234.5 10.0 %collective-permute-done.9.refs_0_ = bf16[96,32,128]{2,1,0:T(8,128)(2,1)S(1)} collective-permute-done((bf16[96,32,128]{2,1,0:T(8,128)(2,1)S(1)}, bf16[96,32,128]{2,1,0:T(8,128)(2,1)S(1)}, u32[]{:S(2)}, u32[]{:S(2)}) %collective-permute-start.9) | collective-permute-done | bytes 786464 | tf_op jit(solution)/shard_map/ppermute | solution.py:379
  245.4 7.8 %expert_half.11 = bf16[96,32,128]{2,1,0:T(8,128)(2,1)} custom-call(bf16[96,32,128]{2,1,0:T(8,128)(2,1)} %copy-done.10, bf16[4096,256]{1,0:T(8,128)(2,1)} %bitcast.8, bf16[4096,256]{1,0:T(8,128)(2,1)} %bitcast.14, bf16[256,4096]{1,0:T(8,128)(2,1)} %bitcast.22, bf16[4096,256]{1,0:T(8,128)(2,1)} %collective-permute-done.refs_4_, ...), custom_call_target="tpu_custom_call" | custom-call | tf_op jit(solution)/shard_map/expert_half/pallas_call | solution.py:230
  253.2 3.0 collective-permute-start.10
  257.2 7.8 %expert_half.10 = bf16[96,32,128]{2,1,0:T(8,128)(2,1)} custom-call(bf16[96,32,128]{2,1,0:T(8,128)(2,1)} %copy-done.6, bf16[4096,256]{1,0:T(8,128)(2,1)} %bitcast.9, bf16[4096,256]{1,0:T(8,128)(2,1)} %bitcast.15, bf16[256,4096]{1,0:T(8,128)(2,1)} %bitcast.23, bf16[4096,256]{1,0:T(8,128)(2,1)} %collective-permute-done.refs_4_, ...), custom_call_target="tpu_custom_call" | custom-call | tf_op jit(solution)/shard_map/expert_half/pallas_call | solution.py:230
  265.4 9.6 %expert_half.9.home_ref = bf16[192,32,128]{2,1,0:T(8,128)(2,1)} custom-call(bf16[192,32,128]{2,1,0:T(8,128)(2,1)} %copy-done.1, bf16[4096,256]{1,0:T(8,128)(2,1)} %bitcast.10, bf16[4096,256]{1,0:T(8,128)(2,1)} %bitcast.16, bf16[256,4096]{1,0:T(8,128)(2,1)} %bitcast.24, bf16[4096,256]{1,0:T(8,128)(2,1)} %collective-permute-done.refs_4_, ...), custom_call_target="tpu_custom_call" | custom-call | tf_op jit(solution)/shard_map/expert_half/pallas_call | solution.py:230
  275.1 3.4 %collective-permute-done.8.first_ref = bf16[96,32,128]{2,1,0:T(8,128)(2,1)S(1)} collective-permute-done((bf16[96,32,128]{2,1,0:T(8,128)(2,1)}, bf16[96,32,128]{2,1,0:T(8,128)(2,1)S(1)}, u32[]{:S(2)}, u32[]{:S(2)}) %collective-permute-start.8) | collective-permute-done | bytes 786464 | tf_op jit(solution)/shard_map/ppermute | solution.py:380
  279.4 4.1 %add_halves.3 = bf16[192,32,128]{2,1,0:T(8,128)(2,1)} custom-call(bf16[192,32,128]{2,1,0:T(8,128)(2,1)} %expert_half.9.home_ref, bf16[96,32,128]{2,1,0:T(8,128)(2,1)} %copy-done.7, bf16[96,32,128]{2,1,0:T(8,128)(2,1)} %copy-done.3), custom_call_target="tpu_custom_call" | custom-call | tf_op jit(solution)/shard_map/add_halves/pallas_call | solution.py:261
  283.5 45.6 %all_to_all.21.terms_ref = bf16[192,32,128]{2,1,0:T(8,128)(2,1)} all-to-all(bf16[192,32,128]{2,1,0:T(8,128)(2,1)} %add_halves.3), channel_id=1, replica_groups=mesh['rep'=4,'exp'=64] {'exp'}, dimensions={0} | all-to-all | bytes 3145728 | tf_op jit(solution)/shard_map/all_to_all | solution.py:383
  329.1 3.1 combine_last.1
  (45 shorter events, 27.4 us)
Async XLA Ops:
  0.0 26.4 %collective-permute-start = (bf16[4096,256]{1,0:T(8,128)(2,1)}, bf16[4096,256]{1,0:T(8,128)(2,1)}, u32[]{:S(2)}, u32[]{:S(2)}) collective-permute-start(bf16[4096,256]{1,0:T(8,128)(2,1)} %bitcast.4), channel_id=1, source_target_pairs={{0,64},{1,193},{2,66},{3,195},{4,68},{5,197},{6,70},{7,199},{8,72}... | collective-permute-start | bytes 6291464 | tf_op jit(solution)/shard_map/ppermute | solution.py:361
  10.5 15.8 %copy-start = (bf16[1,4096,256]{2,1,0:T(8,128)(2,1)S(1)}, bf16[1,4096,256]{2,1,0:T(8,128)(2,1)}, u32[]{:S(2)}) copy-start(bf16[1,4096,256]{2,1,0:T(8,128)(2,1)} %param.28) | copy-start | bytes 6291460
  10.5 52.3 %all-to-all-start = ((bf16[192,32,128]{2,1,0:T(8,128)(2,1)}), bf16[192,32,128]{2,1,0:T(8,128)(2,1)}, u32[]{:S(2)}, u32[]{:S(2)}) async-start(bf16[192,32,128]{2,1,0:T(8,128)(2,1)} %get-tuple-element.27), calls=%async_computation | async-start | bytes 3145728 | tf_op jit(solution)/shard_map/all_to_all | solution.py:376
  26.4 36.5 %collective-permute-start.1 = (bf16[4096,256]{1,0:T(8,128)(2,1)S(1)}, bf16[4096,256]{1,0:T(8,128)(2,1)}, u32[]{:S(2)}, u32[]{:S(2)}) collective-permute-start(bf16[4096,256]{1,0:T(8,128)(2,1)S(1)} %bitcast.17), channel_id=1, source_target_pairs={{0,64},{1,193},{2,66},{3,195},{4,68},{5,197},{6,70},{7,199},{8,72}... | collective-permute-start | bytes 6291464 | tf_op jit(solution)/shard_map/ppermute | solution.py:363
  27.1 47.9 %collective-permute-start.2 = (bf16[256,4096]{1,0:T(8,128)(2,1)}, bf16[256,4096]{1,0:T(8,128)(2,1)}, u32[]{:S(2)}, u32[]{:S(2)}) collective-permute-start(bf16[256,4096]{1,0:T(8,128)(2,1)} %bitcast.18), channel_id=1, source_target_pairs={{0,64},{1,193},{2,66},{3,195},{4,68},{5,197},{6,70},{7,199},{8,72}... | collective-permute-start | bytes 6291464 | tf_op jit(solution)/shard_map/ppermute | solution.py:363
  76.6 13.3 %collective-permute-start.5 = (bf16[96,32,128]{2,1,0:T(8,128)(2,1)S(1)}, bf16[96,32,128]{2,1,0:T(8,128)(2,1)S(1)}, u32[]{:S(2)}, u32[]{:S(2)}) collective-permute-start(bf16[96,32,128]{2,1,0:T(8,128)(2,1)S(1)} %get-tuple-element.51), channel_id=1, source_target_pairs={{0,192},{1,65},{2,194},{3,67},{4,196},{5,69},{6,198},{7,71},{8,200... | collective-permute-start | bytes 2359304 | tf_op jit(solution)/shard_map/ppermute | solution.py:379
  78.7 22.0 %collective-permute-start.3 = (bf16[96,32,128]{2,1,0:T(8,128)(2,1)S(1)}, bf16[96,32,128]{2,1,0:T(8,128)(2,1)S(1)}, u32[]{:S(2)}, u32[]{:S(2)}) collective-permute-start(bf16[96,32,128]{2,1,0:T(8,128)(2,1)S(1)} %get-tuple-element.52), channel_id=1, source_target_pairs={{0,192},{1,65},{2,194},{3,67},{4,196},{5,69},{6,198},{7,71},{8,200... | collective-permute-start | bytes 2359304 | tf_op jit(solution)/shard_map/ppermute | solution.py:379
  89.9 0.9 copy-start.9
  98.7 22.0 %collective-permute-start.6 = (bf16[96,32,128]{2,1,0:T(8,128)(2,1)}, bf16[96,32,128]{2,1,0:T(8,128)(2,1)S(1)}, u32[]{:S(2)}, u32[]{:S(2)}) collective-permute-start(bf16[96,32,128]{2,1,0:T(8,128)(2,1)} %expert_half.8), channel_id=1, source_target_pairs={{0,192},{1,65},{2,194},{3,67},{4,196},{5,69},{6,198},{7,71},{8,200... | collective-permute-start | bytes 2359304 | tf_op jit(solution)/shard_map/ppermute | solution.py:380
  100.7 0.9 copy-start.5
  109.5 13.7 %collective-permute-start.4 = (bf16[96,32,128]{2,1,0:T(8,128)(2,1)}, bf16[96,32,128]{2,1,0:T(8,128)(2,1)S(1)}, u32[]{:S(2)}, u32[]{:S(2)}) collective-permute-start(bf16[96,32,128]{2,1,0:T(8,128)(2,1)} %expert_half.7), channel_id=1, source_target_pairs={{0,192},{1,65},{2,194},{3,67},{4,196},{5,69},{6,198},{7,71},{8,200... | collective-permute-start | bytes 2359304 | tf_op jit(solution)/shard_map/ppermute | solution.py:380
  120.7 2.5 copy-start.4
  128.1 50.4 %all-to-all-start.1 = ((bf16[192,32,128]{2,1,0:T(8,128)(2,1)}), bf16[192,32,128]{2,1,0:T(8,128)(2,1)S(1)}, u32[]{:S(2)}, u32[]{:S(2)}) async-start(bf16[192,32,128]{2,1,0:T(8,128)(2,1)} %add_halves.2), calls=%async_computation.1 | async-start | bytes 3145728 | tf_op jit(solution)/shard_map/all_to_all | solution.py:383
  138.5 6.0 %copy-start.11 = (bf16[2,1,16,8]{2,3,1,0:T(8,128)(2,1)S(1)}, bf16[2,1,16,8]{2,3,1,0:T(8,128)(2,1)}, u32[]{:S(2)}) copy-start(bf16[2,1,16,8]{2,3,1,0:T(8,128)(2,1)} %param.26) | copy-start | bytes 1540
  178.6 1.1 copy-start.2
  230.1 1.1 copy-start.1
  231.3 13.2 %collective-permute-start.9 = (bf16[96,32,128]{2,1,0:T(8,128)(2,1)S(1)}, bf16[96,32,128]{2,1,0:T(8,128)(2,1)S(1)}, u32[]{:S(2)}, u32[]{:S(2)}) collective-permute-start(bf16[96,32,128]{2,1,0:T(8,128)(2,1)S(1)} %get-tuple-element.49), channel_id=1, source_target_pairs={{0,192},{1,65},{2,194},{3,67},{4,196},{5,69},{6,198},{7,71},{8,200... | collective-permute-start | bytes 2359304 | tf_op jit(solution)/shard_map/ppermute | solution.py:379
  234.2 22.0 %collective-permute-start.7 = (bf16[96,32,128]{2,1,0:T(8,128)(2,1)S(1)}, bf16[96,32,128]{2,1,0:T(8,128)(2,1)S(1)}, u32[]{:S(2)}, u32[]{:S(2)}) collective-permute-start(bf16[96,32,128]{2,1,0:T(8,128)(2,1)S(1)} %get-tuple-element.50), channel_id=1, source_target_pairs={{0,192},{1,65},{2,194},{3,67},{4,196},{5,69},{6,198},{7,71},{8,200... | collective-permute-start | bytes 2359304 | tf_op jit(solution)/shard_map/ppermute | solution.py:379
  244.5 0.9 copy-start.10
  253.2 21.8 %collective-permute-start.10 = (bf16[96,32,128]{2,1,0:T(8,128)(2,1)}, bf16[96,32,128]{2,1,0:T(8,128)(2,1)S(1)}, u32[]{:S(2)}, u32[]{:S(2)}) collective-permute-start(bf16[96,32,128]{2,1,0:T(8,128)(2,1)} %expert_half.11), channel_id=1, source_target_pairs={{0,192},{1,65},{2,194},{3,67},{4,196},{5,69},{6,198},{7,71},{8,200... | collective-permute-start | bytes 2359304 | tf_op jit(solution)/shard_map/ppermute | solution.py:380
  256.2 0.9 copy-start.6
  265.0 13.5 %collective-permute-start.8 = (bf16[96,32,128]{2,1,0:T(8,128)(2,1)}, bf16[96,32,128]{2,1,0:T(8,128)(2,1)S(1)}, u32[]{:S(2)}, u32[]{:S(2)}) collective-permute-start(bf16[96,32,128]{2,1,0:T(8,128)(2,1)} %expert_half.10), channel_id=1, source_target_pairs={{0,192},{1,65},{2,194},{3,67},{4,196},{5,69},{6,198},{7,71},{8,200... | collective-permute-start | bytes 2359304 | tf_op jit(solution)/shard_map/ppermute | solution.py:380
  275.1 3.5 %copy-start.3 = (bf16[96,32,128]{2,1,0:T(8,128)(2,1)}, bf16[96,32,128]{2,1,0:T(8,128)(2,1)S(1)}, u32[]{:S(2)}) copy-start(bf16[96,32,128]{2,1,0:T(8,128)(2,1)S(1)} %collective-permute-done.10.second_ref) | copy-start | bytes 2359300
  278.5 0.9 copy-start.7
  (1 other events, 0.9 us)

commit v4 on v2

--- a/solution.py
+++ b/solution.py
@@ -18,8 +18,9 @@
 SLOTS = EXPERTS * CAP
 CACHE = 2048
 QUARTER = 256
+VISITS = 2
 NEG = -1e30
-VMEM_LIMIT = 56 * 1024 * 1024
+VMEM_LIMIT = 24 * 1024 * 1024
 
 
 def smem_spec():
@@ -34,7 +35,7 @@
     def _(t):
         picked = []
         for j in range(TOP):
-            e = ids_ref[denoise, 0, t, j]
+            e = ids_ref[denoise, 0, j, t]
             c = counts[e]
             counts[e] = c + 1
             picked.append(e * CAP + jnp.minimum(c, CAP - 1))
@@ -64,7 +65,7 @@
     def visit(t, picked):
         total = jnp.zeros((H, HD), jnp.float32)
         for j, slot in enumerate(picked):
-            total = total + gates_ref[denoise, 0, t, j] * terms_ref[slot].astype(jnp.float32)
+            total = total + gates_ref[denoise, 0, j, t] * terms_ref[slot].astype(jnp.float32)
         spread[pl.ds(pl.multiple_of(t * H, H), H), :] = total
 
     each_slot(ids_ref, denoise, counts, visit)
@@ -167,7 +168,7 @@
             pltpu.VMEM((ROWS, H, HD), jnp.bfloat16),
             pltpu.SMEM((EXPERTS,), jnp.int32),
         ],
-        compiler_params=pltpu.CompilerParams(vmem_limit_bytes=VMEM_LIMIT),
+        compiler_params=pltpu.CompilerParams(vmem_limit_bytes=56 * 1024 * 1024),
         name="first_attention",
     )(lengths, drift_rows, queries, keys, values, new_keys, new_values, block_in, drift_in, gain, ids)
 
@@ -188,61 +189,91 @@
     )(lengths, drift_rows, queries, keys, values, new_keys, new_values)
 
 
-def expert_half(rows, weights):
-    pieces = len(weights) // 3
-
+def keep_in_vmem(weights):
     def body(*refs):
-        rows_ref = refs[0]
-        weight_refs = refs[1 : 1 + 3 * pieces]
-        out_ref = refs[1 + 3 * pieces]
-        gate, up, down, flat, hidden, sems = refs[2 + 3 * pieces :]
-        copies = []
-        for p in range(pieces):
-            for kind, target in enumerate((gate, up, down)):
-                copies.append(
-                    pltpu.make_async_copy(
-                        weight_refs[3 * p + kind], target.at[p], sems.at[3 * p + kind]
-                    )
-                )
+        sources, targets, sems = refs[: len(weights)], refs[len(weights) : -1], refs[-1]
+        copies = [
+            pltpu.make_async_copy(source, target, sems.at[i])
+            for i, (source, target) in enumerate(zip(sources, targets))
+        ]
         for copy in copies:
             copy.start()
-        for r in range(0, SLOTS, 16):
+        for copy in copies:
+            copy.wait()
+
+    return pl.pallas_call(
+        body,
+        in_specs=[pl.BlockSpec(memory_space=pl.ANY)] * len(weights),
+        out_specs=[pl.BlockSpec(memory_space=pltpu.VMEM)] * len(weights),
+        out_shape=[pltpu.VMEM(part.shape, part.dtype) for part in weights],
+        scratch_shapes=[pltpu.SemaphoreType.DMA((len(weights),))],
+        compiler_params=pltpu.CompilerParams(vmem_limit_bytes=VMEM_LIMIT),
+        name="keep_in_vmem",
+    )(*weights)
+
+
+def expert_half(rows, weights):
+    pieces, count = len(weights), rows.shape[0]
+
+    def body(*refs):
+        rows_ref, weight_refs = refs[0], refs[1 : 1 + 3 * pieces]
+        out_ref, flat, hidden = refs[1 + 3 * pieces :]
+        for r in range(0, count, 16):
             wide = rows_ref[r : r + 16].astype(jnp.float32).reshape(16, D)
             flat[r : r + 16, :] = wide.astype(jnp.bfloat16)
         for p in range(pieces):
-            copies[3 * p].wait()
-            gated = jnp.dot(flat[...], gate[p], preferred_element_type=jnp.float32)
-            copies[3 * p + 1].wait()
-            raised = jnp.dot(flat[...], up[p], preferred_element_type=jnp.float32)
+            gated = jnp.dot(flat[...], weight_refs[3 * p][...], preferred_element_type=jnp.float32)
+            raised = jnp.dot(flat[...], weight_refs[3 * p + 1][...], preferred_element_type=jnp.float32)
             hidden[p] = (jax.nn.silu(gated) * raised).astype(jnp.bfloat16)
-        for p in range(pieces):
-            copies[3 * p + 2].wait()
         width = 512
+        heads = width // HD
         for n in range(D // width):
-            part = jnp.zeros((SLOTS, width), jnp.float32)
+            part = jnp.zeros((count, width), jnp.float32)
             for p in range(pieces):
                 part = part + jnp.dot(
-                    hidden[p], down[p, :, n * width : (n + 1) * width], preferred_element_type=jnp.float32
+                    hidden[p],
+                    weight_refs[3 * p + 2][:, n * width : (n + 1) * width],
+                    preferred_element_type=jnp.float32,
                 )
-            heads = width // HD
-            out_ref[:, n * heads : (n + 1) * heads, :] = part.reshape(SLOTS, heads, HD).astype(jnp.bfloat16)
-
-    return pl.pallas_call(
-        body,
-        in_specs=[pl.BlockSpec(memory_space=pltpu.VMEM)] + [pl.BlockSpec(memory_space=pl.ANY)] * (3 * pieces),
-        out_specs=pl.BlockSpec(memory_space=pltpu.VMEM),
-        out_shape=jax.ShapeDtypeStruct((SLOTS, H, HD), jnp.bfloat16),
+            out_ref[:, n * heads : (n + 1) * heads, :] = part.reshape(count, heads, HD).astype(jnp.bfloat16)
+
+    vmem = pl.BlockSpec(memory_space=pltpu.VMEM)
+    return pl.pallas_call(
+        body,
+        in_specs=[vmem] * (1 + 3 * pieces),
+        out_specs=vmem,
+        out_shape=jax.ShapeDtypeStruct((count, H, HD), jnp.bfloat16),
         scratch_shapes=[
-            pltpu.VMEM((pieces, D, QUARTER), jnp.bfloat16),
-            pltpu.VMEM((pieces, D, QUARTER), jnp.bfloat16),
-            pltpu.VMEM((pieces, QUARTER, D), jnp.bfloat16),
-            pltpu.VMEM((SLOTS, D), jnp.bfloat16),
-            pltpu.VMEM((pieces, SLOTS, QUARTER), jnp.bfloat16),
-            pltpu.SemaphoreType.DMA((3 * pieces,)),
+            pltpu.VMEM((count, D), jnp.bfloat16),
+            pltpu.VMEM((pieces, count, QUARTER), jnp.bfloat16),
         ],
         compiler_params=pltpu.CompilerParams(vmem_limit_bytes=VMEM_LIMIT),
         name="expert_half",
-    )(rows, *weights)
+    )(rows, *[part for piece in weights for part in piece])
+
+
+def add_part(terms, away, part):
+    steps = 2
+    size = away.shape[0] // steps
+    block = (size, H, HD)
+
+    def body(terms_ref, away_ref, out_ref):
+        total = terms_ref[...].astype(jnp.float32) + away_ref[...].astype(jnp.float32)
+        out_ref[...] = total.astype(jnp.bfloat16)
+
+    return pl.pallas_call(
+        body,
+        grid=(steps,),
+        in_specs=[
+            pl.BlockSpec(block, lambda i: (part * steps + i, 0, 0)),
+            pl.BlockSpec(block, lambda i: (i, 0, 0)),
+        ],
+        out_specs=pl.BlockSpec(block, lambda i: (part * steps + i, 0, 0)),
+        out_shape=jax.ShapeDtypeStruct(terms.shape, terms.dtype),
+        input_output_aliases={0: 0},
+        compiler_params=pltpu.CompilerParams(vmem_limit_bytes=VMEM_LIMIT),
+        name="add_part",
+    )(terms, away)
 
 
 def combine_and_dispatch(terms, residual, attended, drift_in, gain, ids, gates):
@@ -335,7 +366,8 @@
     paired_gate, later = lax.optimization_barrier((paired_gate, own[1:]))
     paired = (paired_gate,) + tuple(lax.ppermute(part, axes, beside) for part in later)
     gain = norm_gain.reshape(1, D)
-    gates = gate_weights.astype(jnp.float32)
+    expert_ids = jnp.swapaxes(expert_ids, 2, 3)
+    gates = jnp.swapaxes(gate_weights, 2, 3).astype(jnp.float32)
 
     residual, send = first_attention(
         lengths, drift_rows, queries, cache_keys, cache_values, new_keys, new_values,
@@ -345,13 +377,17 @@
         lengths, drift_rows, queries, cache_keys, cache_values, new_keys, new_values
     )
 
+    weights = (keep_in_vmem(own), keep_in_vmem(paired))
+
     def experts(send):
         rows = lax.all_to_all(send, "exp", split_axis=0, concat_axis=0, tiled=True)
-        rows, weights = lax.optimization_barrier((rows, own + paired))
-        visiting = lax.ppermute(rows, axes, across)
-        home_terms = expert_half(rows, weights)
-        away_terms = lax.ppermute(expert_half(visiting, weights), axes, across)
-        terms = (home_terms.astype(jnp.float32) + away_terms.astype(jnp.float32)).astype(jnp.bfloat16)
+        rows, _ = lax.optimization_barrier((rows, paired))
+        size = SLOTS // VISITS
+        visiting = [lax.ppermute(rows[i * size : (i + 1) * size], axes, across) for i in range(VISITS)]
+        away_terms = [lax.ppermute(expert_half(part, weights), axes, across) for part in visiting]
+        terms = expert_half(rows, weights)
+        for i, away in enumerate(away_terms):
+            terms = add_part(terms, away, i)
         return lax.all_to_all(terms, "exp", split_axis=0, concat_axis=0, tiled=True)
 
     terms = experts(send)

time: 342 us -> 305 us (0.89)
  waiting for transfers between devices: 147 us -> 123 us
  Pallas kernels: 60 us -> 40.8 us
  starting transfers between devices: 31.7 us -> 38.8 us
  other arithmetic: 5.48 us -> 0.01 us
  local copies, waits for them, and re-layouts: 5.11 us -> 9.74 us
    ppermute x4 -> x8, waiting for transfers between devices: 63.6 us -> 39.2 us  [the longest x4 19.6 us: experts(): lax.ppermute(expert_half(part, weights), axes, across)]
    pallas_call x4 -> x12, Pallas kernels: 38.2 us -> 22.5 us  [the longest x6 16.7 us: expert_half(): pl.pallas_call(body, in_specs=[vmem] * (1 + 3 * pieces), out_specs=vmem,...]
    ppermute x4 -> x8, starting transfers between devices: 4.71 us -> 11.7 us  [the longest x4 6.65 us: experts(): lax.ppermute(rows[i * size:(i + 1) * size], axes, across)]
    convert_element_type x3 -> x1, other arithmetic: 5.48 us -> 0.01 us  [on_device(): gates = jnp.swapaxes(gate_weights, 2, 3).astype(jnp.float32)]
    unnamed x14 -> x54, local copies, waits for them, and re-layouts: 5.11 us -> 9.2 us
  transfers between devices with their start and end apart: 9 -> 13, of which waited for: 8 -> 12; matrix products, arithmetic and copies ran while one was open for 1% -> 0% of each run, Pallas kernels for 10% -> 11%
where the time goes in v4:
time: 305 us; the launch traced here: 304 us
  waiting for transfers between devices  123 us (40%)
  blocking collectives  90.8 us (30%)
  Pallas kernels  40.8 us (13%)
  starting transfers between devices  38.8 us (13%)
  local copies, waits for them, and re-layouts  9.74 us (3%)
    all_to_all x1, blocking collectives, experts(): rows = lax.all_to_all(send, 'exp', split_axis=0, concat_axis=0, tiled=True)  45.5 us
    all_to_all x1, blocking collectives, experts(): return lax.all_to_all(terms, 'exp', split_axis=0, concat_axis=0, tiled=True)  45.3 us
    all_to_all x1, waiting for transfers between devices, experts(): rows = lax.all_to_all(send, 'exp', split_axis=0, concat_axis=0, tiled=True)  32.8 us
    all_to_all x1, waiting for transfers between devices, experts(): return lax.all_to_all(terms, 'exp', split_axis=0, concat_axis=0, tiled=True)  32.1 us
    ppermute x4, waiting for transfers between devices, experts(): lax.ppermute(expert_half(part, weights), axes, across)  19.6 us
    ppermute x4, waiting for transfers between devices, experts(): lax.ppermute(rows[i * size:(i + 1) * size], axes, across)  19.5 us
    pallas_call x6, Pallas kernels, expert_half(): pl.pallas_call(body, in_specs=[vmem] * (1 + 3 * pieces), out_specs=vmem,...  16.7 us
    ppermute x2, waiting for transfers between devices, on_device(): lax.ppermute(part, axes, beside)  14 us
  transfers between devices with their start and end apart: 13, of which 12 were waited for; matrix products, arithmetic and copies ran while one was open for 0% of the time, Pallas kernels for 11%

profile of v4, /device:TPU:24, one launch (start us, length us, event | category | flops | bytes accessed | tf_op | source)
XLA Modules:
  0.0 304.5 jit_solution(9208531827385784574)
XLA Ops:
  1.4 7.7 %first_attention.1 = (f32[16,4096]{1,0:T(8,128)}, bf16[192,32,128]{2,1,0:T(8,128)(2,1)}) custom-call(s32[1]{0:T(128)S(6)} %copy.24.lengths_ref, s32[2,1,8]{2,1,0:T(1,128)} %drift_ref.3, bf16[2,1,16,4096]{3,2,1,0:T(8,128)(2,1)} %q_ref.3, bf16[1,2048,512]{2,1,0:T(8,128)(2,1)} %k_ref.3, bf16[1,2048,512]{2,1,0:T(8,128)(2,1)} %v_ref.3, ...), custom_call_target="tpu_custom_call" | custom-call | tf_op jit(solution)/shard_map/first_attention/pallas_call | solution.py:146
  9.1 11.9 %all-to-all-start = ((bf16[192,32,128]{2,1,0:T(8,128)(2,1)}), bf16[192,32,128]{2,1,0:T(8,128)(2,1)S(1)}, u32[]{:S(2)}, u32[]{:S(2)}) async-start(bf16[192,32,128]{2,1,0:T(8,128)(2,1)} %get-tuple-element.21), calls=%async_computation | async-start | bytes 3145728 | tf_op jit(solution)/shard_map/all_to_all | solution.py:383
  21.0 5.3 %collective-permute-done.refs_0_ = bf16[4096,256]{1,0:T(8,128)(2,1)} collective-permute-done((bf16[4096,256]{1,0:T(8,128)(2,1)}, bf16[4096,256]{1,0:T(8,128)(2,1)}, u32[]{:S(2)}, u32[]{:S(2)}) %collective-permute-start) | collective-permute-done | bytes 2097184 | tf_op jit(solution)/shard_map/ppermute | solution.py:365
  28.4 32.8 %all-to-all-done.refs_0_ = bf16[192,32,128]{2,1,0:T(8,128)(2,1)S(1)} async-done(((bf16[192,32,128]{2,1,0:T(8,128)(2,1)}), bf16[192,32,128]{2,1,0:T(8,128)(2,1)S(1)}, u32[]{:S(2)}, u32[]{:S(2)}) %all-to-all-start) | async-done | bytes 1572896 | tf_op jit(solution)/shard_map/all_to_all | solution.py:383
  61.2 14.0 %collective-permute-done.2.refs_2_ = bf16[256,4096]{1,0:T(8,128)(2,1)} collective-permute-done((bf16[256,4096]{1,0:T(8,128)(2,1)}, bf16[256,4096]{1,0:T(8,128)(2,1)}, u32[]{:S(2)}, u32[]{:S(2)}) %collective-permute-start.2) | collective-permute-done | bytes 2097184 | tf_op jit(solution)/shard_map/ppermute | solution.py:367
  82.4 4.4 %keep_in_vmem.3 = (bf16[4096,256]{1,0:T(8,128)(2,1)S(1)}, bf16[4096,256]{1,0:T(8,128)(2,1)S(1)}, bf16[256,4096]{1,0:T(8,128)(2,1)S(1)}) custom-call(bf16[4096,256]{1,0:T(8,128)(2,1)} %collective-permute-done.refs_0_, bf16[4096,256]{1,0:T(8,128)(2,1)} %collective-permute-done.1.refs_1_, bf16[256,4096]{1,0:T(8,128)(2,1)} %collective-permute-done.2.refs_2_), custom_call_target="tpu_custom_call" | custom-call | tf_op jit(solution)/shard_map/keep_in_vmem/pallas_call | solution.py:204
  93.3 3.9 %collective-permute-done.5.refs_0_ = bf16[96,32,128]{2,1,0:T(8,128)(2,1)S(1)} collective-permute-done((bf16[96,32,128]{2,1,0:T(8,128)(2,1)S(1)}, bf16[96,32,128]{2,1,0:T(8,128)(2,1)S(1)}, u32[]{:S(2)}, u32[]{:S(2)}) %collective-permute-start.5) | collective-permute-done | bytes 786464 | tf_op jit(solution)/shard_map/ppermute | solution.py:386
  97.2 2.5 expert_half.8
  101.9 3.4 %expert_half.6.terms_ref = bf16[192,32,128]{2,1,0:T(8,128)(2,1)S(1)} custom-call(bf16[192,32,128]{2,1,0:T(8,128)(2,1)S(1)} %copy-done.12, bf16[4096,256]{1,0:T(8,128)(2,1)S(1)} %get-tuple-element.26.refs_1_, bf16[4096,256]{1,0:T(8,128)(2,1)S(1)} %get-tuple-element.27.refs_2_, bf16[256,4096]{1,0:T(8,128)(2,1)S(1)} %get-tuple-element.28.refs_3_, ...), custom_call_target="tpu_custom_call" | custom-call | tf_op jit(solution)/shard_map/expert_half/pallas_call | solution.py:241
  105.8 8.2 %collective-permute-done.6.away_ref = bf16[96,32,128]{2,1,0:T(8,128)(2,1)S(1)} collective-permute-done((bf16[96,32,128]{2,1,0:T(8,128)(2,1)S(1)}, bf16[96,32,128]{2,1,0:T(8,128)(2,1)S(1)}, u32[]{:S(2)}, u32[]{:S(2)}) %collective-permute-start.6) | collective-permute-done | bytes 786464 | tf_op jit(solution)/shard_map/ppermute | solution.py:387
  115.5 12.3 %all-to-all-start.1 = ((bf16[192,32,128]{2,1,0:T(8,128)(2,1)}), bf16[192,32,128]{2,1,0:T(8,128)(2,1)}, u32[]{:S(2)}, u32[]{:S(2)}) async-start(bf16[192,32,128]{2,1,0:T(8,128)(2,1)} %copy-done.10), calls=%async_computation.1 | async-start | bytes 3145728 | tf_op jit(solution)/shard_map/all_to_all | solution.py:391
  131.0 4.6 %second_attention.1.attended_ref = f32[16,4096]{1,0:T(8,128)S(1)} custom-call(s32[1]{0:T(128)S(6)} %copy.24.lengths_ref, s32[2,1,8]{2,1,0:T(1,128)S(1)} %copy-done.25, bf16[2,1,16,4096]{3,2,1,0:T(8,128)(2,1)S(1)} %copy-done.18, bf16[1,2048,512]{2,1,0:T(8,128)(2,1)S(1)} %copy-done.13, bf16[1,2048,512]{2,1,0:T(8,128)(2,1)S(1)} %copy-done.14, ...), custom_call_target="tpu_custom_call" | custom-call | tf_op jit(solution)/shard_map/second_attention/pallas_call | solution.py:180
  135.7 32.1 %all-to-all-done.1.terms_ref = bf16[192,32,128]{2,1,0:T(8,128)(2,1)} async-done(((bf16[192,32,128]{2,1,0:T(8,128)(2,1)}), bf16[192,32,128]{2,1,0:T(8,128)(2,1)}, u32[]{:S(2)}, u32[]{:S(2)}) %all-to-all-start.1) | async-done | bytes 1572896 | tf_op jit(solution)/shard_map/all_to_all | solution.py:391
  167.8 3.6 %combine_and_dispatch.1 = (bf16[16,4096]{1,0:T(8,128)(2,1)S(1)}, f32[16,4096]{1,0:T(8,128)S(1)}, bf16[192,32,128]{2,1,0:T(8,128)(2,1)S(1)}) custom-call(bf16[192,32,128]{2,1,0:T(8,128)(2,1)} %all-to-all-done.1.terms_ref, f32[16,4096]{1,0:T(8,128)S(1)} %copy-done.20, f32[16,4096]{1,0:T(8,128)S(1)} %second_attention.1.attended_ref, ...), custom_call_target="tpu_custom_call" | custom-call | tf_op jit(solution)/shard_map/combine_and_dispatch/pallas_call | solution.py:293
  171.4 45.5 %all_to_all.20.refs_0_ = bf16[192,32,128]{2,1,0:T(8,128)(2,1)S(1)} all-to-all(bf16[192,32,128]{2,1,0:T(8,128)(2,1)S(1)} %get-tuple-element.33), channel_id=1, replica_groups=mesh['rep'=4,'exp'=64] {'exp'}, dimensions={0} | all-to-all | bytes 3145728 | tf_op jit(solution)/shard_map/all_to_all | solution.py:383
  217.5 3.0 collective-permute-start.9
  220.5 10.0 %collective-permute-done.7.refs_0_ = bf16[96,32,128]{2,1,0:T(8,128)(2,1)S(1)} collective-permute-done((bf16[96,32,128]{2,1,0:T(8,128)(2,1)S(1)}, bf16[96,32,128]{2,1,0:T(8,128)(2,1)S(1)}, u32[]{:S(2)}, u32[]{:S(2)}) %collective-permute-start.7) | collective-permute-done | bytes 786464 | tf_op jit(solution)/shard_map/ppermute | solution.py:386
  232.1 2.5 expert_half.10
  235.1 3.8 %collective-permute-done.9.refs_0_ = bf16[96,32,128]{2,1,0:T(8,128)(2,1)S(1)} collective-permute-done((bf16[96,32,128]{2,1,0:T(8,128)(2,1)S(1)}, bf16[96,32,128]{2,1,0:T(8,128)(2,1)S(1)}, u32[]{:S(2)}, u32[]{:S(2)}) %collective-permute-start.9) | collective-permute-done | bytes 786464 | tf_op jit(solution)/shard_map/ppermute | solution.py:386
  238.9 2.5 expert_half.11
  241.7 3.4 %expert_half.9.terms_ref = bf16[192,32,128]{2,1,0:T(8,128)(2,1)S(1)} custom-call(bf16[192,32,128]{2,1,0:T(8,128)(2,1)S(1)} %all_to_all.20.refs_0_, bf16[4096,256]{1,0:T(8,128)(2,1)S(1)} %get-tuple-element.26.refs_1_, bf16[4096,256]{1,0:T(8,128)(2,1)S(1)} %copy-done.1, bf16[256,4096]{1,0:T(8,128)(2,1)S(1)} %copy-done.3, bf16[4096,256]{1,0:T(8,128)(2,1)S(1)} %copy-done.5, ...), custom_call_target="tpu_custom_call" | custom-call | tf_op jit(solution)/shard_map/expert_half/pallas_call | solution.py:241
  245.1 3.0 collective-permute-done.8.away_ref
  248.3 8.2 %collective-permute-done.10.away_ref = bf16[96,32,128]{2,1,0:T(8,128)(2,1)S(1)} collective-permute-done((bf16[96,32,128]{2,1,0:T(8,128)(2,1)S(1)}, bf16[96,32,128]{2,1,0:T(8,128)(2,1)S(1)}, u32[]{:S(2)}, u32[]{:S(2)}) %collective-permute-start.10) | collective-permute-done | bytes 786464 | tf_op jit(solution)/shard_map/ppermute | solution.py:387
  256.8 45.3 %all_to_all.21.terms_ref = bf16[192,32,128]{2,1,0:T(8,128)(2,1)S(1)} all-to-all(bf16[192,32,128]{2,1,0:T(8,128)(2,1)S(1)} %add_part.7), channel_id=1, replica_groups=mesh['rep'=4,'exp'=64] {'exp'}, dimensions={0} | all-to-all | bytes 3145728 | tf_op jit(solution)/shard_map/all_to_all | solution.py:391
  (77 shorter events, 29.7 us)
Async XLA Ops:
  0.0 26.4 %collective-permute-start = (bf16[4096,256]{1,0:T(8,128)(2,1)}, bf16[4096,256]{1,0:T(8,128)(2,1)}, u32[]{:S(2)}, u32[]{:S(2)}) collective-permute-start(bf16[4096,256]{1,0:T(8,128)(2,1)} %bitcast.7), channel_id=1, source_target_pairs={{0,64},{1,193},{2,66},{3,195},{4,68},{5,197},{6,70},{7,199},{8,72}... | collective-permute-start | bytes 6291464 | tf_op jit(solution)/shard_map/ppermute | solution.py:365
  9.1 52.1 %all-to-all-start = ((bf16[192,32,128]{2,1,0:T(8,128)(2,1)}), bf16[192,32,128]{2,1,0:T(8,128)(2,1)S(1)}, u32[]{:S(2)}, u32[]{:S(2)}) async-start(bf16[192,32,128]{2,1,0:T(8,128)(2,1)} %get-tuple-element.21), calls=%async_computation | async-start | bytes 3145728 | tf_op jit(solution)/shard_map/all_to_all | solution.py:383
  26.4 34.8 %collective-permute-start.1 = (bf16[4096,256]{1,0:T(8,128)(2,1)}, bf16[4096,256]{1,0:T(8,128)(2,1)}, u32[]{:S(2)}, u32[]{:S(2)}) collective-permute-start(bf16[4096,256]{1,0:T(8,128)(2,1)} %bitcast.9), channel_id=1, source_target_pairs={{0,64},{1,193},{2,66},{3,195},{4,68},{5,197},{6,70},{7,199},{8,72}... | collective-permute-start | bytes 6291464 | tf_op jit(solution)/shard_map/ppermute | solution.py:367
  27.1 48.1 %collective-permute-start.2 = (bf16[256,4096]{1,0:T(8,128)(2,1)}, bf16[256,4096]{1,0:T(8,128)(2,1)}, u32[]{:S(2)}, u32[]{:S(2)}) collective-permute-start(bf16[256,4096]{1,0:T(8,128)(2,1)} %bitcast.11), channel_id=1, source_target_pairs={{0,64},{1,193},{2,66},{3,195},{4,68},{5,197},{6,70},{7,199},{8,72}... | collective-permute-start | bytes 6291464 | tf_op jit(solution)/shard_map/ppermute | solution.py:367
  61.2 16.3 %copy-start.11 = (bf16[192,32,128]{2,1,0:T(8,128)(2,1)}, bf16[192,32,128]{2,1,0:T(8,128)(2,1)S(1)}, u32[]{:S(2)}) copy-start(bf16[192,32,128]{2,1,0:T(8,128)(2,1)S(1)} %all-to-all-done.refs_0_) | copy-start | bytes 4718596
  61.2 17.6 %copy-start.15 = (bf16[1,4096,256]{2,1,0:T(8,128)(2,1)S(1)}, bf16[1,4096,256]{2,1,0:T(8,128)(2,1)}, u32[]{:S(2)}) copy-start(bf16[1,4096,256]{2,1,0:T(8,128)(2,1)} %param.27) | copy-start | bytes 6291460
  75.4 13.3 %collective-permute-start.3 = (bf16[96,32,128]{2,1,0:T(8,128)(2,1)S(1)}, bf16[96,32,128]{2,1,0:T(8,128)(2,1)S(1)}, u32[]{:S(2)}, u32[]{:S(2)}) collective-permute-start(bf16[96,32,128]{2,1,0:T(8,128)(2,1)S(1)} %get-tuple-element.40), channel_id=1, source_target_pairs={{0,192},{1,65},{2,194},{3,67},{4,196},{5,69},{6,198},{7,71},{8,200... | collective-permute-start | bytes 2359304 | tf_op jit(solution)/shard_map/ppermute | solution.py:386
  77.5 19.7 %collective-permute-start.5 = (bf16[96,32,128]{2,1,0:T(8,128)(2,1)S(1)}, bf16[96,32,128]{2,1,0:T(8,128)(2,1)S(1)}, u32[]{:S(2)}, u32[]{:S(2)}) collective-permute-start(bf16[96,32,128]{2,1,0:T(8,128)(2,1)S(1)} %get-tuple-element.39), channel_id=1, source_target_pairs={{0,192},{1,65},{2,194},{3,67},{4,196},{5,69},{6,198},{7,71},{8,200... | collective-permute-start | bytes 2359304 | tf_op jit(solution)/shard_map/ppermute | solution.py:386
  82.4 19.4 %copy-start = (bf16[4096,256]{1,0:T(8,128)(2,1)}, bf16[4096,256]{1,0:T(8,128)(2,1)S(1)}, u32[]{:S(2)}) copy-start(bf16[4096,256]{1,0:T(8,128)(2,1)S(1)} %get-tuple-element.27.refs_2_) | copy-start | bytes 6291460
  82.4 19.4 %copy-start.2 = (bf16[256,4096]{1,0:T(8,128)(2,1)}, bf16[256,4096]{1,0:T(8,128)(2,1)S(1)}, u32[]{:S(2)}) copy-start(bf16[256,4096]{1,0:T(8,128)(2,1)S(1)} %get-tuple-element.28.refs_3_) | copy-start | bytes 6291460
  91.2 14.4 %collective-permute-start.4 = (bf16[96,32,128]{2,1,0:T(8,128)(2,1)S(1)}, bf16[96,32,128]{2,1,0:T(8,128)(2,1)S(1)}, u32[]{:S(2)}, u32[]{:S(2)}) collective-permute-start(bf16[96,32,128]{2,1,0:T(8,128)(2,1)S(1)} %expert_half.7), channel_id=1, source_target_pairs={{0,192},{1,65},{2,194},{3,67},{4,196},{5,69},{6,198},{7,71},{8,200... | collective-permute-start | bytes 2359304 | tf_op jit(solution)/shard_map/ppermute | solution.py:387
  99.6 14.4 %collective-permute-start.6 = (bf16[96,32,128]{2,1,0:T(8,128)(2,1)S(1)}, bf16[96,32,128]{2,1,0:T(8,128)(2,1)S(1)}, u32[]{:S(2)}, u32[]{:S(2)}) collective-permute-start(bf16[96,32,128]{2,1,0:T(8,128)(2,1)S(1)} %expert_half.8), channel_id=1, source_target_pairs={{0,192},{1,65},{2,194},{3,67},{4,196},{5,69},{6,198},{7,71},{8,200... | collective-permute-start | bytes 2359304 | tf_op jit(solution)/shard_map/ppermute | solution.py:387
  115.5 52.3 %all-to-all-start.1 = ((bf16[192,32,128]{2,1,0:T(8,128)(2,1)}), bf16[192,32,128]{2,1,0:T(8,128)(2,1)}, u32[]{:S(2)}, u32[]{:S(2)}) async-start(bf16[192,32,128]{2,1,0:T(8,128)(2,1)} %copy-done.10), calls=%async_computation.1 | async-start | bytes 3145728 | tf_op jit(solution)/shard_map/all_to_all | solution.py:391
  131.0 36.8 %copy-start.19 = (bf16[2,1,8,4096]{3,2,1,0:T(8,128)(2,1)S(1)}, bf16[2,1,8,4096]{3,2,1,0:T(8,128)(2,1)}, u32[]{:S(2)}) copy-start(bf16[2,1,8,4096]{3,2,1,0:T(8,128)(2,1)} %drift_in_ref.3) | copy-start | bytes 393220
  131.0 36.8 %copy-start.20 = (f32[16,4096]{1,0:T(8,128)S(1)}, f32[16,4096]{1,0:T(8,128)}, u32[]{:S(2)}) copy-start(f32[16,4096]{1,0:T(8,128)} %get-tuple-element.32.residual_ref) | copy-start | bytes 786436
  131.0 36.8 %copy-start.23 = (s32[2,1,16,8]{2,3,1,0:T(8,128)S(1)}, s32[2,1,16,8]{2,3,1,0:T(8,128)}, u32[]{:S(2)}) copy-start(s32[2,1,16,8]{2,3,1,0:T(8,128)} %param.25) | copy-start | bytes 3076
  131.0 36.8 %copy-start.24 = (f32[4096]{0:T(1024)S(1)}, f32[4096]{0:T(1024)}, u32[]{:S(2)}) copy-start(f32[4096]{0:T(1024)} %param.24) | copy-start | bytes 49156
  167.8 62.7 %copy-start.7 = (bf16[4096,256]{1,0:T(8,128)(2,1)S(1)}, bf16[4096,256]{1,0:T(8,128)(2,1)}, u32[]{:S(2)}) copy-start(bf16[4096,256]{1,0:T(8,128)(2,1)} %copy-done.6) | copy-start | bytes 6291460
  171.4 59.1 %copy-start.3 = (bf16[256,4096]{1,0:T(8,128)(2,1)S(1)}, bf16[256,4096]{1,0:T(8,128)(2,1)}, u32[]{:S(2)}) copy-start(bf16[256,4096]{1,0:T(8,128)(2,1)} %copy-done.2) | copy-start | bytes 6291460
  171.4 59.1 %copy-start.5 = (bf16[4096,256]{1,0:T(8,128)(2,1)S(1)}, bf16[4096,256]{1,0:T(8,128)(2,1)}, u32[]{:S(2)}) copy-start(bf16[4096,256]{1,0:T(8,128)(2,1)} %copy-done.4) | copy-start | bytes 6291460
  217.2 13.3 %collective-permute-start.7 = (bf16[96,32,128]{2,1,0:T(8,128)(2,1)S(1)}, bf16[96,32,128]{2,1,0:T(8,128)(2,1)S(1)}, u32[]{:S(2)}, u32[]{:S(2)}) collective-permute-start(bf16[96,32,128]{2,1,0:T(8,128)(2,1)S(1)} %get-tuple-element.38), channel_id=1, source_target_pairs={{0,192},{1,65},{2,194},{3,67},{4,196},{5,69},{6,198},{7,71},{8,200... | collective-permute-start | bytes 2359304 | tf_op jit(solution)/shard_map/ppermute | solution.py:386
  217.5 21.4 %collective-permute-start.9 = (bf16[96,32,128]{2,1,0:T(8,128)(2,1)S(1)}, bf16[96,32,128]{2,1,0:T(8,128)(2,1)S(1)}, u32[]{:S(2)}, u32[]{:S(2)}) collective-permute-start(bf16[96,32,128]{2,1,0:T(8,128)(2,1)S(1)} %get-tuple-element.37), channel_id=1, source_target_pairs={{0,192},{1,65},{2,194},{3,67},{4,196},{5,69},{6,198},{7,71},{8,200... | collective-permute-start | bytes 2359304 | tf_op jit(solution)/shard_map/ppermute | solution.py:386
  234.6 13.5 %collective-permute-start.8 = (bf16[96,32,128]{2,1,0:T(8,128)(2,1)S(1)}, bf16[96,32,128]{2,1,0:T(8,128)(2,1)S(1)}, u32[]{:S(2)}, u32[]{:S(2)}) collective-permute-start(bf16[96,32,128]{2,1,0:T(8,128)(2,1)S(1)} %expert_half.10), channel_id=1, source_target_pairs={{0,192},{1,65},{2,194},{3,67},{4,196},{5,69},{6,198},{7,71},{8,200... | collective-permute-start | bytes 2359304 | tf_op jit(solution)/shard_map/ppermute | solution.py:387
  241.4 15.1 %collective-permute-start.10 = (bf16[96,32,128]{2,1,0:T(8,128)(2,1)S(1)}, bf16[96,32,128]{2,1,0:T(8,128)(2,1)S(1)}, u32[]{:S(2)}, u32[]{:S(2)}) collective-permute-start(bf16[96,32,128]{2,1,0:T(8,128)(2,1)S(1)} %expert_half.11), channel_id=1, source_target_pairs={{0,192},{1,65},{2,194},{3,67},{4,196},{5,69},{6,198},{7,71},{8,200... | collective-permute-start | bytes 2359304 | tf_op jit(solution)/shard_map/ppermute | solution.py:387
  (16 other events, 132.5 us)

commit v5 on v4

--- a/solution.py
+++ b/solution.py
@@ -190,8 +190,15 @@
 
 
 def keep_in_vmem(weights):
+    downs = weights[2:]
+    shapes = (weights[0].shape, weights[1].shape, (sum(part.shape[0] for part in downs), D))
+
     def body(*refs):
-        sources, targets, sems = refs[: len(weights)], refs[len(weights) : -1], refs[-1]
+        sources, (gate, up, down), sems = refs[: len(weights)], refs[len(weights) : -1], refs[-1]
+        targets, row = [gate, up], 0
+        for part in downs:
+            targets.append(down.at[row : row + part.shape[0]])
+            row += part.shape[0]
         copies = [
             pltpu.make_async_copy(source, target, sems.at[i])
             for i, (source, target) in enumerate(zip(sources, targets))
@@ -204,8 +211,8 @@
     return pl.pallas_call(
         body,
         in_specs=[pl.BlockSpec(memory_space=pl.ANY)] * len(weights),
-        out_specs=[pl.BlockSpec(memory_space=pltpu.VMEM)] * len(weights),
-        out_shape=[pltpu.VMEM(part.shape, part.dtype) for part in weights],
+        out_specs=[pl.BlockSpec(memory_space=pltpu.VMEM)] * 3,
+        out_shape=[pltpu.VMEM(shape, jnp.bfloat16) for shape in shapes],
         scratch_shapes=[pltpu.SemaphoreType.DMA((len(weights),))],
         compiler_params=pltpu.CompilerParams(vmem_limit_bytes=VMEM_LIMIT),
         name="keep_in_vmem",
@@ -362,9 +369,12 @@
     axes = ("rep", "exp")
     beside, across = pairings(lax.axis_size("rep"), lax.axis_size("exp"))
     own = (w_gate[0], w_up[0], w_down[0])
-    paired_gate = lax.ppermute(own[0], axes, beside)
-    paired_gate, later = lax.optimization_barrier((paired_gate, own[1:]))
-    paired = (paired_gate,) + tuple(lax.ppermute(part, axes, beside) for part in later)
+    gate_up = [lax.ppermute(part, axes, beside) for part in own[:2]]
+    downs = []
+    for i, half in enumerate(jnp.split(own[2], 2)):
+        gate_up[i], half = lax.optimization_barrier((gate_up[i], half))
+        downs.append(lax.ppermute(half, axes, beside))
+    paired = (*gate_up, *downs)
     gain = norm_gain.reshape(1, D)
     expert_ids = jnp.swapaxes(expert_ids, 2, 3)
     gates = jnp.swapaxes(gate_weights, 2, 3).astype(jnp.float32)
@@ -379,22 +389,22 @@
 
     weights = (keep_in_vmem(own), keep_in_vmem(paired))
 
-    def experts(send):
+    def experts(send, first):
         rows = lax.all_to_all(send, "exp", split_axis=0, concat_axis=0, tiled=True)
-        rows, _ = lax.optimization_barrier((rows, paired))
+        rows, first = lax.optimization_barrier((rows, first))
         size = SLOTS // VISITS
         visiting = [lax.ppermute(rows[i * size : (i + 1) * size], axes, across) for i in range(VISITS)]
         away_terms = [lax.ppermute(expert_half(part, weights), axes, across) for part in visiting]
         terms = expert_half(rows, weights)
         for i, away in enumerate(away_terms):
             terms = add_part(terms, away, i)
-        return lax.all_to_all(terms, "exp", split_axis=0, concat_axis=0, tiled=True)
-
-    terms = experts(send)
+        return lax.all_to_all(terms, "exp", split_axis=0, concat_axis=0, tiled=True), first
+
+    terms, (_, attended, gates) = experts(send, (paired, attended, gates))
     result, residual, send = combine_and_dispatch(
         terms, residual, attended, drift_in, gain, expert_ids, gates
     )
-    terms = experts(send)
+    terms, _ = experts(send, paired)
     return combine_last(terms, residual, result, expert_ids, gates)
 
 

time: 305 us -> 298 us (0.977)
  blocking collectives: 90.8 us -> 143 us
  waiting for transfers between devices: 123 us -> 81.1 us
  starting transfers between devices: 38.8 us -> 27.4 us
    all_to_all x1 -> x2, blocking collectives: 45.3 us -> 97.3 us  [experts(): lax.all_to_all(terms, 'exp', split_axis=0, concat_axis=0, tiled=True)]
    all_to_all x1 -> x0, waiting for transfers between devices: 32.1 us -> none  [experts(): return lax.all_to_all(terms, 'exp', split_axis=0, concat_axis=0, tiled=True)]
    all_to_all x1, waiting for transfers between devices: 32.8 us -> 8.42 us  [experts(): rows = lax.all_to_all(send, 'exp', split_axis=0, concat_axis=0, tiled=True)]
    all_to_all x1 -> x0, starting transfers between devices: 12.3 us -> none  [experts(): return lax.all_to_all(terms, 'exp', split_axis=0, concat_axis=0, tiled=True)]
    ppermute x3 -> x4, waiting for transfers between devices: 19.3 us -> 30.8 us  [the longest x2 22.2 us: on_device(): gate_up = [lax.ppermute(part, axes, beside) for part in own[:2]]]
    unnamed x54 -> x28, local copies, waits for them, and re-layouts: 9.2 us -> 3.25 us
    ppermute x4, waiting for transfers between devices: 19.5 us -> 23.1 us  [experts(): lax.ppermute(rows[i * size:(i + 1) * size], axes, across)]
    split x0 -> x1, local copies, waits for them, and re-layouts: none -> 3.3 us  [on_device(): jnp.split(own[2], 2)]
  transfers between devices with their start and end apart: 13 -> 13, of which waited for: 12 -> 12; matrix products, arithmetic and copies ran while one was open for 0% -> 1% of each run, Pallas kernels for 11% -> 11%
where the time goes in v5:
time: 298 us; the launch traced here: 297 us
  blocking collectives  143 us (48%)
  waiting for transfers between devices  81.1 us (27%)
  Pallas kernels  38.3 us (13%)
  starting transfers between devices  27.4 us (9%)
  local copies, waits for them, and re-layouts  7.09 us (2%)
    all_to_all x2, blocking collectives, experts(): lax.all_to_all(terms, 'exp', split_axis=0, concat_axis=0, tiled=True)  97.3 us
    all_to_all x1, blocking collectives, experts(): rows = lax.all_to_all(send, 'exp', split_axis=0, concat_axis=0, tiled=True)  45.3 us
    ppermute x4, waiting for transfers between devices, experts(): lax.ppermute(rows[i * size:(i + 1) * size], axes, across)  23.1 us
    ppermute x2, waiting for transfers between devices, on_device(): gate_up = [lax.ppermute(part, axes, beside) for part in own[:2]]  22.2 us
    ppermute x4, waiting for transfers between devices, experts(): lax.ppermute(expert_half(part, weights), axes, across)  18.8 us
    pallas_call x6, Pallas kernels, expert_half(): pl.pallas_call(body, in_specs=[vmem] * (1 + 3 * pieces), out_specs=vmem,...  16.7 us
    all_to_all x1, starting transfers between devices, experts(): rows = lax.all_to_all(send, 'exp', split_axis=0, concat_axis=0, tiled=True)  12.2 us
    ppermute x2, waiting for transfers between devices, on_device(): downs.append(lax.ppermute(half, axes, beside))  8.6 us
  transfers between devices with their start and end apart: 13, of which 12 were waited for; matrix products, arithmetic and copies ran while one was open for 1% of the time, Pallas kernels for 11%

profile of v5, /device:TPU:24, one launch (start us, length us, event | category | flops | bytes accessed | tf_op | source)
XLA Modules:
  0.0 297.3 jit_solution(13266002742267277680)
XLA Ops:
  2.7 7.7 %first_attention.1 = (f32[16,4096]{1,0:T(8,128)}, bf16[192,32,128]{2,1,0:T(8,128)(2,1)}) custom-call(s32[1]{0:T(128)S(6)} %copy.24.lengths_ref, s32[2,1,8]{2,1,0:T(1,128)} %drift_ref.3, bf16[2,1,16,4096]{3,2,1,0:T(8,128)(2,1)} %q_ref.3, bf16[1,2048,512]{2,1,0:T(8,128)(2,1)} %k_ref.3, bf16[1,2048,512]{2,1,0:T(8,128)(2,1)} %v_ref.3, ...), custom_call_target="tpu_custom_call" | custom-call | tf_op jit(solution)/shard_map/first_attention/pallas_call | solution.py:146
  10.4 12.2 %all-to-all-start = ((bf16[192,32,128]{2,1,0:T(8,128)(2,1)}), bf16[192,32,128]{2,1,0:T(8,128)(2,1)S(1)}, u32[]{:S(2)}, u32[]{:S(2)}) async-start(bf16[192,32,128]{2,1,0:T(8,128)(2,1)} %get-tuple-element.24), calls=%async_computation | async-start | bytes 3145728 | tf_op jit(solution)/shard_map/all_to_all | solution.py:393
  22.6 3.3 %slice_bitcast_fusion = (bf16[128,4096]{1,0:T(8,128)(2,1)}, bf16[128,4096]{1,0:T(8,128)(2,1)}) fusion(bf16[1,256,4096]{2,1,0:T(8,128)(2,1)} %param.29), kind=kLoop, calls=%fused_computation | loop fusion | bytes 4194304 | tf_op jit(solution)/shard_map/split | solution.py:374
  27.1 21.7 %collective-permute-done.1.refs_1_ = bf16[4096,256]{1,0:T(8,128)(2,1)} collective-permute-done((bf16[4096,256]{1,0:T(8,128)(2,1)}, bf16[4096,256]{1,0:T(8,128)(2,1)}, u32[]{:S(2)}, u32[]{:S(2)}) %collective-permute-start.1) | collective-permute-done | bytes 2097184 | tf_op jit(solution)/shard_map/ppermute | solution.py:372
  49.6 4.6 %second_attention.1.attended_ref = f32[16,4096]{1,0:T(8,128)S(1)} custom-call(s32[1]{0:T(128)S(6)} %copy.24.lengths_ref, s32[2,1,8]{2,1,0:T(1,128)S(1)} %copy-done.12, bf16[2,1,16,4096]{3,2,1,0:T(8,128)(2,1)S(1)} %copy-done.5, bf16[1,2048,512]{2,1,0:T(8,128)(2,1)S(1)} %copy-done.1, bf16[1,2048,512]{2,1,0:T(8,128)(2,1)S(1)} %copy-done.2, ...), custom_call_target="tpu_custom_call" | custom-call | tf_op jit(solution)/shard_map/second_attention/pallas_call | solution.py:180
  54.3 8.4 %all-to-all-done.refs_0_ = bf16[192,32,128]{2,1,0:T(8,128)(2,1)S(1)} async-done(((bf16[192,32,128]{2,1,0:T(8,128)(2,1)}), bf16[192,32,128]{2,1,0:T(8,128)(2,1)S(1)}, u32[]{:S(2)}, u32[]{:S(2)}) %all-to-all-start) | async-done | bytes 1572896 | tf_op jit(solution)/shard_map/all_to_all | solution.py:393
  62.7 8.6 %collective-permute-done.3.refs_3_ = bf16[128,4096]{1,0:T(8,128)(2,1)} collective-permute-done((bf16[128,4096]{1,0:T(8,128)(2,1)}, bf16[128,4096]{1,0:T(8,128)(2,1)}, u32[]{:S(2)}, u32[]{:S(2)}) %collective-permute-start.3) | collective-permute-done | bytes 1048608 | tf_op jit(solution)/shard_map/ppermute | solution.py:376
  78.5 2.5 keep_in_vmem.3
  81.1 3.8 %collective-permute-done.4.refs_0_ = bf16[96,32,128]{2,1,0:T(8,128)(2,1)S(1)} collective-permute-done((bf16[96,32,128]{2,1,0:T(8,128)(2,1)S(1)}, bf16[96,32,128]{2,1,0:T(8,128)(2,1)S(1)}, u32[]{:S(2)}, u32[]{:S(2)}) %collective-permute-start.4) | collective-permute-done | bytes 786464 | tf_op jit(solution)/shard_map/ppermute | solution.py:396
  84.9 2.5 expert_half.7
  89.4 3.9 %collective-permute-done.6.refs_0_ = bf16[96,32,128]{2,1,0:T(8,128)(2,1)S(1)} collective-permute-done((bf16[96,32,128]{2,1,0:T(8,128)(2,1)S(1)}, bf16[96,32,128]{2,1,0:T(8,128)(2,1)S(1)}, u32[]{:S(2)}, u32[]{:S(2)}) %collective-permute-start.6) | collective-permute-done | bytes 786464 | tf_op jit(solution)/shard_map/ppermute | solution.py:396
  98.0 3.5 %expert_half.6.terms_ref = bf16[192,32,128]{2,1,0:T(8,128)(2,1)S(1)} custom-call(bf16[192,32,128]{2,1,0:T(8,128)(2,1)S(1)} %all-to-all-done.refs_0_, bf16[4096,256]{1,0:T(8,128)(2,1)S(1)} %get-tuple-element.30.refs_1_, bf16[4096,256]{1,0:T(8,128)(2,1)S(1)} %get-tuple-element.31.refs_2_, bf16[256,4096]{1,0:T(8,128)(2,1)S(1)} %get-tuple-element.32.refs_3_, ...), custom_call_target="tpu_custom_call" | custom-call | tf_op jit(solution)/shard_map/expert_half/pallas_call | solution.py:248
  102.0 8.2 %collective-permute-done.7.away_ref = bf16[96,32,128]{2,1,0:T(8,128)(2,1)S(1)} collective-permute-done((bf16[96,32,128]{2,1,0:T(8,128)(2,1)S(1)}, bf16[96,32,128]{2,1,0:T(8,128)(2,1)S(1)}, u32[]{:S(2)}, u32[]{:S(2)}) %collective-permute-start.7) | collective-permute-done | bytes 786464 | tf_op jit(solution)/shard_map/ppermute | solution.py:397
  110.4 52.0 %all_to_all.20.terms_ref = bf16[192,32,128]{2,1,0:T(8,128)(2,1)S(1)} all-to-all(bf16[192,32,128]{2,1,0:T(8,128)(2,1)S(1)} %add_part.5), channel_id=1, replica_groups=mesh['rep'=4,'exp'=64] {'exp'}, dimensions={0} | all-to-all | bytes 3145728 | tf_op jit(solution)/shard_map/all_to_all | solution.py:401
  162.4 2.8 combine_and_dispatch.1
  165.3 45.3 %all_to_all.21.refs_0_ = bf16[192,32,128]{2,1,0:T(8,128)(2,1)S(1)} all-to-all(bf16[192,32,128]{2,1,0:T(8,128)(2,1)S(1)} %get-tuple-element.39), channel_id=1, replica_groups=mesh['rep'=4,'exp'=64] {'exp'}, dimensions={0} | all-to-all | bytes 3145728 | tf_op jit(solution)/shard_map/all_to_all | solution.py:393
  211.1 3.0 %collective-permute-start.10 = (bf16[96,32,128]{2,1,0:T(8,128)(2,1)S(1)}, bf16[96,32,128]{2,1,0:T(8,128)(2,1)S(1)}, u32[]{:S(2)}, u32[]{:S(2)}) collective-permute-start(bf16[96,32,128]{2,1,0:T(8,128)(2,1)S(1)} %get-tuple-element.45), channel_id=1, source_target_pairs={{0,192},{1,65},{2,194},{3,67},{4,196},{5,69},{6,198},{7,71},{8,200... | collective-permute-start | bytes 2359304 | tf_op jit(solution)/shard_map/ppermute | solution.py:396
  214.1 10.0 %collective-permute-done.8.refs_0_ = bf16[96,32,128]{2,1,0:T(8,128)(2,1)S(1)} collective-permute-done((bf16[96,32,128]{2,1,0:T(8,128)(2,1)S(1)}, bf16[96,32,128]{2,1,0:T(8,128)(2,1)S(1)}, u32[]{:S(2)}, u32[]{:S(2)}) %collective-permute-start.8) | collective-permute-done | bytes 786464 | tf_op jit(solution)/shard_map/ppermute | solution.py:396
  224.1 2.5 expert_half.10
  227.1 5.4 %collective-permute-done.10.refs_0_ = bf16[96,32,128]{2,1,0:T(8,128)(2,1)S(1)} collective-permute-done((bf16[96,32,128]{2,1,0:T(8,128)(2,1)S(1)}, bf16[96,32,128]{2,1,0:T(8,128)(2,1)S(1)}, u32[]{:S(2)}, u32[]{:S(2)}) %collective-permute-start.10) | collective-permute-done | bytes 786464 | tf_op jit(solution)/shard_map/ppermute | solution.py:396
  232.5 2.5 expert_half.11
  235.3 3.4 %expert_half.9.terms_ref = bf16[192,32,128]{2,1,0:T(8,128)(2,1)S(1)} custom-call(bf16[192,32,128]{2,1,0:T(8,128)(2,1)S(1)} %all_to_all.21.refs_0_, bf16[4096,256]{1,0:T(8,128)(2,1)S(1)} %get-tuple-element.30.refs_1_, bf16[4096,256]{1,0:T(8,128)(2,1)S(1)} %get-tuple-element.31.refs_2_, bf16[256,4096]{1,0:T(8,128)(2,1)S(1)} %get-tuple-element.32.refs_3_, ...), custom_call_target="tpu_custom_call" | custom-call | tf_op jit(solution)/shard_map/expert_half/pallas_call | solution.py:248
  241.2 8.2 %collective-permute-done.11.away_ref = bf16[96,32,128]{2,1,0:T(8,128)(2,1)S(1)} collective-permute-done((bf16[96,32,128]{2,1,0:T(8,128)(2,1)S(1)}, bf16[96,32,128]{2,1,0:T(8,128)(2,1)S(1)}, u32[]{:S(2)}, u32[]{:S(2)}) %collective-permute-start.11) | collective-permute-done | bytes 786464 | tf_op jit(solution)/shard_map/ppermute | solution.py:397
  249.6 45.3 %all_to_all.22.terms_ref = bf16[192,32,128]{2,1,0:T(8,128)(2,1)S(1)} all-to-all(bf16[192,32,128]{2,1,0:T(8,128)(2,1)S(1)} %add_part.7), channel_id=1, replica_groups=mesh['rep'=4,'exp'=64] {'exp'}, dimensions={0} | all-to-all | bytes 3145728 | tf_op jit(solution)/shard_map/all_to_all | solution.py:401
  (53 shorter events, 25.3 us)
Async XLA Ops:
  0.0 26.4 %collective-permute-start = (bf16[4096,256]{1,0:T(8,128)(2,1)}, bf16[4096,256]{1,0:T(8,128)(2,1)}, u32[]{:S(2)}, u32[]{:S(2)}) collective-permute-start(bf16[4096,256]{1,0:T(8,128)(2,1)} %bitcast.12), channel_id=1, source_target_pairs={{0,64},{1,193},{2,66},{3,195},{4,68},{5,197},{6,70},{7,199},{8,72}... | collective-permute-start | bytes 6291464 | tf_op jit(solution)/shard_map/ppermute | solution.py:372
  0.7 48.1 %collective-permute-start.1 = (bf16[4096,256]{1,0:T(8,128)(2,1)}, bf16[4096,256]{1,0:T(8,128)(2,1)}, u32[]{:S(2)}, u32[]{:S(2)}) collective-permute-start(bf16[4096,256]{1,0:T(8,128)(2,1)} %bitcast.14), channel_id=1, source_target_pairs={{0,64},{1,193},{2,66},{3,195},{4,68},{5,197},{6,70},{7,199},{8,72}... | collective-permute-start | bytes 6291464 | tf_op jit(solution)/shard_map/ppermute | solution.py:372
  10.4 39.2 %copy-start.5 = (bf16[2,1,16,4096]{3,2,1,0:T(8,128)(2,1)S(1)}, bf16[2,1,16,4096]{3,2,1,0:T(8,128)(2,1)}, u32[]{:S(2)}) copy-start(bf16[2,1,16,4096]{3,2,1,0:T(8,128)(2,1)} %q_ref.3) | copy-start | bytes 786436
  10.4 39.2 %copy-start.8 = (bf16[2,1,16,512]{3,2,1,0:T(8,128)(2,1)S(1)}, bf16[2,1,16,512]{3,2,1,0:T(8,128)(2,1)}, u32[]{:S(2)}) copy-start(bf16[2,1,16,512]{3,2,1,0:T(8,128)(2,1)} %nk_ref.3) | copy-start | bytes 98308
  10.4 39.2 %copy-start.9 = (bf16[2,1,16,512]{3,2,1,0:T(8,128)(2,1)S(1)}, bf16[2,1,16,512]{3,2,1,0:T(8,128)(2,1)}, u32[]{:S(2)}) copy-start(bf16[2,1,16,512]{3,2,1,0:T(8,128)(2,1)} %nv_ref.3) | copy-start | bytes 98308
  10.4 52.3 %all-to-all-start = ((bf16[192,32,128]{2,1,0:T(8,128)(2,1)}), bf16[192,32,128]{2,1,0:T(8,128)(2,1)S(1)}, u32[]{:S(2)}, u32[]{:S(2)}) async-start(bf16[192,32,128]{2,1,0:T(8,128)(2,1)} %get-tuple-element.24), calls=%async_computation | async-start | bytes 3145728 | tf_op jit(solution)/shard_map/all_to_all | solution.py:393
  22.6 27.0 %copy-start.1 = (bf16[1,2048,512]{2,1,0:T(8,128)(2,1)S(1)}, bf16[1,2048,512]{2,1,0:T(8,128)(2,1)}, u32[]{:S(2)}) copy-start(bf16[1,2048,512]{2,1,0:T(8,128)(2,1)} %k_ref.3) | copy-start | bytes 6291460
  22.6 27.0 %copy-start.2 = (bf16[1,2048,512]{2,1,0:T(8,128)(2,1)S(1)}, bf16[1,2048,512]{2,1,0:T(8,128)(2,1)}, u32[]{:S(2)}) copy-start(bf16[1,2048,512]{2,1,0:T(8,128)(2,1)} %v_ref.3) | copy-start | bytes 6291460
  22.6 27.0 %copy-start.12 = (s32[2,1,8]{2,1,0:T(1,128)S(1)}, s32[2,1,8]{2,1,0:T(1,128)}, u32[]{:S(2)}) copy-start(s32[2,1,8]{2,1,0:T(1,128)} %drift_ref.3) | copy-start | bytes 196
  26.4 36.3 %collective-permute-start.2 = (bf16[128,4096]{1,0:T(8,128)(2,1)}, bf16[128,4096]{1,0:T(8,128)(2,1)S(1)}, u32[]{:S(2)}, u32[]{:S(2)}) collective-permute-start(bf16[128,4096]{1,0:T(8,128)(2,1)} %get-tuple-element.27), channel_id=1, source_target_pairs={{0,64},{1,193},{2,66},{3,195},{4,68},{5,197},{6,70},{7,199},{8,72}... | collective-permute-start | bytes 3145736 | tf_op jit(solution)/shard_map/ppermute | solution.py:376
  48.8 22.5 %collective-permute-start.3 = (bf16[128,4096]{1,0:T(8,128)(2,1)}, bf16[128,4096]{1,0:T(8,128)(2,1)}, u32[]{:S(2)}, u32[]{:S(2)}) collective-permute-start(bf16[128,4096]{1,0:T(8,128)(2,1)} %get-tuple-element.28), channel_id=1, source_target_pairs={{0,64},{1,193},{2,66},{3,195},{4,68},{5,197},{6,70},{7,199},{8,72}... | collective-permute-start | bytes 3145736 | tf_op jit(solution)/shard_map/ppermute | solution.py:376
  62.7 12.2 %copy-start = (bf16[1,256,4096]{2,1,0:T(8,128)(2,1)S(1)}, bf16[1,256,4096]{2,1,0:T(8,128)(2,1)}, u32[]{:S(2)}) copy-start(bf16[1,256,4096]{2,1,0:T(8,128)(2,1)} %param.29) | copy-start | bytes 6291460
  71.6 13.3 %collective-permute-start.4 = (bf16[96,32,128]{2,1,0:T(8,128)(2,1)S(1)}, bf16[96,32,128]{2,1,0:T(8,128)(2,1)S(1)}, u32[]{:S(2)}, u32[]{:S(2)}) collective-permute-start(bf16[96,32,128]{2,1,0:T(8,128)(2,1)S(1)} %get-tuple-element.48), channel_id=1, source_target_pairs={{0,192},{1,65},{2,194},{3,67},{4,196},{5,69},{6,198},{7,71},{8,200... | collective-permute-start | bytes 2359304 | tf_op jit(solution)/shard_map/ppermute | solution.py:396
  73.6 19.7 %collective-permute-start.6 = (bf16[96,32,128]{2,1,0:T(8,128)(2,1)S(1)}, bf16[96,32,128]{2,1,0:T(8,128)(2,1)S(1)}, u32[]{:S(2)}, u32[]{:S(2)}) collective-permute-start(bf16[96,32,128]{2,1,0:T(8,128)(2,1)S(1)} %get-tuple-element.47), channel_id=1, source_target_pairs={{0,192},{1,65},{2,194},{3,67},{4,196},{5,69},{6,198},{7,71},{8,200... | collective-permute-start | bytes 2359304 | tf_op jit(solution)/shard_map/ppermute | solution.py:396
  87.3 14.4 %collective-permute-start.5 = (bf16[96,32,128]{2,1,0:T(8,128)(2,1)S(1)}, bf16[96,32,128]{2,1,0:T(8,128)(2,1)S(1)}, u32[]{:S(2)}, u32[]{:S(2)}) collective-permute-start(bf16[96,32,128]{2,1,0:T(8,128)(2,1)S(1)} %expert_half.7), channel_id=1, source_target_pairs={{0,192},{1,65},{2,194},{3,67},{4,196},{5,69},{6,198},{7,71},{8,200... | collective-permute-start | bytes 2359304 | tf_op jit(solution)/shard_map/ppermute | solution.py:397
  95.7 14.4 %collective-permute-start.7 = (bf16[96,32,128]{2,1,0:T(8,128)(2,1)S(1)}, bf16[96,32,128]{2,1,0:T(8,128)(2,1)S(1)}, u32[]{:S(2)}, u32[]{:S(2)}) collective-permute-start(bf16[96,32,128]{2,1,0:T(8,128)(2,1)S(1)} %expert_half.8), channel_id=1, source_target_pairs={{0,192},{1,65},{2,194},{3,67},{4,196},{5,69},{6,198},{7,71},{8,200... | collective-permute-start | bytes 2359304 | tf_op jit(solution)/shard_map/ppermute | solution.py:397
  110.4 52.0 %copy-start.6 = (bf16[2,1,8,4096]{3,2,1,0:T(8,128)(2,1)S(1)}, bf16[2,1,8,4096]{3,2,1,0:T(8,128)(2,1)}, u32[]{:S(2)}) copy-start(bf16[2,1,8,4096]{3,2,1,0:T(8,128)(2,1)} %drift_in_ref.3) | copy-start | bytes 393220
  110.4 52.0 %copy-start.7 = (f32[16,4096]{1,0:T(8,128)S(1)}, f32[16,4096]{1,0:T(8,128)}, u32[]{:S(2)}) copy-start(f32[16,4096]{1,0:T(8,128)} %get-tuple-element.36.residual_ref) | copy-start | bytes 786436
  110.4 52.0 %copy-start.10 = (s32[2,1,16,8]{2,3,1,0:T(8,128)S(1)}, s32[2,1,16,8]{2,3,1,0:T(8,128)}, u32[]{:S(2)}) copy-start(s32[2,1,16,8]{2,3,1,0:T(8,128)} %param.25) | copy-start | bytes 3076
  110.4 52.0 %copy-start.11 = (f32[4096]{0:T(1024)S(1)}, f32[4096]{0:T(1024)}, u32[]{:S(2)}) copy-start(f32[4096]{0:T(1024)} %param.24) | copy-start | bytes 49156
  210.8 13.3 %collective-permute-start.8 = (bf16[96,32,128]{2,1,0:T(8,128)(2,1)S(1)}, bf16[96,32,128]{2,1,0:T(8,128)(2,1)S(1)}, u32[]{:S(2)}, u32[]{:S(2)}) collective-permute-start(bf16[96,32,128]{2,1,0:T(8,128)(2,1)S(1)} %get-tuple-element.46), channel_id=1, source_target_pairs={{0,192},{1,65},{2,194},{3,67},{4,196},{5,69},{6,198},{7,71},{8,200... | collective-permute-start | bytes 2359304 | tf_op jit(solution)/shard_map/ppermute | solution.py:396
  211.1 21.4 %collective-permute-start.10 = (bf16[96,32,128]{2,1,0:T(8,128)(2,1)S(1)}, bf16[96,32,128]{2,1,0:T(8,128)(2,1)S(1)}, u32[]{:S(2)}, u32[]{:S(2)}) collective-permute-start(bf16[96,32,128]{2,1,0:T(8,128)(2,1)S(1)} %get-tuple-element.45), channel_id=1, source_target_pairs={{0,192},{1,65},{2,194},{3,67},{4,196},{5,69},{6,198},{7,71},{8,200... | collective-permute-start | bytes 2359304 | tf_op jit(solution)/shard_map/ppermute | solution.py:396
  226.6 14.4 %collective-permute-start.9 = (bf16[96,32,128]{2,1,0:T(8,128)(2,1)S(1)}, bf16[96,32,128]{2,1,0:T(8,128)(2,1)S(1)}, u32[]{:S(2)}, u32[]{:S(2)}) collective-permute-start(bf16[96,32,128]{2,1,0:T(8,128)(2,1)S(1)} %expert_half.10), channel_id=1, source_target_pairs={{0,192},{1,65},{2,194},{3,67},{4,196},{5,69},{6,198},{7,71},{8,200... | collective-permute-start | bytes 2359304 | tf_op jit(solution)/shard_map/ppermute | solution.py:397
  235.0 14.4 %collective-permute-start.11 = (bf16[96,32,128]{2,1,0:T(8,128)(2,1)S(1)}, bf16[96,32,128]{2,1,0:T(8,128)(2,1)S(1)}, u32[]{:S(2)}, u32[]{:S(2)}) collective-permute-start(bf16[96,32,128]{2,1,0:T(8,128)(2,1)S(1)} %expert_half.11), channel_id=1, source_target_pairs={{0,192},{1,65},{2,194},{3,67},{4,196},{5,69},{6,198},{7,71},{8,200... | collective-permute-start | bytes 2359304 | tf_op jit(solution)/shard_map/ppermute | solution.py:397
  (3 other events, 8.6 us)

commit v6 on v5

--- a/solution.py
+++ b/solution.py
@@ -369,12 +369,15 @@
     axes = ("rep", "exp")
     beside, across = pairings(lax.axis_size("rep"), lax.axis_size("exp"))
     own = (w_gate[0], w_up[0], w_down[0])
-    gate_up = [lax.ppermute(part, axes, beside) for part in own[:2]]
-    downs = []
-    for i, half in enumerate(jnp.split(own[2], 2)):
-        gate_up[i], half = lax.optimization_barrier((gate_up[i], half))
-        downs.append(lax.ppermute(half, axes, beside))
-    paired = (*gate_up, *downs)
+    paired_gate, paired_up = (lax.ppermute(part, axes, beside) for part in own[:2])
+    quarter = QUARTER // 4
+    paired_gate, piece = lax.optimization_barrier((paired_gate, own[2][:quarter]))
+    first_down = lax.ppermute(piece, axes, beside)
+    paired_up, piece = lax.optimization_barrier((paired_up, own[2][quarter : 2 * quarter]))
+    second_down = lax.ppermute(piece, axes, beside)
+    first_down, piece = lax.optimization_barrier((first_down, own[2][2 * quarter :]))
+    last_down = lax.ppermute(piece, axes, beside)
+    paired = (paired_gate, paired_up, first_down, second_down, last_down)
     gain = norm_gain.reshape(1, D)
     expert_ids = jnp.swapaxes(expert_ids, 2, 3)
     gates = jnp.swapaxes(gate_weights, 2, 3).astype(jnp.float32)
@@ -400,11 +403,11 @@
             terms = add_part(terms, away, i)
         return lax.all_to_all(terms, "exp", split_axis=0, concat_axis=0, tiled=True), first
 
-    terms, (_, attended, gates) = experts(send, (paired, attended, gates))
+    terms, (_, attended, gates) = experts(send, (paired[:4], attended, gates))
     result, residual, send = combine_and_dispatch(
         terms, residual, attended, drift_in, gain, expert_ids, gates
     )
-    terms, _ = experts(send, paired)
+    terms, _ = experts(send, ())
     return combine_last(terms, residual, result, expert_ids, gates)
 
 

time: 298 us -> 298 us (level)
  waiting for transfers between devices: 81.1 us -> 70.4 us
  starting transfers between devices: 27.4 us -> 33.3 us
    ppermute x4, waiting for transfers between devices: 23.1 us -> 14.7 us  [experts(): lax.ppermute(rows[i * size:(i + 1) * size], axes, across)]
    all_to_all x1, waiting for transfers between devices: 8.42 us -> 1.89 us  [experts(): rows = lax.all_to_all(send, 'exp', split_axis=0, concat_axis=0, tiled=True)]
    ppermute x4 -> x5, waiting for transfers between devices: 30.8 us -> 35.8 us  [the longest x2 24 us: on_device(): lax.ppermute(part, axes, beside)]
    ppermute x4, starting transfers between devices: 5.1 us -> 9.73 us  [experts(): lax.ppermute(expert_half(part, weights), axes, across)]
    split x1 -> x0, local copies, waits for them, and re-layouts: 3.3 us -> none  [on_device(): jnp.split(own[2], 2)]
    unnamed x28 -> x38, local copies, waits for them, and re-layouts: 3.25 us -> 6.47 us
  transfers between devices with their start and end apart: 13 -> 14, of which waited for: 12 -> 12; matrix products, arithmetic and copies ran while one was open for 1% -> 1% of each run, Pallas kernels for 11% -> 11%
where the time goes in v6:
time: 298 us; the launch traced here: 296 us
  blocking collectives  143 us (48%)
  waiting for transfers between devices  70.4 us (24%)
  Pallas kernels  37.9 us (13%)
  starting transfers between devices  33.3 us (11%)
  local copies, waits for them, and re-layouts  9.51 us (3%)
    all_to_all x2, blocking collectives, experts(): lax.all_to_all(terms, 'exp', split_axis=0, concat_axis=0, tiled=True)  98.2 us
    all_to_all x1, blocking collectives, experts(): rows = lax.all_to_all(send, 'exp', split_axis=0, concat_axis=0, tiled=True)  45.3 us
    ppermute x2, waiting for transfers between devices, on_device(): lax.ppermute(part, axes, beside)  24 us
    ppermute x4, waiting for transfers between devices, experts(): lax.ppermute(expert_half(part, weights), axes, across)  17.9 us
    pallas_call x6, Pallas kernels, expert_half(): pl.pallas_call(body, in_specs=[vmem] * (1 + 3 * pieces), out_specs=vmem,...  16.7 us
    ppermute x4, waiting for transfers between devices, experts(): lax.ppermute(rows[i * size:(i + 1) * size], axes, across)  14.7 us
    all_to_all x1, starting transfers between devices, experts(): rows = lax.all_to_all(send, 'exp', split_axis=0, concat_axis=0, tiled=True)  12.2 us
    ppermute x1, waiting for transfers between devices, on_device(): last_down = lax.ppermute(piece, axes, beside)  10.8 us
  transfers between devices with their start and end apart: 14, of which 12 were waited for; matrix products, arithmetic and copies ran while one was open for 1% of the time, Pallas kernels for 11%

profile of v6, /device:TPU:24, one launch (start us, length us, event | category | flops | bytes accessed | tf_op | source)
XLA Modules:
  0.0 295.5 jit_solution(13715129620895932807)
XLA Ops:
  2.7 7.7 %first_attention.1 = (f32[16,4096]{1,0:T(8,128)}, bf16[192,32,128]{2,1,0:T(8,128)(2,1)}) custom-call(s32[1]{0:T(128)S(6)} %copy.24.lengths_ref, s32[2,1,8]{2,1,0:T(1,128)} %drift_ref.3, bf16[2,1,16,4096]{3,2,1,0:T(8,128)(2,1)} %q_ref.3, bf16[1,2048,512]{2,1,0:T(8,128)(2,1)} %k_ref.3, bf16[1,2048,512]{2,1,0:T(8,128)(2,1)} %v_ref.3, ...), custom_call_target="tpu_custom_call" | custom-call | tf_op jit(solution)/shard_map/first_attention/pallas_call | solution.py:146
  10.4 12.2 %all-to-all-start = ((bf16[192,32,128]{2,1,0:T(8,128)(2,1)}), bf16[192,32,128]{2,1,0:T(8,128)(2,1)S(1)}, u32[]{:S(2)}, u32[]{:S(2)}) async-start(bf16[192,32,128]{2,1,0:T(8,128)(2,1)} %get-tuple-element.25), calls=%async_computation | async-start | bytes 3145728 | tf_op jit(solution)/shard_map/all_to_all | solution.py:396
  24.1 2.3 collective-permute-done.refs_0_
  27.1 21.7 %collective-permute-done.1.refs_1_ = bf16[4096,256]{1,0:T(8,128)(2,1)} collective-permute-done((bf16[4096,256]{1,0:T(8,128)(2,1)}, bf16[4096,256]{1,0:T(8,128)(2,1)}, u32[]{:S(2)}, u32[]{:S(2)}) %collective-permute-start.1) | collective-permute-done | bytes 2097184 | tf_op jit(solution)/shard_map/ppermute | solution.py:372
  52.3 4.6 %second_attention.1.attended_ref = f32[16,4096]{1,0:T(8,128)S(1)} custom-call(s32[1]{0:T(128)S(6)} %copy.24.lengths_ref, s32[2,1,8]{2,1,0:T(1,128)S(1)} %copy-done.17, bf16[2,1,16,4096]{3,2,1,0:T(8,128)(2,1)S(1)} %copy-done.6, bf16[1,2048,512]{2,1,0:T(8,128)(2,1)S(1)} %copy-done.2, bf16[1,2048,512]{2,1,0:T(8,128)(2,1)S(1)} %copy-done.3, ...), custom_call_target="tpu_custom_call" | custom-call | tf_op jit(solution)/shard_map/second_attention/pallas_call | solution.py:180
  63.4 2.9 collective-permute-start.7
  69.9 10.8 %collective-permute-done.4.refs_4_ = bf16[128,4096]{1,0:T(8,128)(2,1)S(1)} collective-permute-done((bf16[128,4096]{1,0:T(8,128)(2,1)}, bf16[128,4096]{1,0:T(8,128)(2,1)S(1)}, u32[]{:S(2)}, u32[]{:S(2)}) %collective-permute-start.4) | collective-permute-done | bytes 1048608 | tf_op jit(solution)/shard_map/ppermute | solution.py:379
  83.1 2.5 expert_half.7
  85.5 2.7 collective-permute-start.6
  89.1 2.5 expert_half.8
  91.6 3.0 %collective-permute-start.8 = (bf16[96,32,128]{2,1,0:T(8,128)(2,1)S(1)}, bf16[96,32,128]{2,1,0:T(8,128)(2,1)S(1)}, u32[]{:S(2)}, u32[]{:S(2)}) collective-permute-start(bf16[96,32,128]{2,1,0:T(8,128)(2,1)S(1)} %expert_half.8), channel_id=1, source_target_pairs={{0,192},{1,65},{2,194},{3,67},{4,196},{5,69},{6,198},{7,71},{8,200... | collective-permute-start | bytes 2359304 | tf_op jit(solution)/shard_map/ppermute | solution.py:400
  94.7 3.4 %expert_half.6.terms_ref = bf16[192,32,128]{2,1,0:T(8,128)(2,1)S(1)} custom-call(bf16[192,32,128]{2,1,0:T(8,128)(2,1)S(1)} %all-to-all-done.refs_0_, bf16[4096,256]{1,0:T(8,128)(2,1)S(1)} %get-tuple-element.32.refs_1_, bf16[4096,256]{1,0:T(8,128)(2,1)S(1)} %get-tuple-element.33.refs_2_, bf16[256,4096]{1,0:T(8,128)(2,1)S(1)} %get-tuple-element.34.refs_3_, ...), custom_call_target="tpu_custom_call" | custom-call | tf_op jit(solution)/shard_map/expert_half/pallas_call | solution.py:248
  99.2 8.2 %collective-permute-done.8.away_ref = bf16[96,32,128]{2,1,0:T(8,128)(2,1)S(1)} collective-permute-done((bf16[96,32,128]{2,1,0:T(8,128)(2,1)S(1)}, bf16[96,32,128]{2,1,0:T(8,128)(2,1)S(1)}, u32[]{:S(2)}, u32[]{:S(2)}) %collective-permute-start.8) | collective-permute-done | bytes 786464 | tf_op jit(solution)/shard_map/ppermute | solution.py:400
  107.7 52.9 %all_to_all.20.terms_ref = bf16[192,32,128]{2,1,0:T(8,128)(2,1)S(1)} all-to-all(bf16[192,32,128]{2,1,0:T(8,128)(2,1)S(1)} %add_part.5), channel_id=1, replica_groups=mesh['rep'=4,'exp'=64] {'exp'}, dimensions={0} | all-to-all | bytes 3145728 | tf_op jit(solution)/shard_map/all_to_all | solution.py:404
  160.7 2.8 combine_and_dispatch.1
  163.5 45.3 %all_to_all.21.refs_0_ = bf16[192,32,128]{2,1,0:T(8,128)(2,1)S(1)} all-to-all(bf16[192,32,128]{2,1,0:T(8,128)(2,1)S(1)} %get-tuple-element.42), channel_id=1, replica_groups=mesh['rep'=4,'exp'=64] {'exp'}, dimensions={0} | all-to-all | bytes 3145728 | tf_op jit(solution)/shard_map/all_to_all | solution.py:396
  212.3 10.0 %collective-permute-done.9.refs_0_ = bf16[96,32,128]{2,1,0:T(8,128)(2,1)S(1)} collective-permute-done((bf16[96,32,128]{2,1,0:T(8,128)(2,1)S(1)}, bf16[96,32,128]{2,1,0:T(8,128)(2,1)S(1)}, u32[]{:S(2)}, u32[]{:S(2)}) %collective-permute-start.9) | collective-permute-done | bytes 786464 | tf_op jit(solution)/shard_map/ppermute | solution.py:399
  222.3 2.5 expert_half.10
  226.9 3.8 %collective-permute-done.11.refs_0_ = bf16[96,32,128]{2,1,0:T(8,128)(2,1)S(1)} collective-permute-done((bf16[96,32,128]{2,1,0:T(8,128)(2,1)S(1)}, bf16[96,32,128]{2,1,0:T(8,128)(2,1)S(1)}, u32[]{:S(2)}, u32[]{:S(2)}) %collective-permute-start.11) | collective-permute-done | bytes 786464 | tf_op jit(solution)/shard_map/ppermute | solution.py:399
  230.7 2.5 expert_half.11
  235.1 3.4 %expert_half.9.terms_ref = bf16[192,32,128]{2,1,0:T(8,128)(2,1)S(1)} custom-call(bf16[192,32,128]{2,1,0:T(8,128)(2,1)S(1)} %all_to_all.21.refs_0_, bf16[4096,256]{1,0:T(8,128)(2,1)S(1)} %get-tuple-element.32.refs_1_, bf16[4096,256]{1,0:T(8,128)(2,1)S(1)} %get-tuple-element.33.refs_2_, bf16[256,4096]{1,0:T(8,128)(2,1)S(1)} %get-tuple-element.34.refs_3_, ...), custom_call_target="tpu_custom_call" | custom-call | tf_op jit(solution)/shard_map/expert_half/pallas_call | solution.py:248
  239.4 8.2 %collective-permute-done.12.away_ref = bf16[96,32,128]{2,1,0:T(8,128)(2,1)S(1)} collective-permute-done((bf16[96,32,128]{2,1,0:T(8,128)(2,1)S(1)}, bf16[96,32,128]{2,1,0:T(8,128)(2,1)S(1)}, u32[]{:S(2)}, u32[]{:S(2)}) %collective-permute-start.12) | collective-permute-done | bytes 786464 | tf_op jit(solution)/shard_map/ppermute | solution.py:400
  247.8 45.3 %all_to_all.22.terms_ref = bf16[192,32,128]{2,1,0:T(8,128)(2,1)S(1)} all-to-all(bf16[192,32,128]{2,1,0:T(8,128)(2,1)S(1)} %add_part.7), channel_id=1, replica_groups=mesh['rep'=4,'exp'=64] {'exp'}, dimensions={0} | all-to-all | bytes 3145728 | tf_op jit(solution)/shard_map/all_to_all | solution.py:404
  293.1 2.4 combine_last.1
  (66 shorter events, 31.2 us)
Async XLA Ops:
  0.0 26.4 %collective-permute-start = (bf16[4096,256]{1,0:T(8,128)(2,1)}, bf16[4096,256]{1,0:T(8,128)(2,1)}, u32[]{:S(2)}, u32[]{:S(2)}) collective-permute-start(bf16[4096,256]{1,0:T(8,128)(2,1)} %bitcast.14), channel_id=1, source_target_pairs={{0,64},{1,193},{2,66},{3,195},{4,68},{5,197},{6,70},{7,199},{8,72}... | collective-permute-start | bytes 6291464 | tf_op jit(solution)/shard_map/ppermute | solution.py:372
  0.7 48.1 %collective-permute-start.1 = (bf16[4096,256]{1,0:T(8,128)(2,1)}, bf16[4096,256]{1,0:T(8,128)(2,1)}, u32[]{:S(2)}, u32[]{:S(2)}) collective-permute-start(bf16[4096,256]{1,0:T(8,128)(2,1)} %bitcast.16), channel_id=1, source_target_pairs={{0,64},{1,193},{2,66},{3,195},{4,68},{5,197},{6,70},{7,199},{8,72}... | collective-permute-start | bytes 6291464 | tf_op jit(solution)/shard_map/ppermute | solution.py:372
  10.4 40.3 %copy-start.6 = (bf16[2,1,16,4096]{3,2,1,0:T(8,128)(2,1)S(1)}, bf16[2,1,16,4096]{3,2,1,0:T(8,128)(2,1)}, u32[]{:S(2)}) copy-start(bf16[2,1,16,4096]{3,2,1,0:T(8,128)(2,1)} %q_ref.3) | copy-start | bytes 786436
  10.4 40.3 %copy-start.13 = (bf16[2,1,16,512]{3,2,1,0:T(8,128)(2,1)S(1)}, bf16[2,1,16,512]{3,2,1,0:T(8,128)(2,1)}, u32[]{:S(2)}) copy-start(bf16[2,1,16,512]{3,2,1,0:T(8,128)(2,1)} %nk_ref.3) | copy-start | bytes 98308
  10.4 40.3 %copy-start.14 = (bf16[2,1,16,512]{3,2,1,0:T(8,128)(2,1)S(1)}, bf16[2,1,16,512]{3,2,1,0:T(8,128)(2,1)}, u32[]{:S(2)}) copy-start(bf16[2,1,16,512]{3,2,1,0:T(8,128)(2,1)} %nv_ref.3) | copy-start | bytes 98308
  10.4 52.3 %all-to-all-start = ((bf16[192,32,128]{2,1,0:T(8,128)(2,1)}), bf16[192,32,128]{2,1,0:T(8,128)(2,1)S(1)}, u32[]{:S(2)}, u32[]{:S(2)}) async-start(bf16[192,32,128]{2,1,0:T(8,128)(2,1)} %get-tuple-element.25), calls=%async_computation | async-start | bytes 3145728 | tf_op jit(solution)/shard_map/all_to_all | solution.py:396
  22.6 27.0 %copy-start = (bf16[1,256,4096]{2,1,0:T(8,128)(2,1)S(1)}, bf16[1,256,4096]{2,1,0:T(8,128)(2,1)}, u32[]{:S(2)}) copy-start(bf16[1,256,4096]{2,1,0:T(8,128)(2,1)} %param.29) | copy-start | bytes 6291460
  22.6 28.1 %copy-start.2 = (bf16[1,2048,512]{2,1,0:T(8,128)(2,1)S(1)}, bf16[1,2048,512]{2,1,0:T(8,128)(2,1)}, u32[]{:S(2)}) copy-start(bf16[1,2048,512]{2,1,0:T(8,128)(2,1)} %k_ref.3) | copy-start | bytes 6291460
  22.6 28.1 %copy-start.17 = (s32[2,1,8]{2,1,0:T(1,128)S(1)}, s32[2,1,8]{2,1,0:T(1,128)}, u32[]{:S(2)}) copy-start(s32[2,1,8]{2,1,0:T(1,128)} %drift_ref.3) | copy-start | bytes 196
  26.4 30.5 %collective-permute-start.2 = (bf16[64,4096]{1,0:T(8,128)(2,1)S(1)}, bf16[64,4096]{1,0:T(8,128)(2,1)S(1)}, u32[]{:S(2)}, u32[]{:S(2)}) collective-permute-start(bf16[64,4096]{1,0:T(8,128)(2,1)S(1)} %get-tuple-element.28), channel_id=1, source_target_pairs={{0,64},{1,193},{2,66},{3,195},{4,68},{5,197},{6,70},{7,199},{8,72}... | collective-permute-start | bytes 1572872 | tf_op jit(solution)/shard_map/ppermute | solution.py:375
  48.8 11.1 %collective-permute-start.3 = (bf16[64,4096]{1,0:T(8,128)(2,1)S(1)}, bf16[64,4096]{1,0:T(8,128)(2,1)S(1)}, u32[]{:S(2)}, u32[]{:S(2)}) collective-permute-start(bf16[64,4096]{1,0:T(8,128)(2,1)S(1)} %get-tuple-element.30), channel_id=1, source_target_pairs={{0,64},{1,193},{2,66},{3,195},{4,68},{5,197},{6,70},{7,199},{8,72}... | collective-permute-start | bytes 1572872 | tf_op jit(solution)/shard_map/ppermute | solution.py:377
  57.7 23.1 %collective-permute-start.4 = (bf16[128,4096]{1,0:T(8,128)(2,1)}, bf16[128,4096]{1,0:T(8,128)(2,1)S(1)}, u32[]{:S(2)}, u32[]{:S(2)}) collective-permute-start(bf16[128,4096]{1,0:T(8,128)(2,1)} %slice_bitcast_fusion), channel_id=1, source_target_pairs={{0,64},{1,193},{2,66},{3,195},{4,68},{5,197},{6,70},{7,199},{8,72}... | collective-permute-start | bytes 3145736 | tf_op jit(solution)/shard_map/ppermute | solution.py:379
  63.0 20.1 %collective-permute-start.5 = (bf16[96,32,128]{2,1,0:T(8,128)(2,1)S(1)}, bf16[96,32,128]{2,1,0:T(8,128)(2,1)S(1)}, u32[]{:S(2)}, u32[]{:S(2)}) collective-permute-start(bf16[96,32,128]{2,1,0:T(8,128)(2,1)S(1)} %get-tuple-element.50), channel_id=1, source_target_pairs={{0,192},{1,65},{2,194},{3,67},{4,196},{5,69},{6,198},{7,71},{8,200... | collective-permute-start | bytes 2359304 | tf_op jit(solution)/shard_map/ppermute | solution.py:399
  63.4 25.8 %collective-permute-start.7 = (bf16[96,32,128]{2,1,0:T(8,128)(2,1)S(1)}, bf16[96,32,128]{2,1,0:T(8,128)(2,1)S(1)}, u32[]{:S(2)}, u32[]{:S(2)}) collective-permute-start(bf16[96,32,128]{2,1,0:T(8,128)(2,1)S(1)} %get-tuple-element.49), channel_id=1, source_target_pairs={{0,192},{1,65},{2,194},{3,67},{4,196},{5,69},{6,198},{7,71},{8,200... | collective-permute-start | bytes 2359304 | tf_op jit(solution)/shard_map/ppermute | solution.py:399
  85.5 13.5 %collective-permute-start.6 = (bf16[96,32,128]{2,1,0:T(8,128)(2,1)S(1)}, bf16[96,32,128]{2,1,0:T(8,128)(2,1)S(1)}, u32[]{:S(2)}, u32[]{:S(2)}) collective-permute-start(bf16[96,32,128]{2,1,0:T(8,128)(2,1)S(1)} %expert_half.7), channel_id=1, source_target_pairs={{0,192},{1,65},{2,194},{3,67},{4,196},{5,69},{6,198},{7,71},{8,200... | collective-permute-start | bytes 2359304 | tf_op jit(solution)/shard_map/ppermute | solution.py:400
  91.6 15.8 %collective-permute-start.8 = (bf16[96,32,128]{2,1,0:T(8,128)(2,1)S(1)}, bf16[96,32,128]{2,1,0:T(8,128)(2,1)S(1)}, u32[]{:S(2)}, u32[]{:S(2)}) collective-permute-start(bf16[96,32,128]{2,1,0:T(8,128)(2,1)S(1)} %expert_half.8), channel_id=1, source_target_pairs={{0,192},{1,65},{2,194},{3,67},{4,196},{5,69},{6,198},{7,71},{8,200... | collective-permute-start | bytes 2359304 | tf_op jit(solution)/shard_map/ppermute | solution.py:400
  107.7 53.0 %copy-start.11 = (bf16[2,1,8,4096]{3,2,1,0:T(8,128)(2,1)S(1)}, bf16[2,1,8,4096]{3,2,1,0:T(8,128)(2,1)}, u32[]{:S(2)}) copy-start(bf16[2,1,8,4096]{3,2,1,0:T(8,128)(2,1)} %drift_in_ref.3) | copy-start | bytes 393220
  107.7 53.0 %copy-start.12 = (f32[16,4096]{1,0:T(8,128)S(1)}, f32[16,4096]{1,0:T(8,128)}, u32[]{:S(2)}) copy-start(f32[16,4096]{1,0:T(8,128)} %get-tuple-element.39.residual_ref) | copy-start | bytes 786436
  107.7 52.9 %copy-start.15 = (s32[2,1,16,8]{2,3,1,0:T(8,128)S(1)}, s32[2,1,16,8]{2,3,1,0:T(8,128)}, u32[]{:S(2)}) copy-start(s32[2,1,16,8]{2,3,1,0:T(8,128)} %param.25) | copy-start | bytes 3076
  107.7 52.9 %copy-start.16 = (f32[4096]{0:T(1024)S(1)}, f32[4096]{0:T(1024)}, u32[]{:S(2)}) copy-start(f32[4096]{0:T(1024)} %param.24) | copy-start | bytes 49156
  209.0 13.3 %collective-permute-start.9 = (bf16[96,32,128]{2,1,0:T(8,128)(2,1)S(1)}, bf16[96,32,128]{2,1,0:T(8,128)(2,1)S(1)}, u32[]{:S(2)}, u32[]{:S(2)}) collective-permute-start(bf16[96,32,128]{2,1,0:T(8,128)(2,1)S(1)} %get-tuple-element.48), channel_id=1, source_target_pairs={{0,192},{1,65},{2,194},{3,67},{4,196},{5,69},{6,198},{7,71},{8,200... | collective-permute-start | bytes 2359304 | tf_op jit(solution)/shard_map/ppermute | solution.py:399
  210.9 19.8 %collective-permute-start.11 = (bf16[96,32,128]{2,1,0:T(8,128)(2,1)S(1)}, bf16[96,32,128]{2,1,0:T(8,128)(2,1)S(1)}, u32[]{:S(2)}, u32[]{:S(2)}) collective-permute-start(bf16[96,32,128]{2,1,0:T(8,128)(2,1)S(1)} %get-tuple-element.47), channel_id=1, source_target_pairs={{0,192},{1,65},{2,194},{3,67},{4,196},{5,69},{6,198},{7,71},{8,200... | collective-permute-start | bytes 2359304 | tf_op jit(solution)/shard_map/ppermute | solution.py:399
  224.8 14.4 %collective-permute-start.10 = (bf16[96,32,128]{2,1,0:T(8,128)(2,1)S(1)}, bf16[96,32,128]{2,1,0:T(8,128)(2,1)S(1)}, u32[]{:S(2)}, u32[]{:S(2)}) collective-permute-start(bf16[96,32,128]{2,1,0:T(8,128)(2,1)S(1)} %expert_half.10), channel_id=1, source_target_pairs={{0,192},{1,65},{2,194},{3,67},{4,196},{5,69},{6,198},{7,71},{8,200... | collective-permute-start | bytes 2359304 | tf_op jit(solution)/shard_map/ppermute | solution.py:400
  233.2 14.4 %collective-permute-start.12 = (bf16[96,32,128]{2,1,0:T(8,128)(2,1)S(1)}, bf16[96,32,128]{2,1,0:T(8,128)(2,1)S(1)}, u32[]{:S(2)}, u32[]{:S(2)}) collective-permute-start(bf16[96,32,128]{2,1,0:T(8,128)(2,1)S(1)} %expert_half.11), channel_id=1, source_target_pairs={{0,192},{1,65},{2,194},{3,67},{4,196},{5,69},{6,198},{7,71},{8,200... | collective-permute-start | bytes 2359304 | tf_op jit(solution)/shard_map/ppermute | solution.py:400
  (9 other events, 37.2 us)

commit v7 on v5

--- a/solution.py
+++ b/solution.py
@@ -42,12 +42,38 @@
         visit(t, picked)
 
 
+def slot_places(ids):
+    def body(ids_ref, places_ref, counts):
+        for denoise in range(2):
+
+            def visit(t, picked):
+                for j, slot in enumerate(picked):
+                    places_ref[denoise, 0, j, t] = slot
+
+            each_slot(ids_ref, denoise, counts, visit)
+
+    return pl.pallas_call(
+        body,
+        in_specs=[smem_spec()],
+        out_specs=smem_spec(),
+        out_shape=jax.ShapeDtypeStruct(ids.shape, jnp.int32),
+        scratch_shapes=[pltpu.SMEM((EXPERTS,), jnp.int32)],
+        name="slot_places",
+    )(ids)
+
+
+def each_place(places_ref, denoise, visit):
+    @pl.loop(0, ROWS, unroll=4)
+    def _(t):
+        visit(t, [places_ref[denoise, 0, j, t] for j in range(TOP)])
+
+
 def normalize(residual, gain):
     inverse = lax.rsqrt(jnp.mean(residual * residual, axis=-1, keepdims=True) + 1e-06)
     return residual * inverse * gain
 
 
-def dispatch(normed, ids_ref, denoise, counts, spread, packed, send_ref):
+def dispatch(normed, walk, spread, packed, send_ref):
     for k in range(H):
         spread[pl.ds(k, ROWS, stride=H), :] = normed[:, k * HD : (k + 1) * HD]
     packed[...] = spread[...].reshape(ROWS, H, HD).astype(jnp.bfloat16)
@@ -58,17 +84,17 @@
         for slot in picked:
             send_ref[slot] = row
 
-    each_slot(ids_ref, denoise, counts, visit)
-
-
-def combine(terms_ref, ids_ref, gates_ref, denoise, counts, spread):
+    walk(visit)
+
+
+def combine(terms_ref, places_ref, gates_ref, denoise, spread):
     def visit(t, picked):
         total = jnp.zeros((H, HD), jnp.float32)
         for j, slot in enumerate(picked):
             total = total + gates_ref[denoise, 0, j, t] * terms_ref[slot].astype(jnp.float32)
         spread[pl.ds(pl.multiple_of(t * H, H), H), :] = total
 
-    each_slot(ids_ref, denoise, counts, visit)
+    each_place(places_ref, denoise, visit)
     return jnp.concatenate([spread[pl.ds(k, ROWS, stride=H), :] for k in range(H)], axis=1)
 
 
@@ -141,7 +167,8 @@
             )
             residual = inputs + attended[...]
             residual_ref[...] = residual
-            dispatch(normalize(residual, gain_ref[...]), ids_ref, 0, counts, spread, packed, send_ref)
+            walk = lambda visit: each_slot(ids_ref, 0, counts, visit)
+            dispatch(normalize(residual, gain_ref[...]), walk, spread, packed, send_ref)
 
     return pl.pallas_call(
         body,
@@ -283,58 +310,58 @@
     )(terms, away)
 
 
-def combine_and_dispatch(terms, residual, attended, drift_in, gain, ids, gates):
-    def body(terms_ref, residual_ref, attended_ref, drift_in_ref, gain_ref, ids_ref, gates_ref,
-             result_ref, next_ref, send_ref, spread, packed, counts):
-        moe = combine(terms_ref, ids_ref, gates_ref, 0, counts, spread)
+def combine_and_dispatch(terms, residual, attended, drift_in, gain, places, gates):
+    def body(terms_ref, residual_ref, attended_ref, drift_in_ref, gain_ref, places_ref, gates_ref,
+             out_ref, next_ref, send_ref, spread, packed):
+        moe = combine(terms_ref, places_ref, gates_ref, 0, spread)
         result = (residual_ref[...] + moe).astype(jnp.bfloat16)
-        result_ref[...] = result
+        out_ref[0, 0] = result
         inputs = jnp.concatenate(
             [result.astype(jnp.float32)[:BLOCK], drift_in_ref[1, 0].astype(jnp.float32)], axis=0
         )
         following = inputs + attended_ref[...]
         next_ref[...] = following
-        dispatch(normalize(following, gain_ref[...]), ids_ref, 1, counts, spread, packed, send_ref)
+        walk = lambda visit: each_place(places_ref, 1, visit)
+        dispatch(normalize(following, gain_ref[...]), walk, spread, packed, send_ref)
 
     vmem = pl.BlockSpec(memory_space=pltpu.VMEM)
-    return pl.pallas_call(
-        body,
+    first_half = pl.BlockSpec((1, 1, ROWS, D), lambda i: (0, 0, 0, 0))
+    return pl.pallas_call(
+        body,
+        grid=(1,),
         in_specs=[vmem] * 5 + [smem_spec()] * 2,
-        out_specs=[vmem] * 3,
+        out_specs=[first_half, vmem, vmem],
         out_shape=[
-            jax.ShapeDtypeStruct((ROWS, D), jnp.bfloat16),
+            jax.ShapeDtypeStruct((2, 1, ROWS, D), jnp.bfloat16),
             jax.ShapeDtypeStruct((ROWS, D), jnp.float32),
             jax.ShapeDtypeStruct((SLOTS, H, HD), jnp.bfloat16),
         ],
         scratch_shapes=[
             pltpu.VMEM((ROWS * H, HD), jnp.float32),
             pltpu.VMEM((ROWS, H, HD), jnp.bfloat16),
-            pltpu.SMEM((EXPERTS,), jnp.int32),
         ],
         compiler_params=pltpu.CompilerParams(vmem_limit_bytes=VMEM_LIMIT),
         name="combine_and_dispatch",
-    )(terms, residual, attended, drift_in, gain, ids, gates)
-
-
-def combine_last(terms, residual, first_result, ids, gates):
-    def body(terms_ref, residual_ref, first_ref, ids_ref, gates_ref, out_ref, spread, counts):
-        moe = combine(terms_ref, ids_ref, gates_ref, 1, counts, spread)
-        out_ref[0, 0] = first_ref[...]
-        out_ref[1, 0] = (residual_ref[...] + moe).astype(jnp.bfloat16)
+    )(terms, residual, attended, drift_in, gain, places, gates)
+
+
+def combine_last(terms, residual, output, places, gates):
+    def body(terms_ref, residual_ref, output_ref, places_ref, gates_ref, out_ref, spread):
+        moe = combine(terms_ref, places_ref, gates_ref, 1, spread)
+        out_ref[0, 0] = (residual_ref[...] + moe).astype(jnp.bfloat16)
 
     vmem = pl.BlockSpec(memory_space=pltpu.VMEM)
     return pl.pallas_call(
         body,
-        in_specs=[vmem] * 3 + [smem_spec()] * 2,
-        out_specs=vmem,
-        out_shape=jax.ShapeDtypeStruct((2, 1, ROWS, D), jnp.bfloat16),
-        scratch_shapes=[
-            pltpu.VMEM((ROWS * H, HD), jnp.float32),
-            pltpu.SMEM((EXPERTS,), jnp.int32),
-        ],
+        grid=(1,),
+        in_specs=[vmem] * 2 + [pl.BlockSpec(memory_space=pl.ANY)] + [smem_spec()] * 2,
+        out_specs=pl.BlockSpec((1, 1, ROWS, D), lambda i: (1, 0, 0, 0)),
+        out_shape=jax.ShapeDtypeStruct(output.shape, output.dtype),
+        input_output_aliases={2: 0},
+        scratch_shapes=[pltpu.VMEM((ROWS * H, HD), jnp.float32)],
         compiler_params=pltpu.CompilerParams(vmem_limit_bytes=VMEM_LIMIT),
         name="combine_last",
-    )(terms, residual, first_result, ids, gates)
+    )(terms, residual, output, places, gates)
 
 
 def pairings(reps, exps):
@@ -400,12 +427,14 @@
             terms = add_part(terms, away, i)
         return lax.all_to_all(terms, "exp", split_axis=0, concat_axis=0, tiled=True), first
 
-    terms, (_, attended, gates) = experts(send, (paired, attended, gates))
-    result, residual, send = combine_and_dispatch(
-        terms, residual, attended, drift_in, gain, expert_ids, gates
-    )
-    terms, _ = experts(send, paired)
-    return combine_last(terms, residual, result, expert_ids, gates)
+    terms, (_, attended, gates, places) = experts(
+        send, (paired, attended, gates, slot_places(expert_ids))
+    )
+    output, residual, send = combine_and_dispatch(
+        terms, residual, attended, drift_in, gain, places, gates
+    )
+    terms, _ = experts(send, ())
+    return combine_last(terms, residual, output, places, gates)
 
 
 def solution(mesh):

time: 298 us -> 297 us (level)
  waiting for transfers between devices: 81.1 us -> 75.4 us
  local copies, waits for them, and re-layouts: 7.09 us -> 10.1 us
    all_to_all x1, waiting for transfers between devices: 8.42 us -> 2.3 us  [experts(): rows = lax.all_to_all(send, 'exp', split_axis=0, concat_axis=0, tiled=True)]
    unnamed x28, local copies, waits for them, and re-layouts: 3.25 us -> 6.41 us
    pallas_call x2 -> x3, Pallas kernels: 5.23 us -> 7.33 us  [the longest x1 2.77 us: slot_places(): pl.pallas_call(body, in_specs=[smem_spec()], out_specs=smem_spec(), out_s...]
  transfers between devices with their start and end apart: 13 -> 13, of which waited for: 12 -> 12; matrix products, arithmetic and copies ran while one was open for 1% -> 1% of each run, Pallas kernels for 11% -> 12%
where the time goes in v7:
time: 297 us
  blocking collectives  142 us (48%)
  waiting for transfers between devices  75.4 us (25%)
  Pallas kernels  40.3 us (14%)
  starting transfers between devices  27.3 us (9%)
  local copies, waits for them, and re-layouts  10.1 us (3%)
    all_to_all x2, blocking collectives, experts(): lax.all_to_all(terms, 'exp', split_axis=0, concat_axis=0, tiled=True)  97.3 us
    all_to_all x1, blocking collectives, experts(): rows = lax.all_to_all(send, 'exp', split_axis=0, concat_axis=0, tiled=True)  45.2 us
    ppermute x4, waiting for transfers between devices, experts(): lax.ppermute(rows[i * size:(i + 1) * size], axes, across)  22.9 us
    ppermute x2, waiting for transfers between devices, on_device(): gate_up = [lax.ppermute(part, axes, beside) for part in own[:2]]  22.4 us
    ppermute x4, waiting for transfers between devices, experts(): lax.ppermute(expert_half(part, weights), axes, across)  19 us
    pallas_call x6, Pallas kernels, expert_half(): pl.pallas_call(body, in_specs=[vmem] * (1 + 3 * pieces), out_specs=vmem,...  16.7 us
    all_to_all x1, starting transfers between devices, experts(): rows = lax.all_to_all(send, 'exp', split_axis=0, concat_axis=0, tiled=True)  12 us
    ppermute x2, waiting for transfers between devices, on_device(): downs.append(lax.ppermute(half, axes, beside))  8.77 us
  transfers between devices with their start and end apart: 13, of which 12 were waited for; matrix products, arithmetic and copies ran while one was open for 1% of the time, Pallas kernels for 12%

profile of v7, /device:TPU:24, one launch (start us, length us, event | category | flops | bytes accessed | tf_op | source)
XLA Modules:
  0.0 296.6 jit_solution(10825567020942460820)
XLA Ops:
  2.7 7.7 %first_attention.1 = (f32[16,4096]{1,0:T(8,128)}, bf16[192,32,128]{2,1,0:T(8,128)(2,1)}) custom-call(s32[1]{0:T(128)S(6)} %copy.26.lengths_ref, s32[2,1,8]{2,1,0:T(1,128)} %drift_ref.3, bf16[2,1,16,4096]{3,2,1,0:T(8,128)(2,1)} %q_ref.3, bf16[1,2048,512]{2,1,0:T(8,128)(2,1)} %k_ref.3, bf16[1,2048,512]{2,1,0:T(8,128)(2,1)} %v_ref.3, ...), custom_call_target="tpu_custom_call" | custom-call | tf_op jit(solution)/shard_map/first_attention/pallas_call | solution.py:173
  10.4 12.0 %all-to-all-start = ((bf16[192,32,128]{2,1,0:T(8,128)(2,1)}), bf16[192,32,128]{2,1,0:T(8,128)(2,1)S(1)}, u32[]{:S(2)}, u32[]{:S(2)}) async-start(bf16[192,32,128]{2,1,0:T(8,128)(2,1)} %get-tuple-element.24), calls=%async_computation | async-start | bytes 3145728 | tf_op jit(solution)/shard_map/all_to_all | solution.py:420
  22.4 3.2 %slice_bitcast_fusion = (bf16[128,4096]{1,0:T(8,128)(2,1)}, bf16[128,4096]{1,0:T(8,128)(2,1)}) fusion(bf16[1,256,4096]{2,1,0:T(8,128)(2,1)} %param.29), kind=kLoop, calls=%fused_computation | loop fusion | bytes 4194304 | tf_op jit(solution)/shard_map/split | solution.py:401
  27.1 21.7 %collective-permute-done.1.refs_1_ = bf16[4096,256]{1,0:T(8,128)(2,1)} collective-permute-done((bf16[4096,256]{1,0:T(8,128)(2,1)}, bf16[4096,256]{1,0:T(8,128)(2,1)}, u32[]{:S(2)}, u32[]{:S(2)}) %collective-permute-start.1) | collective-permute-done | bytes 2097184 | tf_op jit(solution)/shard_map/ppermute | solution.py:399
  49.6 2.8 slot_places.1.places_ref
  55.6 4.6 %second_attention.1.attended_ref = f32[16,4096]{1,0:T(8,128)S(1)} custom-call(s32[1]{0:T(128)S(6)} %copy.26.lengths_ref, s32[2,1,8]{2,1,0:T(1,128)S(1)} %copy-done.12, bf16[2,1,16,4096]{3,2,1,0:T(8,128)(2,1)S(1)} %copy-done.5, bf16[1,2048,512]{2,1,0:T(8,128)(2,1)S(1)} %copy-done.1, bf16[1,2048,512]{2,1,0:T(8,128)(2,1)S(1)} %copy-done.2, ...), custom_call_target="tpu_custom_call" | custom-call | tf_op jit(solution)/shard_map/second_attention/pallas_call | solution.py:207
  62.5 8.8 %collective-permute-done.3.refs_3_ = bf16[128,4096]{1,0:T(8,128)(2,1)} collective-permute-done((bf16[128,4096]{1,0:T(8,128)(2,1)}, bf16[128,4096]{1,0:T(8,128)(2,1)}, u32[]{:S(2)}, u32[]{:S(2)}) %collective-permute-start.3) | collective-permute-done | bytes 1048608 | tf_op jit(solution)/shard_map/ppermute | solution.py:403
  78.5 2.5 keep_in_vmem.3
  81.1 3.8 %collective-permute-done.4.refs_0_ = bf16[96,32,128]{2,1,0:T(8,128)(2,1)S(1)} collective-permute-done((bf16[96,32,128]{2,1,0:T(8,128)(2,1)S(1)}, bf16[96,32,128]{2,1,0:T(8,128)(2,1)S(1)}, u32[]{:S(2)}, u32[]{:S(2)}) %collective-permute-start.4) | collective-permute-done | bytes 786464 | tf_op jit(solution)/shard_map/ppermute | solution.py:423
  84.9 2.5 expert_half.7
  89.5 3.7 %collective-permute-done.6.refs_0_ = bf16[96,32,128]{2,1,0:T(8,128)(2,1)S(1)} collective-permute-done((bf16[96,32,128]{2,1,0:T(8,128)(2,1)S(1)}, bf16[96,32,128]{2,1,0:T(8,128)(2,1)S(1)}, u32[]{:S(2)}, u32[]{:S(2)}) %collective-permute-start.6) | collective-permute-done | bytes 786464 | tf_op jit(solution)/shard_map/ppermute | solution.py:423
  97.8 3.5 %expert_half.6.terms_ref = bf16[192,32,128]{2,1,0:T(8,128)(2,1)S(1)} custom-call(bf16[192,32,128]{2,1,0:T(8,128)(2,1)S(1)} %all-to-all-done.refs_0_, bf16[4096,256]{1,0:T(8,128)(2,1)S(1)} %get-tuple-element.30.refs_1_, bf16[4096,256]{1,0:T(8,128)(2,1)S(1)} %get-tuple-element.31.refs_2_, bf16[256,4096]{1,0:T(8,128)(2,1)S(1)} %get-tuple-element.32.refs_3_, ...), custom_call_target="tpu_custom_call" | custom-call | tf_op jit(solution)/shard_map/expert_half/pallas_call | solution.py:275
  102.0 8.2 %collective-permute-done.7.away_ref = bf16[96,32,128]{2,1,0:T(8,128)(2,1)S(1)} collective-permute-done((bf16[96,32,128]{2,1,0:T(8,128)(2,1)S(1)}, bf16[96,32,128]{2,1,0:T(8,128)(2,1)S(1)}, u32[]{:S(2)}, u32[]{:S(2)}) %collective-permute-start.7) | collective-permute-done | bytes 786464 | tf_op jit(solution)/shard_map/ppermute | solution.py:424
  110.4 52.0 %all_to_all.20.terms_ref = bf16[192,32,128]{2,1,0:T(8,128)(2,1)S(1)} all-to-all(bf16[192,32,128]{2,1,0:T(8,128)(2,1)S(1)} %add_part.5), channel_id=1, replica_groups=mesh['rep'=4,'exp'=64] {'exp'}, dimensions={0} | all-to-all | bytes 3145728 | tf_op jit(solution)/shard_map/all_to_all | solution.py:428
  162.4 2.6 combine_and_dispatch.1
  165.1 45.2 %all_to_all.21.refs_0_ = bf16[192,32,128]{2,1,0:T(8,128)(2,1)S(1)} all-to-all(bf16[192,32,128]{2,1,0:T(8,128)(2,1)S(1)} %get-tuple-element.40), channel_id=1, replica_groups=mesh['rep'=4,'exp'=64] {'exp'}, dimensions={0} | all-to-all | bytes 3145728 | tf_op jit(solution)/shard_map/all_to_all | solution.py:420
  210.9 3.0 %collective-permute-start.10 = (bf16[96,32,128]{2,1,0:T(8,128)(2,1)S(1)}, bf16[96,32,128]{2,1,0:T(8,128)(2,1)S(1)}, u32[]{:S(2)}, u32[]{:S(2)}) collective-permute-start(bf16[96,32,128]{2,1,0:T(8,128)(2,1)S(1)} %get-tuple-element.45), channel_id=1, source_target_pairs={{0,192},{1,65},{2,194},{3,67},{4,196},{5,69},{6,198},{7,71},{8,200... | collective-permute-start | bytes 2359304 | tf_op jit(solution)/shard_map/ppermute | solution.py:423
  213.9 10.0 %collective-permute-done.8.refs_0_ = bf16[96,32,128]{2,1,0:T(8,128)(2,1)S(1)} collective-permute-done((bf16[96,32,128]{2,1,0:T(8,128)(2,1)S(1)}, bf16[96,32,128]{2,1,0:T(8,128)(2,1)S(1)}, u32[]{:S(2)}, u32[]{:S(2)}) %collective-permute-start.8) | collective-permute-done | bytes 786464 | tf_op jit(solution)/shard_map/ppermute | solution.py:423
  223.9 2.5 expert_half.10
  226.9 5.4 %collective-permute-done.10.refs_0_ = bf16[96,32,128]{2,1,0:T(8,128)(2,1)S(1)} collective-permute-done((bf16[96,32,128]{2,1,0:T(8,128)(2,1)S(1)}, bf16[96,32,128]{2,1,0:T(8,128)(2,1)S(1)}, u32[]{:S(2)}, u32[]{:S(2)}) %collective-permute-start.10) | collective-permute-done | bytes 786464 | tf_op jit(solution)/shard_map/ppermute | solution.py:423
  232.3 2.5 expert_half.11
  235.1 3.4 %expert_half.9.terms_ref = bf16[192,32,128]{2,1,0:T(8,128)(2,1)S(1)} custom-call(bf16[192,32,128]{2,1,0:T(8,128)(2,1)S(1)} %all_to_all.21.refs_0_, bf16[4096,256]{1,0:T(8,128)(2,1)S(1)} %get-tuple-element.30.refs_1_, bf16[4096,256]{1,0:T(8,128)(2,1)S(1)} %get-tuple-element.31.refs_2_, bf16[256,4096]{1,0:T(8,128)(2,1)S(1)} %get-tuple-element.32.refs_3_, ...), custom_call_target="tpu_custom_call" | custom-call | tf_op jit(solution)/shard_map/expert_half/pallas_call | solution.py:275
  241.0 8.2 %collective-permute-done.11.away_ref = bf16[96,32,128]{2,1,0:T(8,128)(2,1)S(1)} collective-permute-done((bf16[96,32,128]{2,1,0:T(8,128)(2,1)S(1)}, bf16[96,32,128]{2,1,0:T(8,128)(2,1)S(1)}, u32[]{:S(2)}, u32[]{:S(2)}) %collective-permute-start.11) | collective-permute-done | bytes 786464 | tf_op jit(solution)/shard_map/ppermute | solution.py:424
  249.4 45.3 %all_to_all.22.terms_ref = bf16[192,32,128]{2,1,0:T(8,128)(2,1)S(1)} all-to-all(bf16[192,32,128]{2,1,0:T(8,128)(2,1)S(1)} %add_part.7), channel_id=1, replica_groups=mesh['rep'=4,'exp'=64] {'exp'}, dimensions={0} | all-to-all | bytes 3145728 | tf_op jit(solution)/shard_map/all_to_all | solution.py:428
  (54 shorter events, 30.7 us)
Async XLA Ops:
  0.0 26.4 %collective-permute-start = (bf16[4096,256]{1,0:T(8,128)(2,1)}, bf16[4096,256]{1,0:T(8,128)(2,1)}, u32[]{:S(2)}, u32[]{:S(2)}) collective-permute-start(bf16[4096,256]{1,0:T(8,128)(2,1)} %bitcast.12), channel_id=1, source_target_pairs={{0,64},{1,193},{2,66},{3,195},{4,68},{5,197},{6,70},{7,199},{8,72}... | collective-permute-start | bytes 6291464 | tf_op jit(solution)/shard_map/ppermute | solution.py:399
  0.7 48.1 %collective-permute-start.1 = (bf16[4096,256]{1,0:T(8,128)(2,1)}, bf16[4096,256]{1,0:T(8,128)(2,1)}, u32[]{:S(2)}, u32[]{:S(2)}) collective-permute-start(bf16[4096,256]{1,0:T(8,128)(2,1)} %bitcast.14), channel_id=1, source_target_pairs={{0,64},{1,193},{2,66},{3,195},{4,68},{5,197},{6,70},{7,199},{8,72}... | collective-permute-start | bytes 6291464 | tf_op jit(solution)/shard_map/ppermute | solution.py:399
  10.4 52.2 %all-to-all-start = ((bf16[192,32,128]{2,1,0:T(8,128)(2,1)}), bf16[192,32,128]{2,1,0:T(8,128)(2,1)S(1)}, u32[]{:S(2)}, u32[]{:S(2)}) async-start(bf16[192,32,128]{2,1,0:T(8,128)(2,1)} %get-tuple-element.24), calls=%async_computation | async-start | bytes 3145728 | tf_op jit(solution)/shard_map/all_to_all | solution.py:420
  22.4 29.9 %copy-start.5 = (bf16[2,1,16,4096]{3,2,1,0:T(8,128)(2,1)S(1)}, bf16[2,1,16,4096]{3,2,1,0:T(8,128)(2,1)}, u32[]{:S(2)}) copy-start(bf16[2,1,16,4096]{3,2,1,0:T(8,128)(2,1)} %q_ref.3) | copy-start | bytes 786436
  22.4 29.9 %copy-start.8 = (bf16[2,1,16,512]{3,2,1,0:T(8,128)(2,1)S(1)}, bf16[2,1,16,512]{3,2,1,0:T(8,128)(2,1)}, u32[]{:S(2)}) copy-start(bf16[2,1,16,512]{3,2,1,0:T(8,128)(2,1)} %nk_ref.3) | copy-start | bytes 98308
  22.4 29.9 %copy-start.9 = (bf16[2,1,16,512]{3,2,1,0:T(8,128)(2,1)S(1)}, bf16[2,1,16,512]{3,2,1,0:T(8,128)(2,1)}, u32[]{:S(2)}) copy-start(bf16[2,1,16,512]{3,2,1,0:T(8,128)(2,1)} %nv_ref.3) | copy-start | bytes 98308
  22.4 29.9 %copy-start.12 = (s32[2,1,8]{2,1,0:T(1,128)S(1)}, s32[2,1,8]{2,1,0:T(1,128)}, u32[]{:S(2)}) copy-start(s32[2,1,8]{2,1,0:T(1,128)} %drift_ref.3) | copy-start | bytes 196
  26.4 36.2 %collective-permute-start.2 = (bf16[128,4096]{1,0:T(8,128)(2,1)}, bf16[128,4096]{1,0:T(8,128)(2,1)S(1)}, u32[]{:S(2)}, u32[]{:S(2)}) collective-permute-start(bf16[128,4096]{1,0:T(8,128)(2,1)} %get-tuple-element.27), channel_id=1, source_target_pairs={{0,64},{1,193},{2,66},{3,195},{4,68},{5,197},{6,70},{7,199},{8,72}... | collective-permute-start | bytes 3145736 | tf_op jit(solution)/shard_map/ppermute | solution.py:403
  48.8 22.5 %collective-permute-start.3 = (bf16[128,4096]{1,0:T(8,128)(2,1)}, bf16[128,4096]{1,0:T(8,128)(2,1)}, u32[]{:S(2)}, u32[]{:S(2)}) collective-permute-start(bf16[128,4096]{1,0:T(8,128)(2,1)} %get-tuple-element.28), channel_id=1, source_target_pairs={{0,64},{1,193},{2,66},{3,195},{4,68},{5,197},{6,70},{7,199},{8,72}... | collective-permute-start | bytes 3145736 | tf_op jit(solution)/shard_map/ppermute | solution.py:403
  52.4 1.6 copy-start.1
  55.6 4.6 %copy-start.13 = (bf16[2,1,16,8]{2,3,1,0:T(8,128)(2,1)S(1)}, bf16[2,1,16,8]{2,3,1,0:T(8,128)(2,1)}, u32[]{:S(2)}) copy-start(bf16[2,1,16,8]{2,3,1,0:T(8,128)(2,1)} %param.26) | copy-start | bytes 1540
  62.5 12.4 %copy-start = (bf16[1,256,4096]{2,1,0:T(8,128)(2,1)S(1)}, bf16[1,256,4096]{2,1,0:T(8,128)(2,1)}, u32[]{:S(2)}) copy-start(bf16[1,256,4096]{2,1,0:T(8,128)(2,1)} %param.29) | copy-start | bytes 6291460
  71.6 13.3 %collective-permute-start.4 = (bf16[96,32,128]{2,1,0:T(8,128)(2,1)S(1)}, bf16[96,32,128]{2,1,0:T(8,128)(2,1)S(1)}, u32[]{:S(2)}, u32[]{:S(2)}) collective-permute-start(bf16[96,32,128]{2,1,0:T(8,128)(2,1)S(1)} %get-tuple-element.48), channel_id=1, source_target_pairs={{0,192},{1,65},{2,194},{3,67},{4,196},{5,69},{6,198},{7,71},{8,200... | collective-permute-start | bytes 2359304 | tf_op jit(solution)/shard_map/ppermute | solution.py:423
  73.6 19.7 %collective-permute-start.6 = (bf16[96,32,128]{2,1,0:T(8,128)(2,1)S(1)}, bf16[96,32,128]{2,1,0:T(8,128)(2,1)S(1)}, u32[]{:S(2)}, u32[]{:S(2)}) collective-permute-start(bf16[96,32,128]{2,1,0:T(8,128)(2,1)S(1)} %get-tuple-element.47), channel_id=1, source_target_pairs={{0,192},{1,65},{2,194},{3,67},{4,196},{5,69},{6,198},{7,71},{8,200... | collective-permute-start | bytes 2359304 | tf_op jit(solution)/shard_map/ppermute | solution.py:423
  87.3 14.4 %collective-permute-start.5 = (bf16[96,32,128]{2,1,0:T(8,128)(2,1)S(1)}, bf16[96,32,128]{2,1,0:T(8,128)(2,1)S(1)}, u32[]{:S(2)}, u32[]{:S(2)}) collective-permute-start(bf16[96,32,128]{2,1,0:T(8,128)(2,1)S(1)} %expert_half.7), channel_id=1, source_target_pairs={{0,192},{1,65},{2,194},{3,67},{4,196},{5,69},{6,198},{7,71},{8,200... | collective-permute-start | bytes 2359304 | tf_op jit(solution)/shard_map/ppermute | solution.py:424
  95.7 14.4 %collective-permute-start.7 = (bf16[96,32,128]{2,1,0:T(8,128)(2,1)S(1)}, bf16[96,32,128]{2,1,0:T(8,128)(2,1)S(1)}, u32[]{:S(2)}, u32[]{:S(2)}) collective-permute-start(bf16[96,32,128]{2,1,0:T(8,128)(2,1)S(1)} %expert_half.8), channel_id=1, source_target_pairs={{0,192},{1,65},{2,194},{3,67},{4,196},{5,69},{6,198},{7,71},{8,200... | collective-permute-start | bytes 2359304 | tf_op jit(solution)/shard_map/ppermute | solution.py:424
  110.4 52.0 %copy-start.6 = (bf16[2,1,8,4096]{3,2,1,0:T(8,128)(2,1)S(1)}, bf16[2,1,8,4096]{3,2,1,0:T(8,128)(2,1)}, u32[]{:S(2)}) copy-start(bf16[2,1,8,4096]{3,2,1,0:T(8,128)(2,1)} %drift_in_ref.3) | copy-start | bytes 393220
  110.4 52.0 %copy-start.7 = (f32[16,4096]{1,0:T(8,128)S(1)}, f32[16,4096]{1,0:T(8,128)}, u32[]{:S(2)}) copy-start(f32[16,4096]{1,0:T(8,128)} %get-tuple-element.36.residual_ref) | copy-start | bytes 786436
  110.4 52.0 %copy-start.10 = (s32[2,1,8,16]{3,2,1,0:T(8,128)S(1)}, s32[2,1,8,16]{3,2,1,0:T(8,128)}, u32[]{:S(2)}) copy-start(s32[2,1,8,16]{3,2,1,0:T(8,128)} %slot_places.1.places_ref) | copy-start | bytes 3076
  110.4 52.0 %copy-start.11 = (f32[4096]{0:T(1024)S(1)}, f32[4096]{0:T(1024)}, u32[]{:S(2)}) copy-start(f32[4096]{0:T(1024)} %param.24) | copy-start | bytes 49156
  210.6 13.3 %collective-permute-start.8 = (bf16[96,32,128]{2,1,0:T(8,128)(2,1)S(1)}, bf16[96,32,128]{2,1,0:T(8,128)(2,1)S(1)}, u32[]{:S(2)}, u32[]{:S(2)}) collective-permute-start(bf16[96,32,128]{2,1,0:T(8,128)(2,1)S(1)} %get-tuple-element.46), channel_id=1, source_target_pairs={{0,192},{1,65},{2,194},{3,67},{4,196},{5,69},{6,198},{7,71},{8,200... | collective-permute-start | bytes 2359304 | tf_op jit(solution)/shard_map/ppermute | solution.py:423
  210.9 21.4 %collective-permute-start.10 = (bf16[96,32,128]{2,1,0:T(8,128)(2,1)S(1)}, bf16[96,32,128]{2,1,0:T(8,128)(2,1)S(1)}, u32[]{:S(2)}, u32[]{:S(2)}) collective-permute-start(bf16[96,32,128]{2,1,0:T(8,128)(2,1)S(1)} %get-tuple-element.45), channel_id=1, source_target_pairs={{0,192},{1,65},{2,194},{3,67},{4,196},{5,69},{6,198},{7,71},{8,200... | collective-permute-start | bytes 2359304 | tf_op jit(solution)/shard_map/ppermute | solution.py:423
  226.4 14.4 %collective-permute-start.9 = (bf16[96,32,128]{2,1,0:T(8,128)(2,1)S(1)}, bf16[96,32,128]{2,1,0:T(8,128)(2,1)S(1)}, u32[]{:S(2)}, u32[]{:S(2)}) collective-permute-start(bf16[96,32,128]{2,1,0:T(8,128)(2,1)S(1)} %expert_half.10), channel_id=1, source_target_pairs={{0,192},{1,65},{2,194},{3,67},{4,196},{5,69},{6,198},{7,71},{8,200... | collective-permute-start | bytes 2359304 | tf_op jit(solution)/shard_map/ppermute | solution.py:424
  234.8 14.4 %collective-permute-start.11 = (bf16[96,32,128]{2,1,0:T(8,128)(2,1)S(1)}, bf16[96,32,128]{2,1,0:T(8,128)(2,1)S(1)}, u32[]{:S(2)}, u32[]{:S(2)}) collective-permute-start(bf16[96,32,128]{2,1,0:T(8,128)(2,1)S(1)} %expert_half.11), channel_id=1, source_target_pairs={{0,192},{1,65},{2,194},{3,67},{4,196},{5,69},{6,198},{7,71},{8,200... | collective-permute-start | bytes 2359304 | tf_op jit(solution)/shard_map/ppermute | solution.py:424
  (3 other events, 4.8 us)

commit v8 on v7

--- a/solution.py
+++ b/solution.py
@@ -63,8 +63,7 @@
 
 
 def each_place(places_ref, denoise, visit):
-    @pl.loop(0, ROWS, unroll=4)
-    def _(t):
+    for t in range(ROWS):
         visit(t, [places_ref[denoise, 0, j, t] for j in range(TOP)])
 
 
@@ -89,10 +88,13 @@
 
 def combine(terms_ref, places_ref, gates_ref, denoise, spread):
     def visit(t, picked):
-        total = jnp.zeros((H, HD), jnp.float32)
-        for j, slot in enumerate(picked):
-            total = total + gates_ref[denoise, 0, j, t] * terms_ref[slot].astype(jnp.float32)
-        spread[pl.ds(pl.multiple_of(t * H, H), H), :] = total
+        shares = [
+            gates_ref[denoise, 0, j, t] * terms_ref[slot].astype(jnp.float32)
+            for j, slot in enumerate(picked)
+        ]
+        while len(shares) > 1:
+            shares = [a + b for a, b in zip(shares[::2], shares[1::2])]
+        spread[t * H : (t + 1) * H, :] = shares[0]
 
     each_place(places_ref, denoise, visit)
     return jnp.concatenate([spread[pl.ds(k, ROWS, stride=H), :] for k in range(H)], axis=1)

time: 297 us -> 297 us (level)
  no operation moved by 1% of the time
where the time goes in v8:
time: 297 us; the launch traced here: 296 us
  blocking collectives  142 us (48%)
  waiting for transfers between devices  75.7 us (25%)
  Pallas kernels  39.9 us (13%)
  starting transfers between devices  27.1 us (9%)
  local copies, waits for them, and re-layouts  10.1 us (3%)
    all_to_all x2, blocking collectives, experts(): lax.all_to_all(terms, 'exp', split_axis=0, concat_axis=0, tiled=True)  97.3 us
    all_to_all x1, blocking collectives, experts(): rows = lax.all_to_all(send, 'exp', split_axis=0, concat_axis=0, tiled=True)  45.2 us
    ppermute x4, waiting for transfers between devices, experts(): lax.ppermute(rows[i * size:(i + 1) * size], axes, across)  23.1 us
    ppermute x2, waiting for transfers between devices, on_device(): gate_up = [lax.ppermute(part, axes, beside) for part in own[:2]]  22.4 us
    ppermute x4, waiting for transfers between devices, experts(): lax.ppermute(expert_half(part, weights), axes, across)  19 us
    pallas_call x6, Pallas kernels, expert_half(): pl.pallas_call(body, in_specs=[vmem] * (1 + 3 * pieces), out_specs=vmem,...  16.7 us
    all_to_all x1, starting transfers between devices, experts(): rows = lax.all_to_all(send, 'exp', split_axis=0, concat_axis=0, tiled=True)  12 us
    ppermute x2, waiting for transfers between devices, on_device(): downs.append(lax.ppermute(half, axes, beside))  8.77 us
  transfers between devices with their start and end apart: 13, of which 12 were waited for; matrix products, arithmetic and copies ran while one was open for 1% of the time, Pallas kernels for 12%

profile of v8, /device:TPU:24, one launch (start us, length us, event | category | flops | bytes accessed | tf_op | source)
XLA Modules:
  0.0 296.2 jit_solution(5997834164764739318)
XLA Ops:
  2.7 7.7 %first_attention.1 = (f32[16,4096]{1,0:T(8,128)}, bf16[192,32,128]{2,1,0:T(8,128)(2,1)}) custom-call(s32[1]{0:T(128)S(6)} %copy.26.lengths_ref, s32[2,1,8]{2,1,0:T(1,128)} %drift_ref.3, bf16[2,1,16,4096]{3,2,1,0:T(8,128)(2,1)} %q_ref.3, bf16[1,2048,512]{2,1,0:T(8,128)(2,1)} %k_ref.3, bf16[1,2048,512]{2,1,0:T(8,128)(2,1)} %v_ref.3, ...), custom_call_target="tpu_custom_call" | custom-call | tf_op jit(solution)/shard_map/first_attention/pallas_call | solution.py:175
  10.4 12.0 %all-to-all-start = ((bf16[192,32,128]{2,1,0:T(8,128)(2,1)}), bf16[192,32,128]{2,1,0:T(8,128)(2,1)S(1)}, u32[]{:S(2)}, u32[]{:S(2)}) async-start(bf16[192,32,128]{2,1,0:T(8,128)(2,1)} %get-tuple-element.24), calls=%async_computation | async-start | bytes 3145728 | tf_op jit(solution)/shard_map/all_to_all | solution.py:422
  22.4 3.2 %slice_bitcast_fusion = (bf16[128,4096]{1,0:T(8,128)(2,1)}, bf16[128,4096]{1,0:T(8,128)(2,1)}) fusion(bf16[1,256,4096]{2,1,0:T(8,128)(2,1)} %param.29), kind=kLoop, calls=%fused_computation | loop fusion | bytes 4194304 | tf_op jit(solution)/shard_map/split | solution.py:403
  27.1 21.7 %collective-permute-done.1.refs_1_ = bf16[4096,256]{1,0:T(8,128)(2,1)} collective-permute-done((bf16[4096,256]{1,0:T(8,128)(2,1)}, bf16[4096,256]{1,0:T(8,128)(2,1)}, u32[]{:S(2)}, u32[]{:S(2)}) %collective-permute-start.1) | collective-permute-done | bytes 2097184 | tf_op jit(solution)/shard_map/ppermute | solution.py:401
  49.6 2.8 slot_places.1.places_ref
  55.6 4.6 %second_attention.1.attended_ref = f32[16,4096]{1,0:T(8,128)S(1)} custom-call(s32[1]{0:T(128)S(6)} %copy.26.lengths_ref, s32[2,1,8]{2,1,0:T(1,128)S(1)} %copy-done.12, bf16[2,1,16,4096]{3,2,1,0:T(8,128)(2,1)S(1)} %copy-done.5, bf16[1,2048,512]{2,1,0:T(8,128)(2,1)S(1)} %copy-done.1, bf16[1,2048,512]{2,1,0:T(8,128)(2,1)S(1)} %copy-done.2, ...), custom_call_target="tpu_custom_call" | custom-call | tf_op jit(solution)/shard_map/second_attention/pallas_call | solution.py:209
  62.5 8.8 %collective-permute-done.3.refs_3_ = bf16[128,4096]{1,0:T(8,128)(2,1)} collective-permute-done((bf16[128,4096]{1,0:T(8,128)(2,1)}, bf16[128,4096]{1,0:T(8,128)(2,1)}, u32[]{:S(2)}, u32[]{:S(2)}) %collective-permute-start.3) | collective-permute-done | bytes 1048608 | tf_op jit(solution)/shard_map/ppermute | solution.py:405
  78.5 2.5 keep_in_vmem.3
  81.1 3.8 %collective-permute-done.4.refs_0_ = bf16[96,32,128]{2,1,0:T(8,128)(2,1)S(1)} collective-permute-done((bf16[96,32,128]{2,1,0:T(8,128)(2,1)S(1)}, bf16[96,32,128]{2,1,0:T(8,128)(2,1)S(1)}, u32[]{:S(2)}, u32[]{:S(2)}) %collective-permute-start.4) | collective-permute-done | bytes 786464 | tf_op jit(solution)/shard_map/ppermute | solution.py:425
  84.9 2.5 expert_half.7
  89.5 3.7 %collective-permute-done.6.refs_0_ = bf16[96,32,128]{2,1,0:T(8,128)(2,1)S(1)} collective-permute-done((bf16[96,32,128]{2,1,0:T(8,128)(2,1)S(1)}, bf16[96,32,128]{2,1,0:T(8,128)(2,1)S(1)}, u32[]{:S(2)}, u32[]{:S(2)}) %collective-permute-start.6) | collective-permute-done | bytes 786464 | tf_op jit(solution)/shard_map/ppermute | solution.py:425
  93.3 2.5 expert_half.8
  97.8 3.5 %expert_half.6.terms_ref = bf16[192,32,128]{2,1,0:T(8,128)(2,1)S(1)} custom-call(bf16[192,32,128]{2,1,0:T(8,128)(2,1)S(1)} %all-to-all-done.refs_0_, bf16[4096,256]{1,0:T(8,128)(2,1)S(1)} %get-tuple-element.30.refs_1_, bf16[4096,256]{1,0:T(8,128)(2,1)S(1)} %get-tuple-element.31.refs_2_, bf16[256,4096]{1,0:T(8,128)(2,1)S(1)} %get-tuple-element.32.refs_3_, ...), custom_call_target="tpu_custom_call" | custom-call | tf_op jit(solution)/shard_map/expert_half/pallas_call | solution.py:277
  102.0 8.2 %collective-permute-done.7.away_ref = bf16[96,32,128]{2,1,0:T(8,128)(2,1)S(1)} collective-permute-done((bf16[96,32,128]{2,1,0:T(8,128)(2,1)S(1)}, bf16[96,32,128]{2,1,0:T(8,128)(2,1)S(1)}, u32[]{:S(2)}, u32[]{:S(2)}) %collective-permute-start.7) | collective-permute-done | bytes 786464 | tf_op jit(solution)/shard_map/ppermute | solution.py:426
  110.4 52.0 %all_to_all.20.terms_ref = bf16[192,32,128]{2,1,0:T(8,128)(2,1)S(1)} all-to-all(bf16[192,32,128]{2,1,0:T(8,128)(2,1)S(1)} %add_part.5), channel_id=1, replica_groups=mesh['rep'=4,'exp'=64] {'exp'}, dimensions={0} | all-to-all | bytes 3145728 | tf_op jit(solution)/shard_map/all_to_all | solution.py:430
  164.8 45.2 %all_to_all.21.refs_0_ = bf16[192,32,128]{2,1,0:T(8,128)(2,1)S(1)} all-to-all(bf16[192,32,128]{2,1,0:T(8,128)(2,1)S(1)} %get-tuple-element.40), channel_id=1, replica_groups=mesh['rep'=4,'exp'=64] {'exp'}, dimensions={0} | all-to-all | bytes 3145728 | tf_op jit(solution)/shard_map/all_to_all | solution.py:422
  210.6 3.0 %collective-permute-start.10 = (bf16[96,32,128]{2,1,0:T(8,128)(2,1)S(1)}, bf16[96,32,128]{2,1,0:T(8,128)(2,1)S(1)}, u32[]{:S(2)}, u32[]{:S(2)}) collective-permute-start(bf16[96,32,128]{2,1,0:T(8,128)(2,1)S(1)} %get-tuple-element.45), channel_id=1, source_target_pairs={{0,192},{1,65},{2,194},{3,67},{4,196},{5,69},{6,198},{7,71},{8,200... | collective-permute-start | bytes 2359304 | tf_op jit(solution)/shard_map/ppermute | solution.py:425
  213.6 10.0 %collective-permute-done.8.refs_0_ = bf16[96,32,128]{2,1,0:T(8,128)(2,1)S(1)} collective-permute-done((bf16[96,32,128]{2,1,0:T(8,128)(2,1)S(1)}, bf16[96,32,128]{2,1,0:T(8,128)(2,1)S(1)}, u32[]{:S(2)}, u32[]{:S(2)}) %collective-permute-start.8) | collective-permute-done | bytes 786464 | tf_op jit(solution)/shard_map/ppermute | solution.py:425
  223.6 2.5 expert_half.10
  226.4 5.6 %collective-permute-done.10.refs_0_ = bf16[96,32,128]{2,1,0:T(8,128)(2,1)S(1)} collective-permute-done((bf16[96,32,128]{2,1,0:T(8,128)(2,1)S(1)}, bf16[96,32,128]{2,1,0:T(8,128)(2,1)S(1)}, u32[]{:S(2)}, u32[]{:S(2)}) %collective-permute-start.10) | collective-permute-done | bytes 786464 | tf_op jit(solution)/shard_map/ppermute | solution.py:425
  232.0 2.5 expert_half.11
  234.8 3.4 %expert_half.9.terms_ref = bf16[192,32,128]{2,1,0:T(8,128)(2,1)S(1)} custom-call(bf16[192,32,128]{2,1,0:T(8,128)(2,1)S(1)} %all_to_all.21.refs_0_, bf16[4096,256]{1,0:T(8,128)(2,1)S(1)} %get-tuple-element.30.refs_1_, bf16[4096,256]{1,0:T(8,128)(2,1)S(1)} %get-tuple-element.31.refs_2_, bf16[256,4096]{1,0:T(8,128)(2,1)S(1)} %get-tuple-element.32.refs_3_, ...), custom_call_target="tpu_custom_call" | custom-call | tf_op jit(solution)/shard_map/expert_half/pallas_call | solution.py:277
  240.7 8.2 %collective-permute-done.11.away_ref = bf16[96,32,128]{2,1,0:T(8,128)(2,1)S(1)} collective-permute-done((bf16[96,32,128]{2,1,0:T(8,128)(2,1)S(1)}, bf16[96,32,128]{2,1,0:T(8,128)(2,1)S(1)}, u32[]{:S(2)}, u32[]{:S(2)}) %collective-permute-start.11) | collective-permute-done | bytes 786464 | tf_op jit(solution)/shard_map/ppermute | solution.py:426
  249.1 45.3 %all_to_all.22.terms_ref = bf16[192,32,128]{2,1,0:T(8,128)(2,1)S(1)} all-to-all(bf16[192,32,128]{2,1,0:T(8,128)(2,1)S(1)} %add_part.7), channel_id=1, replica_groups=mesh['rep'=4,'exp'=64] {'exp'}, dimensions={0} | all-to-all | bytes 3145728 | tf_op jit(solution)/shard_map/all_to_all | solution.py:430
  (54 shorter events, 30.3 us)
Async XLA Ops:
  0.0 26.4 %collective-permute-start = (bf16[4096,256]{1,0:T(8,128)(2,1)}, bf16[4096,256]{1,0:T(8,128)(2,1)}, u32[]{:S(2)}, u32[]{:S(2)}) collective-permute-start(bf16[4096,256]{1,0:T(8,128)(2,1)} %bitcast.12), channel_id=1, source_target_pairs={{0,64},{1,193},{2,66},{3,195},{4,68},{5,197},{6,70},{7,199},{8,72}... | collective-permute-start | bytes 6291464 | tf_op jit(solution)/shard_map/ppermute | solution.py:401
  0.7 48.1 %collective-permute-start.1 = (bf16[4096,256]{1,0:T(8,128)(2,1)}, bf16[4096,256]{1,0:T(8,128)(2,1)}, u32[]{:S(2)}, u32[]{:S(2)}) collective-permute-start(bf16[4096,256]{1,0:T(8,128)(2,1)} %bitcast.14), channel_id=1, source_target_pairs={{0,64},{1,193},{2,66},{3,195},{4,68},{5,197},{6,70},{7,199},{8,72}... | collective-permute-start | bytes 6291464 | tf_op jit(solution)/shard_map/ppermute | solution.py:401
  10.4 52.2 %all-to-all-start = ((bf16[192,32,128]{2,1,0:T(8,128)(2,1)}), bf16[192,32,128]{2,1,0:T(8,128)(2,1)S(1)}, u32[]{:S(2)}, u32[]{:S(2)}) async-start(bf16[192,32,128]{2,1,0:T(8,128)(2,1)} %get-tuple-element.24), calls=%async_computation | async-start | bytes 3145728 | tf_op jit(solution)/shard_map/all_to_all | solution.py:422
  22.4 29.9 %copy-start.5 = (bf16[2,1,16,4096]{3,2,1,0:T(8,128)(2,1)S(1)}, bf16[2,1,16,4096]{3,2,1,0:T(8,128)(2,1)}, u32[]{:S(2)}) copy-start(bf16[2,1,16,4096]{3,2,1,0:T(8,128)(2,1)} %q_ref.3) | copy-start | bytes 786436
  22.4 29.9 %copy-start.8 = (bf16[2,1,16,512]{3,2,1,0:T(8,128)(2,1)S(1)}, bf16[2,1,16,512]{3,2,1,0:T(8,128)(2,1)}, u32[]{:S(2)}) copy-start(bf16[2,1,16,512]{3,2,1,0:T(8,128)(2,1)} %nk_ref.3) | copy-start | bytes 98308
  22.4 29.9 %copy-start.9 = (bf16[2,1,16,512]{3,2,1,0:T(8,128)(2,1)S(1)}, bf16[2,1,16,512]{3,2,1,0:T(8,128)(2,1)}, u32[]{:S(2)}) copy-start(bf16[2,1,16,512]{3,2,1,0:T(8,128)(2,1)} %nv_ref.3) | copy-start | bytes 98308
  22.4 29.9 %copy-start.12 = (s32[2,1,8]{2,1,0:T(1,128)S(1)}, s32[2,1,8]{2,1,0:T(1,128)}, u32[]{:S(2)}) copy-start(s32[2,1,8]{2,1,0:T(1,128)} %drift_ref.3) | copy-start | bytes 196
  26.4 36.2 %collective-permute-start.2 = (bf16[128,4096]{1,0:T(8,128)(2,1)}, bf16[128,4096]{1,0:T(8,128)(2,1)S(1)}, u32[]{:S(2)}, u32[]{:S(2)}) collective-permute-start(bf16[128,4096]{1,0:T(8,128)(2,1)} %get-tuple-element.27), channel_id=1, source_target_pairs={{0,64},{1,193},{2,66},{3,195},{4,68},{5,197},{6,70},{7,199},{8,72}... | collective-permute-start | bytes 3145736 | tf_op jit(solution)/shard_map/ppermute | solution.py:405
  48.8 22.5 %collective-permute-start.3 = (bf16[128,4096]{1,0:T(8,128)(2,1)}, bf16[128,4096]{1,0:T(8,128)(2,1)}, u32[]{:S(2)}, u32[]{:S(2)}) collective-permute-start(bf16[128,4096]{1,0:T(8,128)(2,1)} %get-tuple-element.28), channel_id=1, source_target_pairs={{0,64},{1,193},{2,66},{3,195},{4,68},{5,197},{6,70},{7,199},{8,72}... | collective-permute-start | bytes 3145736 | tf_op jit(solution)/shard_map/ppermute | solution.py:405
  52.4 1.6 copy-start.1
  55.6 4.6 %copy-start.13 = (bf16[2,1,16,8]{2,3,1,0:T(8,128)(2,1)S(1)}, bf16[2,1,16,8]{2,3,1,0:T(8,128)(2,1)}, u32[]{:S(2)}) copy-start(bf16[2,1,16,8]{2,3,1,0:T(8,128)(2,1)} %param.26) | copy-start | bytes 1540
  62.5 12.4 %copy-start = (bf16[1,256,4096]{2,1,0:T(8,128)(2,1)S(1)}, bf16[1,256,4096]{2,1,0:T(8,128)(2,1)}, u32[]{:S(2)}) copy-start(bf16[1,256,4096]{2,1,0:T(8,128)(2,1)} %param.29) | copy-start | bytes 6291460
  71.6 13.3 %collective-permute-start.4 = (bf16[96,32,128]{2,1,0:T(8,128)(2,1)S(1)}, bf16[96,32,128]{2,1,0:T(8,128)(2,1)S(1)}, u32[]{:S(2)}, u32[]{:S(2)}) collective-permute-start(bf16[96,32,128]{2,1,0:T(8,128)(2,1)S(1)} %get-tuple-element.48), channel_id=1, source_target_pairs={{0,192},{1,65},{2,194},{3,67},{4,196},{5,69},{6,198},{7,71},{8,200... | collective-permute-start | bytes 2359304 | tf_op jit(solution)/shard_map/ppermute | solution.py:425
  73.6 19.7 %collective-permute-start.6 = (bf16[96,32,128]{2,1,0:T(8,128)(2,1)S(1)}, bf16[96,32,128]{2,1,0:T(8,128)(2,1)S(1)}, u32[]{:S(2)}, u32[]{:S(2)}) collective-permute-start(bf16[96,32,128]{2,1,0:T(8,128)(2,1)S(1)} %get-tuple-element.47), channel_id=1, source_target_pairs={{0,192},{1,65},{2,194},{3,67},{4,196},{5,69},{6,198},{7,71},{8,200... | collective-permute-start | bytes 2359304 | tf_op jit(solution)/shard_map/ppermute | solution.py:425
  87.3 14.4 %collective-permute-start.5 = (bf16[96,32,128]{2,1,0:T(8,128)(2,1)S(1)}, bf16[96,32,128]{2,1,0:T(8,128)(2,1)S(1)}, u32[]{:S(2)}, u32[]{:S(2)}) collective-permute-start(bf16[96,32,128]{2,1,0:T(8,128)(2,1)S(1)} %expert_half.7), channel_id=1, source_target_pairs={{0,192},{1,65},{2,194},{3,67},{4,196},{5,69},{6,198},{7,71},{8,200... | collective-permute-start | bytes 2359304 | tf_op jit(solution)/shard_map/ppermute | solution.py:426
  95.7 14.4 %collective-permute-start.7 = (bf16[96,32,128]{2,1,0:T(8,128)(2,1)S(1)}, bf16[96,32,128]{2,1,0:T(8,128)(2,1)S(1)}, u32[]{:S(2)}, u32[]{:S(2)}) collective-permute-start(bf16[96,32,128]{2,1,0:T(8,128)(2,1)S(1)} %expert_half.8), channel_id=1, source_target_pairs={{0,192},{1,65},{2,194},{3,67},{4,196},{5,69},{6,198},{7,71},{8,200... | collective-permute-start | bytes 2359304 | tf_op jit(solution)/shard_map/ppermute | solution.py:426
  110.4 52.0 %copy-start.6 = (bf16[2,1,8,4096]{3,2,1,0:T(8,128)(2,1)S(1)}, bf16[2,1,8,4096]{3,2,1,0:T(8,128)(2,1)}, u32[]{:S(2)}) copy-start(bf16[2,1,8,4096]{3,2,1,0:T(8,128)(2,1)} %drift_in_ref.3) | copy-start | bytes 393220
  110.4 52.0 %copy-start.7 = (f32[16,4096]{1,0:T(8,128)S(1)}, f32[16,4096]{1,0:T(8,128)}, u32[]{:S(2)}) copy-start(f32[16,4096]{1,0:T(8,128)} %get-tuple-element.36.residual_ref) | copy-start | bytes 786436
  110.4 52.0 %copy-start.10 = (s32[2,1,8,16]{3,2,1,0:T(8,128)S(1)}, s32[2,1,8,16]{3,2,1,0:T(8,128)}, u32[]{:S(2)}) copy-start(s32[2,1,8,16]{3,2,1,0:T(8,128)} %slot_places.1.places_ref) | copy-start | bytes 3076
  110.4 52.0 %copy-start.11 = (f32[4096]{0:T(1024)S(1)}, f32[4096]{0:T(1024)}, u32[]{:S(2)}) copy-start(f32[4096]{0:T(1024)} %param.24) | copy-start | bytes 49156
  210.3 13.3 %collective-permute-start.8 = (bf16[96,32,128]{2,1,0:T(8,128)(2,1)S(1)}, bf16[96,32,128]{2,1,0:T(8,128)(2,1)S(1)}, u32[]{:S(2)}, u32[]{:S(2)}) collective-permute-start(bf16[96,32,128]{2,1,0:T(8,128)(2,1)S(1)} %get-tuple-element.46), channel_id=1, source_target_pairs={{0,192},{1,65},{2,194},{3,67},{4,196},{5,69},{6,198},{7,71},{8,200... | collective-permute-start | bytes 2359304 | tf_op jit(solution)/shard_map/ppermute | solution.py:425
  210.6 21.4 %collective-permute-start.10 = (bf16[96,32,128]{2,1,0:T(8,128)(2,1)S(1)}, bf16[96,32,128]{2,1,0:T(8,128)(2,1)S(1)}, u32[]{:S(2)}, u32[]{:S(2)}) collective-permute-start(bf16[96,32,128]{2,1,0:T(8,128)(2,1)S(1)} %get-tuple-element.45), channel_id=1, source_target_pairs={{0,192},{1,65},{2,194},{3,67},{4,196},{5,69},{6,198},{7,71},{8,200... | collective-permute-start | bytes 2359304 | tf_op jit(solution)/shard_map/ppermute | solution.py:425
  226.1 14.4 %collective-permute-start.9 = (bf16[96,32,128]{2,1,0:T(8,128)(2,1)S(1)}, bf16[96,32,128]{2,1,0:T(8,128)(2,1)S(1)}, u32[]{:S(2)}, u32[]{:S(2)}) collective-permute-start(bf16[96,32,128]{2,1,0:T(8,128)(2,1)S(1)} %expert_half.10), channel_id=1, source_target_pairs={{0,192},{1,65},{2,194},{3,67},{4,196},{5,69},{6,198},{7,71},{8,200... | collective-permute-start | bytes 2359304 | tf_op jit(solution)/shard_map/ppermute | solution.py:426
  234.5 14.4 %collective-permute-start.11 = (bf16[96,32,128]{2,1,0:T(8,128)(2,1)S(1)}, bf16[96,32,128]{2,1,0:T(8,128)(2,1)S(1)}, u32[]{:S(2)}, u32[]{:S(2)}) collective-permute-start(bf16[96,32,128]{2,1,0:T(8,128)(2,1)S(1)} %expert_half.11), channel_id=1, source_target_pairs={{0,192},{1,65},{2,194},{3,67},{4,196},{5,69},{6,198},{7,71},{8,200... | collective-permute-start | bytes 2359304 | tf_op jit(solution)/shard_map/ppermute | solution.py:426
  (3 other events, 4.8 us)

commit v9 on v8

--- a/solution.py
+++ b/solution.py
@@ -18,7 +18,7 @@
 SLOTS = EXPERTS * CAP
 CACHE = 2048
 QUARTER = 256
-VISITS = 2
+VISITS = 3
 NEG = -1e30
 VMEM_LIMIT = 24 * 1024 * 1024
 

time: 297 us -> 297 us (level)
  waiting for transfers between devices: 75.7 us -> 66.3 us
  Pallas kernels: 39.9 us -> 45.1 us
  starting transfers between devices: 27.1 us -> 31 us
    ppermute x4 -> x6, waiting for transfers between devices: 23.1 us -> 14.1 us  [experts(): lax.ppermute(rows[i * size:(i + 1) * size], axes, across)]
    pallas_call x6 -> x8, Pallas kernels: 16.7 us -> 21.8 us  [expert_half(): pl.pallas_call(body, in_specs=[vmem] * (1 + 3 * pieces), out_specs=vmem,...]
    ppermute x4 -> x6, starting transfers between devices: 6.65 us -> 8.92 us  [experts(): lax.ppermute(rows[i * size:(i + 1) * size], axes, across)]
    ppermute x4 -> x6, starting transfers between devices: 4.89 us -> 6.56 us  [experts(): lax.ppermute(expert_half(part, weights), axes, across)]
    ppermute x4 -> x6, waiting for transfers between devices: 19 us -> 18.7 us  [experts(): lax.ppermute(expert_half(part, weights), axes, across)]
  transfers between devices with their start and end apart: 13 -> 17, of which waited for: 12 -> 13; matrix products, arithmetic and copies ran while one was open for 1% -> 1% of each run, Pallas kernels for 12% -> 14%
where the time goes in v9:
time: 297 us; the launch traced here: 296 us
  blocking collectives  142 us (48%)
  waiting for transfers between devices  66.3 us (22%)
  Pallas kernels  45.1 us (15%)
  starting transfers between devices  31 us (10%)
  local copies, waits for them, and re-layouts  10.3 us (3%)
    all_to_all x2, blocking collectives, experts(): lax.all_to_all(terms, 'exp', split_axis=0, concat_axis=0, tiled=True)  97.3 us
    all_to_all x1, blocking collectives, experts(): rows = lax.all_to_all(send, 'exp', split_axis=0, concat_axis=0, tiled=True)  45.2 us
    ppermute x2, waiting for transfers between devices, on_device(): gate_up = [lax.ppermute(part, axes, beside) for part in own[:2]]  22.4 us
    pallas_call x8, Pallas kernels, expert_half(): pl.pallas_call(body, in_specs=[vmem] * (1 + 3 * pieces), out_specs=vmem,...  21.8 us
    ppermute x6, waiting for transfers between devices, experts(): lax.ppermute(expert_half(part, weights), axes, across)  18.7 us
    ppermute x6, waiting for transfers between devices, experts(): lax.ppermute(rows[i * size:(i + 1) * size], axes, across)  14.1 us
    all_to_all x1, starting transfers between devices, experts(): rows = lax.all_to_all(send, 'exp', split_axis=0, concat_axis=0, tiled=True)  12 us
    ppermute x6, starting transfers between devices, experts(): lax.ppermute(rows[i * size:(i + 1) * size], axes, across)  8.92 us
  transfers between devices with their start and end apart: 17, of which 13 were waited for; matrix products, arithmetic and copies ran while one was open for 1% of the time, Pallas kernels for 14%

profile of v9, /device:TPU:24, one launch (start us, length us, event | category | flops | bytes accessed | tf_op | source)
XLA Modules:
  0.0 296.2 jit_solution(10013616179939446368)
XLA Ops:
  2.7 7.7 %first_attention.1 = (f32[16,4096]{1,0:T(8,128)}, bf16[192,32,128]{2,1,0:T(8,128)(2,1)}) custom-call(s32[1]{0:T(128)S(6)} %copy.30.lengths_ref, s32[2,1,8]{2,1,0:T(1,128)} %drift_ref.3, bf16[2,1,16,4096]{3,2,1,0:T(8,128)(2,1)} %q_ref.3, bf16[1,2048,512]{2,1,0:T(8,128)(2,1)} %k_ref.3, bf16[1,2048,512]{2,1,0:T(8,128)(2,1)} %v_ref.3, ...), custom_call_target="tpu_custom_call" | custom-call | tf_op jit(solution)/shard_map/first_attention/pallas_call | solution.py:175
  10.4 12.0 %all-to-all-start = ((bf16[192,32,128]{2,1,0:T(8,128)(2,1)}), bf16[192,32,128]{2,1,0:T(8,128)(2,1)S(1)}, u32[]{:S(2)}, u32[]{:S(2)}) async-start(bf16[192,32,128]{2,1,0:T(8,128)(2,1)} %get-tuple-element.24), calls=%async_computation | async-start | bytes 3145728 | tf_op jit(solution)/shard_map/all_to_all | solution.py:422
  22.4 3.2 %slice_bitcast_fusion = (bf16[128,4096]{1,0:T(8,128)(2,1)}, bf16[128,4096]{1,0:T(8,128)(2,1)}) fusion(bf16[1,256,4096]{2,1,0:T(8,128)(2,1)} %param.29), kind=kLoop, calls=%fused_computation | loop fusion | bytes 4194304 | tf_op jit(solution)/shard_map/split | solution.py:403
  27.1 21.7 %collective-permute-done.1.refs_1_ = bf16[4096,256]{1,0:T(8,128)(2,1)} collective-permute-done((bf16[4096,256]{1,0:T(8,128)(2,1)}, bf16[4096,256]{1,0:T(8,128)(2,1)}, u32[]{:S(2)}, u32[]{:S(2)}) %collective-permute-start.1) | collective-permute-done | bytes 2097184 | tf_op jit(solution)/shard_map/ppermute | solution.py:401
  49.6 2.8 slot_places.1.places_ref
  55.6 4.6 %second_attention.1.attended_ref = f32[16,4096]{1,0:T(8,128)S(1)} custom-call(s32[1]{0:T(128)S(6)} %copy.30.lengths_ref, s32[2,1,8]{2,1,0:T(1,128)S(1)} %copy-done.12, bf16[2,1,16,4096]{3,2,1,0:T(8,128)(2,1)S(1)} %copy-done.5, bf16[1,2048,512]{2,1,0:T(8,128)(2,1)S(1)} %copy-done.1, bf16[1,2048,512]{2,1,0:T(8,128)(2,1)S(1)} %copy-done.2, ...), custom_call_target="tpu_custom_call" | custom-call | tf_op jit(solution)/shard_map/second_attention/pallas_call | solution.py:209
  62.5 8.8 %collective-permute-done.3.refs_3_ = bf16[128,4096]{1,0:T(8,128)(2,1)} collective-permute-done((bf16[128,4096]{1,0:T(8,128)(2,1)}, bf16[128,4096]{1,0:T(8,128)(2,1)}, u32[]{:S(2)}, u32[]{:S(2)}) %collective-permute-start.3) | collective-permute-done | bytes 1048608 | tf_op jit(solution)/shard_map/ppermute | solution.py:405
  80.6 2.5 keep_in_vmem.3
  87.7 2.5 expert_half.10
  97.9 3.5 %expert_half.8.terms_ref = bf16[192,32,128]{2,1,0:T(8,128)(2,1)S(1)} custom-call(bf16[192,32,128]{2,1,0:T(8,128)(2,1)S(1)} %all-to-all-done.refs_0_, bf16[4096,256]{1,0:T(8,128)(2,1)S(1)} %get-tuple-element.30.refs_1_, bf16[4096,256]{1,0:T(8,128)(2,1)S(1)} %get-tuple-element.31.refs_2_, bf16[256,4096]{1,0:T(8,128)(2,1)S(1)} %get-tuple-element.32.refs_3_, ...), custom_call_target="tpu_custom_call" | custom-call | tf_op jit(solution)/shard_map/expert_half/pallas_call | solution.py:277
  101.6 3.0 %collective-permute-done.7.away_ref = bf16[64,32,128]{2,1,0:T(8,128)(2,1)S(1)} collective-permute-done((bf16[64,32,128]{2,1,0:T(8,128)(2,1)S(1)}, bf16[64,32,128]{2,1,0:T(8,128)(2,1)S(1)}, u32[]{:S(2)}, u32[]{:S(2)}) %collective-permute-start.7) | collective-permute-done | bytes 524320 | tf_op jit(solution)/shard_map/ppermute | solution.py:426
  104.8 5.4 %collective-permute-done.9.away_ref = bf16[64,32,128]{2,1,0:T(8,128)(2,1)S(1)} collective-permute-done((bf16[64,32,128]{2,1,0:T(8,128)(2,1)S(1)}, bf16[64,32,128]{2,1,0:T(8,128)(2,1)S(1)}, u32[]{:S(2)}, u32[]{:S(2)}) %collective-permute-start.9) | collective-permute-done | bytes 524320 | tf_op jit(solution)/shard_map/ppermute | solution.py:426
  110.4 52.0 %all_to_all.20.terms_ref = bf16[192,32,128]{2,1,0:T(8,128)(2,1)S(1)} all-to-all(bf16[192,32,128]{2,1,0:T(8,128)(2,1)S(1)} %add_part.8), channel_id=1, replica_groups=mesh['rep'=4,'exp'=64] {'exp'}, dimensions={0} | all-to-all | bytes 3145728 | tf_op jit(solution)/shard_map/all_to_all | solution.py:430
  164.8 45.2 %all_to_all.21.refs_0_ = bf16[192,32,128]{2,1,0:T(8,128)(2,1)S(1)} all-to-all(bf16[192,32,128]{2,1,0:T(8,128)(2,1)S(1)} %get-tuple-element.40), channel_id=1, replica_groups=mesh['rep'=4,'exp'=64] {'exp'}, dimensions={0} | all-to-all | bytes 3145728 | tf_op jit(solution)/shard_map/all_to_all | solution.py:422
  210.7 3.0 %collective-permute-start.12 = (bf16[64,32,128]{2,1,0:T(8,128)(2,1)S(1)}, bf16[64,32,128]{2,1,0:T(8,128)(2,1)S(1)}, u32[]{:S(2)}, u32[]{:S(2)}) collective-permute-start(bf16[64,32,128]{2,1,0:T(8,128)(2,1)S(1)} %get-tuple-element.46), channel_id=1, source_target_pairs={{0,192},{1,65},{2,194},{3,67},{4,196},{5,69},{6,198},{7,71},{8,200... | collective-permute-start | bytes 1572872 | tf_op jit(solution)/shard_map/ppermute | solution.py:425
  214.0 6.8 %collective-permute-done.10.refs_0_ = bf16[64,32,128]{2,1,0:T(8,128)(2,1)S(1)} collective-permute-done((bf16[64,32,128]{2,1,0:T(8,128)(2,1)S(1)}, bf16[64,32,128]{2,1,0:T(8,128)(2,1)S(1)}, u32[]{:S(2)}, u32[]{:S(2)}) %collective-permute-start.10) | collective-permute-done | bytes 524320 | tf_op jit(solution)/shard_map/ppermute | solution.py:425
  220.8 2.5 expert_half.13
  223.6 2.8 collective-permute-done.12.refs_0_
  226.5 2.5 expert_half.14
  229.3 2.8 collective-permute-done.14.refs_0_
  234.9 3.4 %expert_half.12.terms_ref = bf16[192,32,128]{2,1,0:T(8,128)(2,1)S(1)} custom-call(bf16[192,32,128]{2,1,0:T(8,128)(2,1)S(1)} %all_to_all.21.refs_0_, bf16[4096,256]{1,0:T(8,128)(2,1)S(1)} %get-tuple-element.30.refs_1_, bf16[4096,256]{1,0:T(8,128)(2,1)S(1)} %get-tuple-element.31.refs_2_, bf16[256,4096]{1,0:T(8,128)(2,1)S(1)} %get-tuple-element.32.refs_3_, ...), custom_call_target="tpu_custom_call" | custom-call | tf_op jit(solution)/shard_map/expert_half/pallas_call | solution.py:277
  238.5 4.8 %collective-permute-done.13.away_ref = bf16[64,32,128]{2,1,0:T(8,128)(2,1)S(1)} collective-permute-done((bf16[64,32,128]{2,1,0:T(8,128)(2,1)S(1)}, bf16[64,32,128]{2,1,0:T(8,128)(2,1)S(1)}, u32[]{:S(2)}, u32[]{:S(2)}) %collective-permute-start.13) | collective-permute-done | bytes 524320 | tf_op jit(solution)/shard_map/ppermute | solution.py:426
  243.5 5.4 %collective-permute-done.15.away_ref = bf16[64,32,128]{2,1,0:T(8,128)(2,1)S(1)} collective-permute-done((bf16[64,32,128]{2,1,0:T(8,128)(2,1)S(1)}, bf16[64,32,128]{2,1,0:T(8,128)(2,1)S(1)}, u32[]{:S(2)}, u32[]{:S(2)}) %collective-permute-start.15) | collective-permute-done | bytes 524320 | tf_op jit(solution)/shard_map/ppermute | solution.py:426
  249.1 45.3 %all_to_all.22.terms_ref = bf16[192,32,128]{2,1,0:T(8,128)(2,1)S(1)} all-to-all(bf16[192,32,128]{2,1,0:T(8,128)(2,1)S(1)} %add_part.11), channel_id=1, replica_groups=mesh['rep'=4,'exp'=64] {'exp'}, dimensions={0} | all-to-all | bytes 3145728 | tf_op jit(solution)/shard_map/all_to_all | solution.py:430
  (66 shorter events, 40.9 us)
Async XLA Ops:
  0.0 26.4 %collective-permute-start = (bf16[4096,256]{1,0:T(8,128)(2,1)}, bf16[4096,256]{1,0:T(8,128)(2,1)}, u32[]{:S(2)}, u32[]{:S(2)}) collective-permute-start(bf16[4096,256]{1,0:T(8,128)(2,1)} %bitcast.12), channel_id=1, source_target_pairs={{0,64},{1,193},{2,66},{3,195},{4,68},{5,197},{6,70},{7,199},{8,72}... | collective-permute-start | bytes 6291464 | tf_op jit(solution)/shard_map/ppermute | solution.py:401
  0.7 48.1 %collective-permute-start.1 = (bf16[4096,256]{1,0:T(8,128)(2,1)}, bf16[4096,256]{1,0:T(8,128)(2,1)}, u32[]{:S(2)}, u32[]{:S(2)}) collective-permute-start(bf16[4096,256]{1,0:T(8,128)(2,1)} %bitcast.14), channel_id=1, source_target_pairs={{0,64},{1,193},{2,66},{3,195},{4,68},{5,197},{6,70},{7,199},{8,72}... | collective-permute-start | bytes 6291464 | tf_op jit(solution)/shard_map/ppermute | solution.py:401
  10.4 52.2 %all-to-all-start = ((bf16[192,32,128]{2,1,0:T(8,128)(2,1)}), bf16[192,32,128]{2,1,0:T(8,128)(2,1)S(1)}, u32[]{:S(2)}, u32[]{:S(2)}) async-start(bf16[192,32,128]{2,1,0:T(8,128)(2,1)} %get-tuple-element.24), calls=%async_computation | async-start | bytes 3145728 | tf_op jit(solution)/shard_map/all_to_all | solution.py:422
  22.4 29.9 %copy-start.5 = (bf16[2,1,16,4096]{3,2,1,0:T(8,128)(2,1)S(1)}, bf16[2,1,16,4096]{3,2,1,0:T(8,128)(2,1)}, u32[]{:S(2)}) copy-start(bf16[2,1,16,4096]{3,2,1,0:T(8,128)(2,1)} %q_ref.3) | copy-start | bytes 786436
  22.4 29.9 %copy-start.8 = (bf16[2,1,16,512]{3,2,1,0:T(8,128)(2,1)S(1)}, bf16[2,1,16,512]{3,2,1,0:T(8,128)(2,1)}, u32[]{:S(2)}) copy-start(bf16[2,1,16,512]{3,2,1,0:T(8,128)(2,1)} %nk_ref.3) | copy-start | bytes 98308
  22.4 29.9 %copy-start.9 = (bf16[2,1,16,512]{3,2,1,0:T(8,128)(2,1)S(1)}, bf16[2,1,16,512]{3,2,1,0:T(8,128)(2,1)}, u32[]{:S(2)}) copy-start(bf16[2,1,16,512]{3,2,1,0:T(8,128)(2,1)} %nv_ref.3) | copy-start | bytes 98308
  26.4 36.2 %collective-permute-start.2 = (bf16[128,4096]{1,0:T(8,128)(2,1)}, bf16[128,4096]{1,0:T(8,128)(2,1)S(1)}, u32[]{:S(2)}, u32[]{:S(2)}) collective-permute-start(bf16[128,4096]{1,0:T(8,128)(2,1)} %get-tuple-element.27), channel_id=1, source_target_pairs={{0,64},{1,193},{2,66},{3,195},{4,68},{5,197},{6,70},{7,199},{8,72}... | collective-permute-start | bytes 3145736 | tf_op jit(solution)/shard_map/ppermute | solution.py:405
  48.8 22.5 %collective-permute-start.3 = (bf16[128,4096]{1,0:T(8,128)(2,1)}, bf16[128,4096]{1,0:T(8,128)(2,1)}, u32[]{:S(2)}, u32[]{:S(2)}) collective-permute-start(bf16[128,4096]{1,0:T(8,128)(2,1)} %get-tuple-element.28), channel_id=1, source_target_pairs={{0,64},{1,193},{2,66},{3,195},{4,68},{5,197},{6,70},{7,199},{8,72}... | collective-permute-start | bytes 3145736 | tf_op jit(solution)/shard_map/ppermute | solution.py:405
  71.6 11.5 %collective-permute-start.4 = (bf16[64,32,128]{2,1,0:T(8,128)(2,1)S(1)}, bf16[64,32,128]{2,1,0:T(8,128)(2,1)S(1)}, u32[]{:S(2)}, u32[]{:S(2)}) collective-permute-start(bf16[64,32,128]{2,1,0:T(8,128)(2,1)S(1)} %get-tuple-element.50), channel_id=1, source_target_pairs={{0,192},{1,65},{2,194},{3,67},{4,196},{5,69},{6,198},{7,71},{8,200... | collective-permute-start | bytes 1572872 | tf_op jit(solution)/shard_map/ppermute | solution.py:425
  73.7 14.1 %collective-permute-start.6 = (bf16[64,32,128]{2,1,0:T(8,128)(2,1)S(1)}, bf16[64,32,128]{2,1,0:T(8,128)(2,1)S(1)}, u32[]{:S(2)}, u32[]{:S(2)}) collective-permute-start(bf16[64,32,128]{2,1,0:T(8,128)(2,1)S(1)} %get-tuple-element.49), channel_id=1, source_target_pairs={{0,192},{1,65},{2,194},{3,67},{4,196},{5,69},{6,198},{7,71},{8,200... | collective-permute-start | bytes 1572872 | tf_op jit(solution)/shard_map/ppermute | solution.py:425
  75.0 18.4 %collective-permute-start.8 = (bf16[64,32,128]{2,1,0:T(8,128)(2,1)S(1)}, bf16[64,32,128]{2,1,0:T(8,128)(2,1)S(1)}, u32[]{:S(2)}, u32[]{:S(2)}) collective-permute-start(bf16[64,32,128]{2,1,0:T(8,128)(2,1)S(1)} %get-tuple-element.48), channel_id=1, source_target_pairs={{0,192},{1,65},{2,194},{3,67},{4,196},{5,69},{6,198},{7,71},{8,200... | collective-permute-start | bytes 1572872 | tf_op jit(solution)/shard_map/ppermute | solution.py:425
  85.6 15.8 %collective-permute-start.5 = (bf16[64,32,128]{2,1,0:T(8,128)(2,1)S(1)}, bf16[64,32,128]{2,1,0:T(8,128)(2,1)S(1)}, u32[]{:S(2)}, u32[]{:S(2)}) collective-permute-start(bf16[64,32,128]{2,1,0:T(8,128)(2,1)S(1)} %expert_half.9), channel_id=1, source_target_pairs={{0,192},{1,65},{2,194},{3,67},{4,196},{5,69},{6,198},{7,71},{8,200... | collective-permute-start | bytes 1572872 | tf_op jit(solution)/shard_map/ppermute | solution.py:426
  90.2 14.4 %collective-permute-start.7 = (bf16[64,32,128]{2,1,0:T(8,128)(2,1)S(1)}, bf16[64,32,128]{2,1,0:T(8,128)(2,1)S(1)}, u32[]{:S(2)}, u32[]{:S(2)}) collective-permute-start(bf16[64,32,128]{2,1,0:T(8,128)(2,1)S(1)} %expert_half.10), channel_id=1, source_target_pairs={{0,192},{1,65},{2,194},{3,67},{4,196},{5,69},{6,198},{7,71},{8,200... | collective-permute-start | bytes 1572872 | tf_op jit(solution)/shard_map/ppermute | solution.py:426
  95.9 14.4 %collective-permute-start.9 = (bf16[64,32,128]{2,1,0:T(8,128)(2,1)S(1)}, bf16[64,32,128]{2,1,0:T(8,128)(2,1)S(1)}, u32[]{:S(2)}, u32[]{:S(2)}) collective-permute-start(bf16[64,32,128]{2,1,0:T(8,128)(2,1)S(1)} %expert_half.11), channel_id=1, source_target_pairs={{0,192},{1,65},{2,194},{3,67},{4,196},{5,69},{6,198},{7,71},{8,200... | collective-permute-start | bytes 1572872 | tf_op jit(solution)/shard_map/ppermute | solution.py:426
  110.4 52.0 %copy-start.6 = (bf16[2,1,8,4096]{3,2,1,0:T(8,128)(2,1)S(1)}, bf16[2,1,8,4096]{3,2,1,0:T(8,128)(2,1)}, u32[]{:S(2)}) copy-start(bf16[2,1,8,4096]{3,2,1,0:T(8,128)(2,1)} %drift_in_ref.3) | copy-start | bytes 393220
  110.4 52.0 %copy-start.7 = (f32[16,4096]{1,0:T(8,128)S(1)}, f32[16,4096]{1,0:T(8,128)}, u32[]{:S(2)}) copy-start(f32[16,4096]{1,0:T(8,128)} %get-tuple-element.36.residual_ref) | copy-start | bytes 786436
  110.4 52.0 %copy-start.10 = (s32[2,1,8,16]{3,2,1,0:T(8,128)S(1)}, s32[2,1,8,16]{3,2,1,0:T(8,128)}, u32[]{:S(2)}) copy-start(s32[2,1,8,16]{3,2,1,0:T(8,128)} %slot_places.1.places_ref) | copy-start | bytes 3076
  110.4 52.0 %copy-start.11 = (f32[4096]{0:T(1024)S(1)}, f32[4096]{0:T(1024)}, u32[]{:S(2)}) copy-start(f32[4096]{0:T(1024)} %param.24) | copy-start | bytes 49156
  210.4 10.5 %collective-permute-start.10 = (bf16[64,32,128]{2,1,0:T(8,128)(2,1)S(1)}, bf16[64,32,128]{2,1,0:T(8,128)(2,1)S(1)}, u32[]{:S(2)}, u32[]{:S(2)}) collective-permute-start(bf16[64,32,128]{2,1,0:T(8,128)(2,1)S(1)} %get-tuple-element.47), channel_id=1, source_target_pairs={{0,192},{1,65},{2,194},{3,67},{4,196},{5,69},{6,198},{7,71},{8,200... | collective-permute-start | bytes 1572872 | tf_op jit(solution)/shard_map/ppermute | solution.py:425
  210.7 15.8 %collective-permute-start.12 = (bf16[64,32,128]{2,1,0:T(8,128)(2,1)S(1)}, bf16[64,32,128]{2,1,0:T(8,128)(2,1)S(1)}, u32[]{:S(2)}, u32[]{:S(2)}) collective-permute-start(bf16[64,32,128]{2,1,0:T(8,128)(2,1)S(1)} %get-tuple-element.46), channel_id=1, source_target_pairs={{0,192},{1,65},{2,194},{3,67},{4,196},{5,69},{6,198},{7,71},{8,200... | collective-permute-start | bytes 1572872 | tf_op jit(solution)/shard_map/ppermute | solution.py:425
  213.7 18.4 %collective-permute-start.14 = (bf16[64,32,128]{2,1,0:T(8,128)(2,1)S(1)}, bf16[64,32,128]{2,1,0:T(8,128)(2,1)S(1)}, u32[]{:S(2)}, u32[]{:S(2)}) collective-permute-start(bf16[64,32,128]{2,1,0:T(8,128)(2,1)S(1)} %get-tuple-element.45), channel_id=1, source_target_pairs={{0,192},{1,65},{2,194},{3,67},{4,196},{5,69},{6,198},{7,71},{8,200... | collective-permute-start | bytes 1572872 | tf_op jit(solution)/shard_map/ppermute | solution.py:425
  223.3 15.0 %collective-permute-start.11 = (bf16[64,32,128]{2,1,0:T(8,128)(2,1)S(1)}, bf16[64,32,128]{2,1,0:T(8,128)(2,1)S(1)}, u32[]{:S(2)}, u32[]{:S(2)}) collective-permute-start(bf16[64,32,128]{2,1,0:T(8,128)(2,1)S(1)} %expert_half.13), channel_id=1, source_target_pairs={{0,192},{1,65},{2,194},{3,67},{4,196},{5,69},{6,198},{7,71},{8,200... | collective-permute-start | bytes 1572872 | tf_op jit(solution)/shard_map/ppermute | solution.py:426
  229.0 14.4 %collective-permute-start.13 = (bf16[64,32,128]{2,1,0:T(8,128)(2,1)S(1)}, bf16[64,32,128]{2,1,0:T(8,128)(2,1)S(1)}, u32[]{:S(2)}, u32[]{:S(2)}) collective-permute-start(bf16[64,32,128]{2,1,0:T(8,128)(2,1)S(1)} %expert_half.14), channel_id=1, source_target_pairs={{0,192},{1,65},{2,194},{3,67},{4,196},{5,69},{6,198},{7,71},{8,200... | collective-permute-start | bytes 1572872 | tf_op jit(solution)/shard_map/ppermute | solution.py:426
  234.6 14.4 %collective-permute-start.15 = (bf16[64,32,128]{2,1,0:T(8,128)(2,1)S(1)}, bf16[64,32,128]{2,1,0:T(8,128)(2,1)S(1)}, u32[]{:S(2)}, u32[]{:S(2)}) collective-permute-start(bf16[64,32,128]{2,1,0:T(8,128)(2,1)S(1)} %expert_half.15), channel_id=1, source_target_pairs={{0,192},{1,65},{2,194},{3,67},{4,196},{5,69},{6,198},{7,71},{8,200... | collective-permute-start | bytes 1572872 | tf_op jit(solution)/shard_map/ppermute | solution.py:426
  (7 other events, 55.3 us)
